TPU v7x, 32 devices: a whole 2x2x4 slice. The times are simulated.
32 devices in a mesh: dp: 2 (over core), row: 4 (over z), col: 4 (over y, x).
Axes of the slice: x: 2, y: 2, z: 4, core: 2. Of those that a mesh axis runs over, the one named last changes fastest.
Arguments:
- inputs: bfloat16 [4096, 2048], P(('dp', 'row'), 'col'), may hold values from -20 to 20
- segment: int32 [8, 512], P(('dp', 'col')), may hold values from 0 to 15, as said below
- grad_output: bfloat16 [4096, 2048], P(('dp', 'row'), 'col'), may hold values from -6 to 6
- norm_gain: float32 [2048], P('col'), may hold values from 0.1 to 1.9
- norm_bias: float32 [2048], P('col'), may hold values from -3 to 3
- qkv_weight: bfloat16 [2048, 6144], P('col', 'row'), may hold values from -4 to 4
- qkv_bias: float32 [6144], P('row'), may hold values from -3 to 3
- dense_weight: bfloat16 [2048, 2048], P('row', 'col'), may hold values from -0.5 to 0.5
- dense_bias: float32 [2048], P('col'), may hold values from -2 to 2
- fc1_weight: bfloat16 [2048, 8192], P('col', 'row'), may hold values from -0.125 to 0.125
- fc1_bias: float32 [8192], P('row'), may hold values from -3 to 3
- fc2_weight: bfloat16 [8192, 2048], P('row', 'col'), may hold values from -0.09375 to 0.09375
- fc2_bias: float32 [2048], P('col'), may hold values from -2 to 2
Outputs:
- output: bfloat16 [4096, 2048], P(('dp', 'row'), 'col')
- grad_input: float32 [4096, 2048], P(('dp', 'row'), 'col')
- grad_norm_gain: float32 [2048], P('col')
- grad_norm_bias: float32 [2048], P('col')
- grad_qkv_weight: float32 [2048, 6144], P('col', 'row')
- grad_qkv_bias: float32 [6144], P('row')
- grad_dense_weight: float32 [2048, 2048], P('row', 'col')
- grad_dense_bias: float32 [2048], P('col')
- grad_fc1_weight: float32 [2048, 8192], P('col', 'row')
- grad_fc1_bias: float32 [8192], P('row')
- grad_fc2_weight: float32 [8192, 2048], P('row', 'col')
- grad_fc2_bias: float32 [2048], P('col')
Inputs may be any that keep to these rules, and one draw needn't show every extreme that they name: `segment`: in each row of 512 tokens the ids start at 0 and never fall; a run of equal ids is one sequence. Rows 0, 4, 8 and so on hold one sequence of 512 tokens; rows 3, 7, 11 and so on hold 16 sequences of 32 tokens.
All inputs are finite; a program needn't handle non-finite values.
Results may differ from a plain program's by a relative error of at most 0.0098.
Values may be sent and summed in bfloat16 or wider, within the bound.
No kernel may reach another device: no remote copies, remote signals or barrier semaphores. Data moves between devices by JAX's collectives and lax.ppermute only.
A program may use at most 192 MiB of HBM per device.

v0:
```python
import math

import jax
import jax.numpy as jnp
from jax import lax
from jax.sharding import PartitionSpec as P

HEAD_DIM = 64
ROT = 32
PACK = 512
D = 2048


EPS = 1e-05


def gelu_tanh(values):
    inner = 0.7978845608028654 * (values + 0.044715 * values * values * values)
    return 0.5 * values * (1.0 + jnp.tanh(inner))


def gelu_slope(values):
    inner = 0.7978845608028654 * (values + 0.044715 * values * values * values)
    tangent = jnp.tanh(inner)
    return 0.5 * (1.0 + tangent) + 0.5 * values * (1.0 - tangent * tangent) * 0.7978845608028654 * (
        1.0 + 0.134145 * values * values
    )


def rotary_tables(segment, rot_dims):
    width = segment.shape[1]
    places = jnp.arange(width, dtype=jnp.int32)
    fresh = jnp.concatenate(
        [jnp.ones((segment.shape[0], 1), dtype=jnp.bool_), segment[:, 1:] != segment[:, :-1]],
        axis=1,
    )
    starts = lax.cummax(jnp.where(fresh, places[None, :], jnp.zeros_like(segment)), axis=1)
    offsets = (places[None, :] - starts).astype(jnp.float32)
    half_rot = rot_dims // 2
    freqs = jnp.exp(jnp.arange(half_rot, dtype=jnp.float32) * (-2.0 * math.log(10000.0) / rot_dims))
    angles = offsets[:, :, None] * freqs
    return (jnp.cos(angles)[:, :, None, :], jnp.sin(angles)[:, :, None, :])


def rotate_forward(values, cosines, sines, rot_dims):
    half_rot = rot_dims // 2
    first = values[..., :half_rot]
    second = values[..., half_rot:rot_dims]
    return jnp.concatenate(
        [
            first * cosines - second * sines,
            second * cosines + first * sines,
            values[..., rot_dims:],
        ],
        axis=-1,
    )


def rotate_back(grads, cosines, sines, rot_dims):
    half_rot = rot_dims // 2
    first = grads[..., :half_rot]
    second = grads[..., half_rot:rot_dims]
    return jnp.concatenate(
        [first * cosines + second * sines, second * cosines - first * sines, grads[..., rot_dims:]],
        axis=-1,
    )


def masked_scores(query, key_rows, segment_row):
    places = jnp.arange(segment_row.shape[0], dtype=jnp.int32)
    allowed = (segment_row[:, None] == segment_row[None, :]) & (places[None, :] <= places[:, None])
    scale = query.shape[-1] ** (-0.5)
    scores = jnp.einsum("qhe,khe->hqk", query, key_rows, preferred_element_type=jnp.float32) * scale
    return (jnp.where(allowed[None, :, :], scores, -1e30), scale)


def pack_forward(items):
    query, key_rows, value, segment_row = items
    scores, scale = masked_scores(query, key_rows, segment_row)
    row_top = jnp.max(scores, axis=-1, keepdims=True)
    log_total = row_top[..., 0] + jnp.log(jnp.sum(jnp.exp(scores - row_top), axis=-1))
    chances = jnp.exp(scores - log_total[..., None]).astype(jnp.bfloat16)
    attended = jnp.einsum(
        "hqk,khe->qhe", chances, value, preferred_element_type=jnp.float32
    ).astype(jnp.bfloat16)
    return (attended, log_total)


def pack_backward(items):
    query, key_rows, value, attended, grad_att, log_total, segment_row = items
    scores, scale = masked_scores(query, key_rows, segment_row)
    chances = jnp.exp(scores - log_total[..., None])
    rounded = chances.astype(jnp.bfloat16)
    grad_value = jnp.einsum("hqk,qhe->khe", rounded, grad_att, preferred_element_type=jnp.float32)
    grad_chance = jnp.einsum("qhe,khe->hqk", grad_att, value, preferred_element_type=jnp.float32)
    delta = jnp.transpose(
        jnp.sum(grad_att.astype(jnp.float32) * attended.astype(jnp.float32), axis=-1)
    )
    grad_scores = (chances * (grad_chance - delta[:, :, None]) * scale).astype(jnp.bfloat16)
    grad_query = jnp.einsum(
        "hqk,khe->qhe", grad_scores, key_rows, preferred_element_type=jnp.float32
    )
    grad_key = jnp.einsum("hqk,qhe->khe", grad_scores, query, preferred_element_type=jnp.float32)
    return (grad_query, grad_key, grad_value)


def contract_rows(left, right):
    return lax.dot_general(
        left, right, (((0,), (0,)), ((), ())), preferred_element_type=jnp.float32
    )


def contract_cols(left, right):
    return lax.dot_general(
        left, right, (((1,), (1,)), ((), ())), preferred_element_type=jnp.float32
    )


def body(
    inputs,
    segment,
    grad_output,
    norm_gain,
    norm_bias,
    qkv_weight,
    qkv_bias,
    dense_weight,
    dense_bias,
    fc1_weight,
    fc1_bias,
    fc2_weight,
    fc2_bias,
):
    n_col = lax.axis_size("col")
    wide_in = inputs.astype(jnp.float32)
    row_total, row_squares = lax.psum(
        (jnp.sum(wide_in, axis=1), jnp.sum(wide_in * wide_in, axis=1)), "col"
    )
    row_mean = (row_total / D)[:, None]
    row_square = (row_squares / D)[:, None]
    inv_std = lax.rsqrt(row_square - row_mean * row_mean + EPS)
    centered = (wide_in - row_mean) * inv_std
    normed = (centered * norm_gain + norm_bias).astype(jnp.bfloat16)
    gathered = lax.all_gather(normed, "row", axis=0, tiled=True)
    group_rows = gathered.shape[0]
    att_rows = group_rows // n_col
    in_weight = jnp.concatenate([qkv_weight, fc1_weight], axis=1)
    back_weight = jnp.concatenate([dense_weight, fc2_weight], axis=0)
    qkv_cols = qkv_weight.shape[1]
    projected = lax.psum_scatter(
        jnp.dot(gathered, in_weight, preferred_element_type=jnp.float32),
        "col",
        scatter_dimension=0,
        tiled=True,
    )
    qkv_full = projected[:, :qkv_cols] + qkv_bias
    pre_act = projected[:, qkv_cols:] + fc1_bias
    hidden = gelu_tanh(pre_act).astype(jnp.bfloat16)
    packs_here = segment.shape[0]
    heads_here = qkv_cols // (3 * HEAD_DIM)
    split_qkv = qkv_full.reshape(packs_here, PACK, heads_here, 3, HEAD_DIM)
    cosines, sines = rotary_tables(segment, ROT)
    query = rotate_forward(split_qkv[:, :, :, 0, :], cosines, sines, ROT).astype(jnp.bfloat16)
    key_rows = rotate_forward(split_qkv[:, :, :, 1, :], cosines, sines, ROT).astype(jnp.bfloat16)
    value = split_qkv[:, :, :, 2, :].astype(jnp.bfloat16)
    attended, log_total = lax.map(pack_forward, (query, key_rows, value, segment))
    att_cols = heads_here * HEAD_DIM
    att_flat = attended.reshape(att_rows, att_cols)
    att_all, hidden_all = (
        lax.all_gather(att_flat, "col", axis=0, tiled=True),
        lax.all_gather(hidden, "col", axis=0, tiled=True),
    )
    attn_part = lax.psum_scatter(
        jnp.dot(att_all, dense_weight, preferred_element_type=jnp.float32),
        "row",
        scatter_dimension=0,
        tiled=True,
    )
    mlp_part = lax.psum_scatter(
        jnp.dot(hidden_all, fc2_weight, preferred_element_type=jnp.float32).astype(jnp.bfloat16),
        "row",
        scatter_dimension=0,
        tiled=True,
    ).astype(jnp.float32)
    mixed = attn_part + mlp_part
    output = (wide_in + (mixed + dense_bias + fc2_bias)).astype(jnp.bfloat16)
    grad_all = lax.all_gather(grad_output, "row", axis=0, tiled=True)
    grad_dense_w = contract_rows(att_all, grad_all)
    grad_fc2_w = contract_rows(hidden_all, grad_all)
    grad_out_b = jnp.sum(grad_all.astype(jnp.float32), axis=0)
    backed = lax.psum_scatter(
        contract_cols(grad_all, back_weight), "col", scatter_dimension=0, tiled=True
    )
    grad_att = backed[:, :att_cols].astype(jnp.bfloat16)
    grad_pre = (backed[:, att_cols:] * gelu_slope(pre_act)).astype(jnp.bfloat16)
    grad_query, grad_key, grad_value = lax.map(
        pack_backward,
        (
            query,
            key_rows,
            value,
            attended,
            grad_att.reshape(packs_here, PACK, heads_here, HEAD_DIM),
            log_total,
            segment,
        ),
    )
    grad_query = rotate_back(grad_query, cosines, sines, ROT)
    grad_key = rotate_back(grad_key, cosines, sines, ROT)
    grad_qkv = (
        jnp.stack([grad_query, grad_key, grad_value], axis=3)
        .reshape(att_rows, qkv_cols)
        .astype(jnp.bfloat16)
    )
    grad_first = jnp.concatenate([grad_qkv, grad_pre], axis=1)
    grad_first_all = lax.all_gather(grad_first, "col", axis=0, tiled=True)
    grad_in_w = contract_rows(gathered, grad_first_all)
    grad_in_b = jnp.sum(grad_first_all.astype(jnp.float32), axis=0)
    grad_normed = lax.psum_scatter(
        contract_cols(grad_first_all, in_weight), "row", scatter_dimension=0, tiled=True
    )
    scaled = grad_normed * norm_gain
    scaled_sum, cross_sum = lax.psum(
        (jnp.sum(scaled, axis=1), jnp.sum(scaled * centered, axis=1)), "col"
    )
    grad_input = grad_output.astype(jnp.float32) + inv_std * (
        scaled - (scaled_sum / D)[:, None] - centered * (cross_sum / D)[:, None]
    )
    grad_gain, grad_bias = lax.psum(
        (jnp.sum(grad_normed * centered, axis=0), jnp.sum(grad_normed, axis=0)), ("dp", "row")
    )
    total_in_w, total_dense_w, total_fc2_w, total_in_b, total_out_b = lax.psum(
        (grad_in_w, grad_dense_w, grad_fc2_w, grad_in_b, grad_out_b), "dp"
    )
    grad_qkv_w = total_in_w[:, :qkv_cols]
    grad_fc1_w = total_in_w[:, qkv_cols:]
    grad_qkv_b = total_in_b[:qkv_cols]
    grad_fc1_b = total_in_b[qkv_cols:]
    return (
        output,
        grad_input,
        grad_gain,
        grad_bias,
        grad_qkv_w,
        grad_qkv_b,
        total_dense_w,
        total_out_b,
        grad_fc1_w,
        grad_fc1_b,
        total_fc2_w,
        total_out_b,
    )


def solution(mesh):
    in_specs = (
        P(("dp", "row"), "col"),
        P(("dp", "col"), None),
        P(("dp", "row"), "col"),
        P("col"),
        P("col"),
        P("col", "row"),
        P("row"),
        P("row", "col"),
        P("col"),
        P("col", "row"),
        P("row"),
        P("row", "col"),
        P("col"),
    )
    out_specs = (
        P(("dp", "row"), "col"),
        P(("dp", "row"), "col"),
        P("col"),
        P("col"),
        P("col", "row"),
        P("row"),
        P("row", "col"),
        P("col"),
        P("col", "row"),
        P("row"),
        P("row", "col"),
        P("col"),
    )
    return jax.shard_map(body, mesh=mesh, in_specs=in_specs, out_specs=out_specs, check_vma=False)
```

profile of v0, /device:TPU:0, one launch (start us, length us, event | category | flops | bytes accessed | tf_op | source)
XLA Modules:
  0.0 1129.9 jit_solution(15276972093117507922)
XLA Ops:
  9.2 11.4 %all-reduce.2 = (f32[512]{0:T(512)S(1)}, f32[512]{0:T(512)S(1)}) all-reduce(f32[512]{0:T(512)S(1)} %get-tuple-element.60, f32[512]{0:T(512)S(1)} %get-tuple-element.59), channel_id=1, replica_groups=mesh['dp'=2,'row'=4,'col'=4] {'col'}, use_global_device_ids=true, to_apply=%region_3.0 | all-reduce | flops 1024 | bytes 8192 | tf_op jit(solution)/shard_map/psum | solution.py:136
  22.9 35.1 %all-gather.12.cloned.1.call-done = bf16[2048,512]{1,0:T(8,128)(2,1)} async-done(((bf16[512,512]{1,0:T(8,128)(2,1)}), bf16[2048,512]{1,0:T(8,128)(2,1)}) %all-gather.12.cloned.1.call-update) | async-done | bytes 2097168 | tf_op jit(solution)/shard_map/all_gather | solution.py:187
  58.0 12.1 %convolution_bitcast_fusion = f32[2048,2560]{1,0:T(8,128)} fusion(bf16[2048,512]{1,0:T(8,128)(2,1)} %all-gather.12.cloned.1.call-done, bf16[2048,512]{1,0:T(8,128)(2,1)} %param.24, bf16[512,512]{1,0:T(8,128)(2,1)} %param.20), kind=kOutput, calls=%fused_computation.1 | convolution fusion | flops 5373952000 | bytes 25690112 | tf_op jit(solution)/shard_map/dot_general | solution.py:114
  74.4 30.2 %all-gather.6.cloned.1.call-done = bf16[2048,512]{1,0:T(8,128)(2,1)} async-done(((bf16[512,512]{1,0:T(8,128)(2,1)}), bf16[2048,512]{1,0:T(8,128)(2,1)}) %all-gather.6.cloned.1.call-update) | async-done | bytes 2097168 | tf_op jit(solution)/shard_map/all_gather | solution.py:144
  104.6 16.6 %fusion.47 = f32[2048,3584]{1,0:T(8,128)} fusion(bf16[2048,512]{1,0:T(8,128)(2,1)} %all-gather.6.cloned.1.call-done, bf16[512,3584]{1,0:T(8,128)(2,1)} %constant_dynamic-update-slice_fusion), kind=kOutput, calls=%fused_computation.105 | convolution fusion | flops 7516192768 | bytes 35127296 | tf_op jit(solution)/shard_map/dot_general | solution.py:151
  123.3 171.0 %reduce-scatter.12.cloned.1.call-done = f32[512,2560]{1,0:T(8,128)} async-done(((f32[2048,2560]{1,0:T(8,128)}), f32[512,2560]{1,0:T(8,128)}) %reduce-scatter.12.cloned.1.call-update) | async-done | bytes 5242896 | tf_op jit(solution)/shard_map/reduce_scatter | solution.py:191
  296.6 256.4 %reduce-scatter.6.cloned.1.call-done = f32[512,3584]{1,0:T(8,128)} async-done(((f32[2048,3584]{1,0:T(8,128)}), f32[512,3584]{1,0:T(8,128)}) %reduce-scatter.6.cloned.1.call-update) | async-done | bytes 7340048 | tf_op jit(solution)/shard_map/reduce_scatter | solution.py:150
  576.0 6.3 fusion.8
  585.8 138.6 %all-gather.14.cloned.1.call-done = bf16[2048,3584]{1,0:T(8,128)(2,1)} async-done(((bf16[512,3584]{1,0:T(8,128)(2,1)}), bf16[2048,3584]{1,0:T(8,128)(2,1)}) %all-gather.14.cloned.1.call-update) | async-done | bytes 14680080 | tf_op jit(solution)/shard_map/all_gather | solution.py:216
  724.4 13.4 %fusion.49 = f32[2048,512]{1,0:T(8,128)} fusion(bf16[2048,3584]{1,0:T(8,128)(2,1)} %all-gather.14.cloned.1.call-done, bf16[512,3584]{1,0:T(8,128)(2,1)} %constant_dynamic-update-slice_fusion), kind=kOutput, calls=%fused_computation.107 | convolution fusion | flops 7516192768 | bytes 22544384 | tf_op jit(solution)/shard_map/dot_general | solution.py:114
  737.8 23.8 %all-gather.8.cloned.1.call-done = bf16[2048,512]{0,1:T(8,128)(2,1)} async-done(((bf16[512,512]{0,1:T(8,128)(2,1)}), bf16[2048,512]{0,1:T(8,128)(2,1)}) %all-gather.8.cloned.1.call-update) | async-done | bytes 2097168 | tf_op jit(solution)/shard_map/all_gather | solution.py:170
  761.7 4.9 fusion.48
  766.7 84.9 %all-gather.10.cloned.1.call-done = bf16[2048,2048]{1,0:T(8,128)(2,1)} async-done(((bf16[512,2048]{1,0:T(8,128)(2,1)}), bf16[2048,2048]{1,0:T(8,128)(2,1)}) %all-gather.10.cloned.1.call-update) | async-done | bytes 8388624 | tf_op jit(solution)/shard_map/all_gather | solution.py:171
  851.6 9.8 convolution_convert_fusion
  865.5 10.2 fusion.52
  875.8 10.2 fusion.50
  888.0 7.4 convert_reduce_fusion
  900.0 31.3 %reduce-scatter.14.cloned.1.call-done = f32[512,512]{1,0:T(8,128)} async-done(((f32[2048,512]{1,0:T(8,128)}), f32[512,512]{1,0:T(8,128)}) %reduce-scatter.14.cloned.1.call-update) | async-done | bytes 1048592 | tf_op jit(solution)/shard_map/reduce_scatter | solution.py:219
  933.1 9.8 all-reduce.1
  942.9 17.9 %all-reduce = (f32[512]{0:T(512)}, f32[512]{0:T(512)}) all-reduce(f32[512]{0:T(512)S(1)} %get-tuple-element.55, f32[512]{0:T(512)S(1)} %get-tuple-element.58), channel_id=1, replica_groups=mesh['dp'=2,'row'=4,'col'=4] {'dp','row'}, use_global_device_ids=true, to_apply=%region_19.20 | all-reduce | flops 1024 | bytes 8192 | tf_op jit(solution)/shard_map/psum | solution.py:229
  960.9 51.2 %reduce-scatter.8.cloned.1.call-done = f32[512,512]{1,0:T(8,128)} async-done(((f32[2048,512]{1,0:T(8,128)}), f32[512,512]{1,0:T(8,128)}) %reduce-scatter.8.cloned.1.call-update) | async-done | bytes 1048592 | tf_op jit(solution)/shard_map/reduce_scatter | solution.py:173
  1012.1 46.8 %reduce-scatter.10.cloned.1.call-done = bf16[512,512]{1,0:T(8,128)(2,1)} async-done(((bf16[2048,512]{1,0:T(8,128)(2,1)}), bf16[512,512]{1,0:T(8,128)(2,1)}) %reduce-scatter.10.cloned.1.call-update) | async-done | bytes 524304 | tf_op jit(solution)/shard_map/reduce_scatter | solution.py:179
  1062.3 48.5 %all-reduce.7.cloned.1.call-done = (f32[512,3584]{1,0:T(8,128)}, f32[512,512]{1,0:T(8,128)}, f32[2048,512]{1,0:T(8,128)}) async-done(((f32[512,3584]{1,0:T(8,128)}, f32[512,512]{1,0:T(8,128)}, f32[2048,512]{1,0:T(8,128)}), (f32[512,3584]{1,0:T(8,128)}, f32[512,512]{1,0:T(8,128)}, f32[2048,512]{1,0:T(8,128)})) %all-reduce.7.cloned.1.call-update) | async-done | bytes 12582928 | tf_op jit(solution)/shard_map/psum | solution.py:232
  1114.5 4.8 slice.135
  (125 shorter events, 62.4 us)
Async XLA Ops:
  7.2 50.8 %all-gather.12.cloned.1.call-start = ((), (), s32[]{:S(2)}) async-start(), calls=%async_computation.11 | async-start | bytes 2621440 | tf_op jit(solution)/shard_map/all_gather | solution.py:187
  7.9 96.7 %all-gather.6.cloned.1.call-start = ((), (), s32[]{:S(2)}) async-start(), calls=%async_computation.5 | async-start | bytes 2621440 | tf_op jit(solution)/shard_map/all_gather | solution.py:144
  22.8 271.5 %reduce-scatter.12.cloned.1.call-start = ((), (), s32[]{:S(2)}) async-start(), calls=%async_computation.12 | async-start | bytes 26214400 | tf_op jit(solution)/shard_map/reduce_scatter | solution.py:191
  70.1 482.8 %reduce-scatter.6.cloned.1.call-start = ((), (), s32[]{:S(2)}) async-start(), calls=%async_computation.6 | async-start | bytes 36700160 | tf_op jit(solution)/shard_map/reduce_scatter | solution.py:150
  121.2 431.8 %copy-start.13 = (f32[1536]{0:T(1024)S(1)}, f32[1536]{0:T(1024)}, u32[]{:S(2)}) copy-start(f32[1536]{0:T(1024)} %param.19) | copy-start | bytes 18436
  121.2 603.1 %all-gather.14.cloned.1.call-start = ((), (), s32[]{:S(2)}) async-start(), calls=%async_computation.13 | async-start | bytes 18350080 | tf_op jit(solution)/shard_map/all_gather | solution.py:216
  584.4 177.3 %all-gather.8.cloned.1.call-start = ((), (), s32[]{:S(2)}) async-start(), calls=%async_computation.7 | async-start | bytes 2621440 | tf_op jit(solution)/shard_map/all_gather | solution.py:170
  585.0 266.7 %all-gather.10.cloned.1.call-start = ((), (), s32[]{:S(2)}) async-start(), calls=%async_computation.9 | async-start | bytes 10485760 | tf_op jit(solution)/shard_map/all_gather | solution.py:171
  585.7 345.6 %reduce-scatter.14.cloned.1.call-start = ((), (), s32[]{:S(2)}) async-start(), calls=%async_computation.14 | async-start | bytes 5242880 | tf_op jit(solution)/shard_map/reduce_scatter | solution.py:219
  737.8 23.9 %copy-start.9 = (bf16[512,512]{1,0:T(8,128)(2,1)S(1)}, bf16[512,512]{1,0:T(8,128)(2,1)}, u32[]{:S(2)}) copy-start(bf16[512,512]{1,0:T(8,128)(2,1)} %param.20) | copy-start | bytes 1572868
  737.8 274.3 %reduce-scatter.8.cloned.1.call-start = ((), (), s32[]{:S(2)}) async-start(), calls=%async_computation.8 | async-start | bytes 5242880 | tf_op jit(solution)/shard_map/reduce_scatter | solution.py:173
  766.6 94.9 %copy-start.3 = (bf16[2048,512]{0,1:T(8,128)(2,1)S(1)}, bf16[2048,512]{0,1:T(8,128)(2,1)}, u32[]{:S(2)}) copy-start(bf16[2048,512]{0,1:T(8,128)(2,1)} %all-gather.8.cloned.1.call-done) | copy-start | bytes 6291460
  766.6 292.3 %reduce-scatter.10.cloned.1.call-start = ((), (), s32[]{:S(2)}) async-start(), calls=%async_computation.10 | async-start | bytes 2621440 | tf_op jit(solution)/shard_map/reduce_scatter | solution.py:179
  861.5 249.3 %all-reduce.7.cloned.1.call-start = ((), (), s32[]{:S(2)}) async-start(), calls=%async_computation.15 | async-start | bytes 25165824 | tf_op jit(solution)/shard_map/psum | solution.py:232
  861.5 14.2 %slice-start = ((s8[14680064]{0:T(1024)(128)(4,1)}), s8[4194304]{0:T(1024)(128)(4,1)S(1)}, s32[]{:S(2)}) async-start(s8[14680064]{0:T(1024)(128)(4,1)} %bitcast.81), calls=%async_computation.16 | async-start | bytes 8388608
  865.5 10.2 slice-start.2
  865.5 10.2 slice-start.3
  865.5 10.2 copy-start.18
  887.9 43.4 %copy-start.1 = (bf16[512,512]{1,0:T(8,128)(2,1)S(1)}, bf16[512,512]{1,0:T(8,128)(2,1)}, u32[]{:S(2)}) copy-start(bf16[512,512]{1,0:T(8,128)(2,1)} %param.13) | copy-start | bytes 1572868
  887.9 43.4 %copy-start.12 = (f32[512]{0:T(512)S(1)}, f32[512]{0:T(512)}, u32[]{:S(2)}) copy-start(f32[512]{0:T(512)} %param.16) | copy-start | bytes 6148
  888.0 171.0 %copy-start.7 = (bf16[512,512]{1,0:T(8,128)(2,1)S(1)}, bf16[512,512]{1,0:T(8,128)(2,1)}, u32[]{:S(2)}) copy-start(bf16[512,512]{1,0:T(8,128)(2,1)} %param.15) | copy-start | bytes 1572868
  888.0 171.0 %copy-start.15 = (f32[512]{0:T(512)S(1)}, f32[512]{0:T(512)}, u32[]{:S(2)}) copy-start(f32[512]{0:T(512)} %param.25) | copy-start | bytes 6148
  888.0 171.0 %copy-start.16 = (f32[512]{0:T(512)S(1)}, f32[512]{0:T(512)}, u32[]{:S(2)}) copy-start(f32[512]{0:T(512)} %param.21) | copy-start | bytes 6148
  898.8 220.6 %copy-start.17 = (f32[512]{0:T(512)}, f32[512]{0:T(512)S(1)}, u32[]{:S(2)}) copy-start(f32[512]{0:T(512)S(1)} %get-tuple-element.142) | copy-start | bytes 6148
  (10 other events, 36.3 us)
Sparse Core Ops, SparseCore 0:
  9.6 48.3 all-gather.11
  60.1 44.4 all-gather.5
  107.7 186.5 reduce-scatter.11
  297.2 255.6 reduce-scatter.5
  584.5 139.8 all-gather.13
  726.6 35.0 all-gather.7
  764.1 87.4 all-gather.9
  854.5 76.7 reduce-scatter.13
  934.2 77.8 reduce-scatter.7
  1014.8 44.0 reduce-scatter.9
  1062.3 48.4 all-reduce.6
where the time goes:
time: 1140 us; the launch traced here: 1130 us
  waiting for transfers between devices  920 us (81%)
  matrix products  93.6 us (8%)
  blocking collectives  42.6 us (4%)
  other arithmetic  30.4 us (3%)
  local copies, waits for them, and re-layouts  28.3 us (2%)
  between operations  14.7 us (1%)
    reduce_scatter x1, waiting for transfers between devices, body(): lax.psum_scatter(jnp.dot(gathered, in_weight, preferred_element_type=jnp....  256 us
    reduce_scatter x1, waiting for transfers between devices, body(): lax.psum_scatter(contract_cols(grad_all, back_weight), 'col', scatter_dim...  171 us
    all_gather x1, waiting for transfers between devices, body(): grad_first_all = lax.all_gather(grad_first, 'col', axis=0, tiled=True)  139 us
    all_gather x1, waiting for transfers between devices, body(): lax.all_gather(hidden, 'col', axis=0, tiled=True)  84.9 us
    reduce_scatter x1, waiting for transfers between devices, body(): lax.psum_scatter(jnp.dot(att_all, dense_weight, preferred_element_type=jn...  51.2 us
    psum x1, waiting for transfers between devices, body(): lax.psum((grad_in_w, grad_dense_w, grad_fc2_w, grad_in_b, grad_out_b), 'dp')  48.5 us
    reduce_scatter x1, waiting for transfers between devices, body(): lax.psum_scatter(jnp.dot(hidden_all, fc2_weight, preferred_element_type=j...  46.8 us
    all_gather x1, waiting for transfers between devices, body(): grad_all = lax.all_gather(grad_output, 'row', axis=0, tiled=True)  35.1 us
  transfers between devices with their start and end apart: 11, of which 11 were waited for; matrix products, arithmetic and copies ran while one was open for 9% of the time, Pallas kernels for 0%

commit v1 on v0

--- a/solution.py
+++ b/solution.py
@@ -8,7 +8,6 @@
 HEAD_DIM = 64
 ROT = 32
 PACK = 512
-D = 2048
 
 
 EPS = 1e-05
@@ -110,10 +109,132 @@
     )
 
 
-def contract_cols(left, right):
-    return lax.dot_general(
-        left, right, (((1,), (1,)), ((), ())), preferred_element_type=jnp.float32
-    )
+def col_partner(step, n_col):
+    if n_col & (n_col - 1) == 0:
+        return [(i, i ^ step) for i in range(n_col)]
+    return [(i, (step - i) % n_col) for i in range(n_col)]
+
+
+def partner_of(index, step, n_col):
+    if n_col & (n_col - 1) == 0:
+        return index ^ step
+    return (step - index) % n_col
+
+
+def line_gather(block, axis):
+    count = lax.axis_size(axis)
+    here = lax.axis_index(axis)
+    stacked = jnp.zeros((count,) + block.shape, block.dtype)
+    ups = [block]
+    downs = [block]
+    for step in range(count - 1):
+        ups.append(lax.ppermute(ups[-1], axis, [(i, i + 1) for i in range(step, count - 1)]))
+        downs.append(
+            lax.ppermute(downs[-1], axis, [(i + 1, i) for i in range(0, count - 1 - step)])
+        )
+    zero = (0,) * block.ndim
+    stacked = lax.dynamic_update_slice(stacked, block[None], (here,) + zero)
+    for step in range(1, count):
+        piece = jnp.where(here >= step, ups[step], downs[count - step])
+        stacked = lax.dynamic_update_slice(stacked, piece[None], ((here - step) % count,) + zero)
+    return stacked
+
+
+def line_scatter(blocks, axis):
+    count = lax.axis_size(axis)
+    here = lax.axis_index(axis)
+
+    def pick(index):
+        return lax.dynamic_index_in_dim(blocks, jnp.clip(index, 0, count - 1), 0, keepdims=False)
+
+    up = None
+    down = None
+    for step in range(count - 1):
+        send_up = pick(here + count - 1 - step)
+        send_down = pick(here - (count - 1) + step)
+        if step:
+            send_up = add_wide(send_up, up)
+            send_down = add_wide(send_down, down)
+        up = lax.ppermute(send_up, axis, [(i, i + 1) for i in range(0, step + 1)])
+        down = lax.ppermute(
+            send_down, axis, [(i + 1, i) for i in range(count - 2 - step, count - 1)]
+        )
+    total = pick(here).astype(jnp.float32)
+    if count > 1:
+        total = total + up.astype(jnp.float32) + down.astype(jnp.float32)
+    return total
+
+
+def add_wide(left, right):
+    return (left.astype(jnp.float32) + right.astype(jnp.float32)).astype(left.dtype)
+
+
+def shifts(axis, step):
+    count = lax.axis_size(axis)
+    return [((i + step) % count, i) for i in range(count)]
+
+
+def spread_tokens(block):
+    n_col = lax.axis_size("col")
+    col = lax.axis_index("col")
+    n_dp = lax.axis_size("dp")
+    rows = line_gather(block, "row")
+    width = block.shape[1]
+    groups = rows.reshape(n_col, -1, width)
+    own = lax.dynamic_index_in_dim(groups, col, 0, keepdims=False)
+    wide = jnp.zeros((own.shape[0], n_col * width), block.dtype)
+    got = [(col, own)]
+    start = 1 if n_col & (n_col - 1) == 0 else 0
+    for step in range(start, n_col):
+        other = partner_of(col, step, n_col)
+        sent = lax.dynamic_index_in_dim(groups, other, 0, keepdims=False)
+        got.append((other, lax.ppermute(sent, "col", col_partner(step, n_col))))
+    for index, piece in got:
+        wide = lax.dynamic_update_slice(wide, piece, (0, index * width))
+    return jnp.stack([wide] + [lax.ppermute(wide, "dp", shifts("dp", s)) for s in range(1, n_dp)])
+
+
+def collect_tokens(partial):
+    n_col = lax.axis_size("col")
+    col = lax.axis_index("col")
+    n_dp = lax.axis_size("dp")
+    n_row = lax.axis_size("row")
+    summed = partial[:, 0]
+    for s in range(1, n_dp):
+        summed = add_wide(summed, lax.ppermute(partial[:, s], "dp", shifts("dp", n_dp - s)))
+    own = lax.dynamic_index_in_dim(summed, col, 0, keepdims=False)
+    groups = jnp.zeros_like(summed)
+    got = [(col, own)]
+    start = 1 if n_col & (n_col - 1) == 0 else 0
+    for step in range(start, n_col):
+        other = partner_of(col, step, n_col)
+        sent = lax.dynamic_index_in_dim(summed, other, 0, keepdims=False)
+        got.append((other, lax.ppermute(sent, "col", col_partner(step, n_col))))
+    for index, piece in got:
+        groups = lax.dynamic_update_slice(groups, piece[None], (index, 0, 0))
+    return line_scatter(groups.reshape(n_row, -1, groups.shape[-1]), "row")
+
+
+def half_of(array, axis):
+    size = array.shape[axis] // lax.axis_size("dp")
+    return lax.dynamic_slice_in_dim(array, lax.axis_index("dp") * size, size, axis)
+
+
+def both_halves(own, axis):
+    n_dp = lax.axis_size("dp")
+    here = lax.axis_index("dp")
+    parts = [own] + [lax.ppermute(own, "dp", shifts("dp", s)) for s in range(1, n_dp)]
+    if n_dp == 2:
+        return jnp.where(
+            here == 0,
+            jnp.concatenate(parts, axis=axis),
+            jnp.concatenate(parts[::-1], axis=axis),
+        )
+    size = own.shape[axis]
+    out = jnp.concatenate(parts, axis=axis)
+    for s in range(n_dp):
+        out = lax.dynamic_update_slice_in_dim(out, parts[s], ((here + s) % n_dp) * size, axis)
+    return out
 
 
 def body(
@@ -132,67 +253,75 @@
     fc2_bias,
 ):
     n_col = lax.axis_size("col")
+    n_dp = lax.axis_size("dp")
+    width = inputs.shape[1]
+    in_half = jnp.concatenate([half_of(qkv_weight, 1), half_of(fc1_weight, 1)], axis=1)
+    back_half = jnp.concatenate([half_of(dense_weight, 0), half_of(fc2_weight, 0)], axis=0)
+    qkv_cols = qkv_weight.shape[1] // n_dp
+    att_cols = dense_weight.shape[0] // n_dp
+    back_all = lax.all_gather(back_half, "col", axis=0)
+    in_all = lax.all_gather(in_half, "col", axis=0, tiled=True)
+
+    grad_rows = spread_tokens(grad_output)
+    tokens = grad_rows.shape[0] * grad_rows.shape[1]
+    grad_rows = grad_rows.reshape(tokens, n_col, width)
+
     wide_in = inputs.astype(jnp.float32)
     row_total, row_squares = lax.psum(
         (jnp.sum(wide_in, axis=1), jnp.sum(wide_in * wide_in, axis=1)), "col"
     )
-    row_mean = (row_total / D)[:, None]
-    row_square = (row_squares / D)[:, None]
+    full_width = n_col * width
+    row_mean = (row_total / full_width)[:, None]
+    row_square = (row_squares / full_width)[:, None]
     inv_std = lax.rsqrt(row_square - row_mean * row_mean + EPS)
     centered = (wide_in - row_mean) * inv_std
     normed = (centered * norm_gain + norm_bias).astype(jnp.bfloat16)
-    gathered = lax.all_gather(normed, "row", axis=0, tiled=True)
-    group_rows = gathered.shape[0]
-    att_rows = group_rows // n_col
-    in_weight = jnp.concatenate([qkv_weight, fc1_weight], axis=1)
-    back_weight = jnp.concatenate([dense_weight, fc2_weight], axis=0)
-    qkv_cols = qkv_weight.shape[1]
-    projected = lax.psum_scatter(
-        jnp.dot(gathered, in_weight, preferred_element_type=jnp.float32),
-        "col",
-        scatter_dimension=0,
-        tiled=True,
-    )
-    qkv_full = projected[:, :qkv_cols] + qkv_bias
-    pre_act = projected[:, qkv_cols:] + fc1_bias
+    normed_rows = spread_tokens(normed).reshape(tokens, full_width)
+    seg_rows = jnp.concatenate(
+        [segment] + [lax.ppermute(segment, "dp", shifts("dp", s)) for s in range(1, n_dp)]
+    )
+
+    backed = jnp.einsum(
+        "tjk,jhk->th", grad_rows, back_all, preferred_element_type=jnp.float32
+    )
+    grad_att = backed[:, :att_cols].astype(jnp.bfloat16)
+
+    projected = jnp.dot(normed_rows, in_all, preferred_element_type=jnp.float32)
+    qkv_full = projected[:, :qkv_cols] + half_of(qkv_bias, 0)
+    pre_act = projected[:, qkv_cols:] + half_of(fc1_bias, 0)
     hidden = gelu_tanh(pre_act).astype(jnp.bfloat16)
-    packs_here = segment.shape[0]
+    grad_pre = (backed[:, att_cols:] * gelu_slope(pre_act)).astype(jnp.bfloat16)
+
+    def grads_back(left):
+        part = jnp.einsum(
+            "th,tjk->jhk", left, grad_rows, preferred_element_type=jnp.float32
+        ).astype(jnp.bfloat16)
+        return lax.psum_scatter(part, "col", scatter_dimension=0, tiled=False)
+
+    def grads_in(right):
+        part = contract_rows(normed_rows, right).astype(jnp.bfloat16)
+        return lax.psum_scatter(part, "col", scatter_dimension=0, tiled=True)
+
+    grad_fc2_half = grads_back(hidden)
+    grad_fc1_half = grads_in(grad_pre)
+
+    packs_here = seg_rows.shape[0]
     heads_here = qkv_cols // (3 * HEAD_DIM)
     split_qkv = qkv_full.reshape(packs_here, PACK, heads_here, 3, HEAD_DIM)
-    cosines, sines = rotary_tables(segment, ROT)
+    cosines, sines = rotary_tables(seg_rows, ROT)
     query = rotate_forward(split_qkv[:, :, :, 0, :], cosines, sines, ROT).astype(jnp.bfloat16)
     key_rows = rotate_forward(split_qkv[:, :, :, 1, :], cosines, sines, ROT).astype(jnp.bfloat16)
     value = split_qkv[:, :, :, 2, :].astype(jnp.bfloat16)
-    attended, log_total = lax.map(pack_forward, (query, key_rows, value, segment))
-    att_cols = heads_here * HEAD_DIM
-    att_flat = attended.reshape(att_rows, att_cols)
-    att_all, hidden_all = (
-        lax.all_gather(att_flat, "col", axis=0, tiled=True),
-        lax.all_gather(hidden, "col", axis=0, tiled=True),
-    )
-    attn_part = lax.psum_scatter(
-        jnp.dot(att_all, dense_weight, preferred_element_type=jnp.float32),
-        "row",
-        scatter_dimension=0,
-        tiled=True,
-    )
-    mlp_part = lax.psum_scatter(
-        jnp.dot(hidden_all, fc2_weight, preferred_element_type=jnp.float32).astype(jnp.bfloat16),
-        "row",
-        scatter_dimension=0,
-        tiled=True,
-    ).astype(jnp.float32)
-    mixed = attn_part + mlp_part
+    attended, log_total = lax.map(pack_forward, (query, key_rows, value, seg_rows))
+    att_flat = attended.reshape(tokens, att_cols)
+
+    acts = jnp.concatenate([att_flat, hidden], axis=1)
+    out_part = jnp.einsum(
+        "th,jhk->jtk", acts, back_all, preferred_element_type=jnp.float32
+    ).astype(jnp.bfloat16)
+    mixed = collect_tokens(out_part.reshape(n_col, n_dp, tokens // n_dp, width))
     output = (wide_in + (mixed + dense_bias + fc2_bias)).astype(jnp.bfloat16)
-    grad_all = lax.all_gather(grad_output, "row", axis=0, tiled=True)
-    grad_dense_w = contract_rows(att_all, grad_all)
-    grad_fc2_w = contract_rows(hidden_all, grad_all)
-    grad_out_b = jnp.sum(grad_all.astype(jnp.float32), axis=0)
-    backed = lax.psum_scatter(
-        contract_cols(grad_all, back_weight), "col", scatter_dimension=0, tiled=True
-    )
-    grad_att = backed[:, :att_cols].astype(jnp.bfloat16)
-    grad_pre = (backed[:, att_cols:] * gelu_slope(pre_act)).astype(jnp.bfloat16)
+
     grad_query, grad_key, grad_value = lax.map(
         pack_backward,
         (
@@ -202,53 +331,57 @@
             attended,
             grad_att.reshape(packs_here, PACK, heads_here, HEAD_DIM),
             log_total,
-            segment,
+            seg_rows,
         ),
     )
     grad_query = rotate_back(grad_query, cosines, sines, ROT)
     grad_key = rotate_back(grad_key, cosines, sines, ROT)
     grad_qkv = (
         jnp.stack([grad_query, grad_key, grad_value], axis=3)
-        .reshape(att_rows, qkv_cols)
+        .reshape(tokens, qkv_cols)
         .astype(jnp.bfloat16)
     )
     grad_first = jnp.concatenate([grad_qkv, grad_pre], axis=1)
-    grad_first_all = lax.all_gather(grad_first, "col", axis=0, tiled=True)
-    grad_in_w = contract_rows(gathered, grad_first_all)
-    grad_in_b = jnp.sum(grad_first_all.astype(jnp.float32), axis=0)
-    grad_normed = lax.psum_scatter(
-        contract_cols(grad_first_all, in_weight), "row", scatter_dimension=0, tiled=True
-    )
+    norm_part = jnp.einsum(
+        "tf,jkf->jtk",
+        grad_first,
+        in_all.reshape(n_col, width, -1),
+        preferred_element_type=jnp.float32,
+    ).astype(jnp.bfloat16)
+    grad_normed = collect_tokens(norm_part.reshape(n_col, n_dp, tokens // n_dp, width))
+    grad_dense_half = grads_back(att_flat)
+    grad_qkv_half = grads_in(grad_qkv)
+    grad_in_b = lax.psum(jnp.sum(grad_first.astype(jnp.float32), axis=0), "col")
+
     scaled = grad_normed * norm_gain
     scaled_sum, cross_sum = lax.psum(
         (jnp.sum(scaled, axis=1), jnp.sum(scaled * centered, axis=1)), "col"
     )
-    grad_input = grad_output.astype(jnp.float32) + inv_std * (
-        scaled - (scaled_sum / D)[:, None] - centered * (cross_sum / D)[:, None]
-    )
-    grad_gain, grad_bias = lax.psum(
-        (jnp.sum(grad_normed * centered, axis=0), jnp.sum(grad_normed, axis=0)), ("dp", "row")
-    )
-    total_in_w, total_dense_w, total_fc2_w, total_in_b, total_out_b = lax.psum(
-        (grad_in_w, grad_dense_w, grad_fc2_w, grad_in_b, grad_out_b), "dp"
-    )
-    grad_qkv_w = total_in_w[:, :qkv_cols]
-    grad_fc1_w = total_in_w[:, qkv_cols:]
-    grad_qkv_b = total_in_b[:qkv_cols]
-    grad_fc1_b = total_in_b[qkv_cols:]
+    grad_wide = grad_output.astype(jnp.float32)
+    grad_input = grad_wide + inv_std * (
+        scaled - (scaled_sum / full_width)[:, None] - centered * (cross_sum / full_width)[:, None]
+    )
+    grad_gain, grad_bias, grad_out_b = lax.psum(
+        (
+            jnp.sum(grad_normed * centered, axis=0),
+            jnp.sum(grad_normed, axis=0),
+            jnp.sum(grad_wide, axis=0),
+        ),
+        ("dp", "row"),
+    )
     return (
         output,
         grad_input,
         grad_gain,
         grad_bias,
-        grad_qkv_w,
-        grad_qkv_b,
-        total_dense_w,
-        total_out_b,
-        grad_fc1_w,
-        grad_fc1_b,
-        total_fc2_w,
-        total_out_b,
+        both_halves(grad_qkv_half, 1).astype(jnp.float32),
+        both_halves(grad_in_b[:qkv_cols], 0),
+        both_halves(grad_dense_half, 0).astype(jnp.float32),
+        grad_out_b,
+        both_halves(grad_fc1_half, 1).astype(jnp.float32),
+        both_halves(grad_in_b[qkv_cols:], 0),
+        both_halves(grad_fc2_half, 0).astype(jnp.float32),
+        grad_out_b,
     )
 
 

time: 1140 us -> 607 us (0.53)
  waiting for transfers between devices: 920 us -> 151 us
  local copies, waits for them, and re-layouts: 28.3 us -> 155 us
  starting transfers between devices: 0.45 us -> 76.3 us
  other arithmetic: 30.4 us -> 67.6 us
  matrix products: 93.6 us -> 81.4 us
    reduce_scatter x5 -> x2, waiting for transfers between devices: 557 us -> 0.02 us  [grads_in(): return lax.psum_scatter(part, 'col', scatter_dimension=0, tiled=True)]
    all_gather x5 -> x2, waiting for transfers between devices: 313 us -> 0.02 us  [the longest x1 0.02 us: body(): in_all = lax.all_gather(in_half, 'col', axis=0, tiled=True)]
    ppermute x0 -> x47, waiting for transfers between devices: none -> 150 us  [the longest x6 51.1 us: spread_tokens(): got.append((other, lax.ppermute(sent, 'col', col_partner(step, n_col))))]
    ppermute x0 -> x47, starting transfers between devices: none -> 76 us  [the longest x6 27 us: line_scatter(): up = lax.ppermute(send_up, axis, [(i, i + 1) for i in range(0, step + 1)])]
    unnamed x50 -> x79, local copies, waits for them, and re-layouts: 8.84 us -> 60.3 us
    psum x1 -> x0, waiting for transfers between devices: 48.5 us -> none  [body(): lax.psum((grad_in_w, grad_dense_w, grad_fc2_w, grad_in_b, grad_out_b), 'dp')]
    reshape x0 -> x8, local copies, waits for them, and re-layouts: none -> 37.7 us  [the longest x2 15.2 us: body(): grad_rows = grad_rows.reshape(tokens, n_col, width)]
    convert_element_type x1 -> x13, other arithmetic: 2.16 us -> 27.4 us  [the longest x8 15 us: add_wide(): (left.astype(jnp.float32) + right.astype(jnp.float32)).astype(left.dtype)]
  transfers between devices with their start and end apart: 11 -> 53, of which waited for: 11 -> 19; matrix products, arithmetic and copies ran while one was open for 9% -> 41% of each run, Pallas kernels for 0% -> 0%
where the time goes in v1:
time: 607 us; the launch traced here: 599 us
  local copies, waits for them, and re-layouts  155 us (26%)
  waiting for transfers between devices  151 us (25%)
  matrix products  81.4 us (13%)
  starting transfers between devices  76.3 us (13%)
  other arithmetic  67.6 us (11%)
  blocking collectives  52 us (9%)
  between operations  15.5 us (3%)
    unnamed x79, local copies, waits for them, and re-layouts  60.3 us
    ppermute x6, waiting for transfers between devices, spread_tokens(): got.append((other, lax.ppermute(sent, 'col', col_partner(step, n_col))))  51.1 us
    ppermute x6, waiting for transfers between devices, collect_tokens(): got.append((other, lax.ppermute(sent, 'col', col_partner(step, n_col))))  48.8 us
    ppermute x6, waiting for transfers between devices, line_gather(): lax.ppermute(downs[-1], axis, [(i + 1, i) for i in range(0, count - 1 - s...  34.2 us
    psum x1, blocking collectives, body(): lax.psum((jnp.sum(grad_normed * centered, axis=0), jnp.sum(grad_normed, a...  27.3 us
    ppermute x6, starting transfers between devices, line_scatter(): up = lax.ppermute(send_up, axis, [(i, i + 1) for i in range(0, step + 1)])  27 us
    slice x2, local copies, waits for them, and re-layouts, collect_tokens(): summed = partial[:, 0]  20 us
    ppermute x6, starting transfers between devices, line_gather(): lax.ppermute(ups[-1], axis, [(i, i + 1) for i in range(step, count - 1)])  16.2 us
  transfers between devices with their start and end apart: 53, of which 19 were waited for; matrix products, arithmetic and copies ran while one was open for 41% of the time, Pallas kernels for 0%

profile of v1, /device:TPU:0, one launch (start us, length us, event | category | flops | bytes accessed | tf_op | source)
XLA Modules:
  0.0 599.1 jit_solution(15535820044180644751)
XLA Ops:
  22.4 10.4 %all-reduce.5 = (f32[512]{0:T(512)S(1)}, f32[512]{0:T(512)S(1)}) all-reduce(f32[512]{0:T(512)S(1)} %get-tuple-element.202, f32[512]{0:T(512)S(1)} %get-tuple-element.201), channel_id=1, replica_groups=mesh['dp'=2,'row'=4,'col'=4] {'col'}, use_global_device_ids=true, to_apply=%region_3.4 | all-reduce | flops 1024 | bytes 8192 | tf_op jit(solution)/shard_map/psum | solution.py:270
  53.4 8.6 %collective-permute-done.23 = bf16[512,512]{1,0:T(8,128)(2,1)} collective-permute-done((bf16[512,512]{1,0:T(8,128)(2,1)}, bf16[512,512]{1,0:T(8,128)(2,1)}, u32[]{:S(2)}, u32[]{:S(2)}) %collective-permute-start.23) | collective-permute-done | bytes 524320 | tf_op jit(solution)/shard_map/ppermute | solution.py:133
  64.3 8.9 %collective-permute-done.2 = bf16[512,512]{1,0:T(8,128)(2,1)} collective-permute-done((bf16[512,512]{1,0:T(8,128)(2,1)S(1)}, bf16[512,512]{1,0:T(8,128)(2,1)}, u32[]{:S(2)}, u32[]{:S(2)}) %collective-permute-start.2) | collective-permute-done | bytes 524320 | tf_op jit(solution)/shard_map/ppermute | solution.py:133
  75.2 9.2 %collective-permute-done.24 = bf16[512,512]{1,0:T(8,128)(2,1)} collective-permute-done((bf16[512,512]{1,0:T(8,128)(2,1)}, bf16[512,512]{1,0:T(8,128)(2,1)}, u32[]{:S(2)}, u32[]{:S(2)}) %collective-permute-start.24) | collective-permute-done | bytes 524320 | tf_op jit(solution)/shard_map/ppermute | solution.py:133
  101.8 12.7 %collective-permute-done.27 = bf16[512,512]{1,0:T(8,128)(2,1)S(1)} collective-permute-done((bf16[512,512]{1,0:T(8,128)(2,1)S(1)}, bf16[512,512]{1,0:T(8,128)(2,1)S(1)}, u32[]{:S(2)}, u32[]{:S(2)}) %collective-permute-start.27) | collective-permute-done | bytes 524320 | tf_op jit(solution)/shard_map/ppermute | solution.py:191
  122.4 10.1 %collective-permute-done.29 = bf16[512,512]{1,0:T(8,128)(2,1)S(1)} collective-permute-done((bf16[512,512]{1,0:T(8,128)(2,1)S(1)}, bf16[512,512]{1,0:T(8,128)(2,1)S(1)}, u32[]{:S(2)}, u32[]{:S(2)}) %collective-permute-start.29) | collective-permute-done | bytes 524320 | tf_op jit(solution)/shard_map/ppermute | solution.py:191
  133.3 9.8 %collective-permute-done.6 = bf16[512,512]{1,0:T(8,128)(2,1)S(1)} collective-permute-done((bf16[512,512]{1,0:T(8,128)(2,1)S(1)}, bf16[512,512]{1,0:T(8,128)(2,1)S(1)}, u32[]{:S(2)}, u32[]{:S(2)}) %collective-permute-start.6) | collective-permute-done | bytes 524320 | tf_op jit(solution)/shard_map/ppermute | solution.py:191
  144.0 8.6 %collective-permute-done.7 = bf16[512,512]{1,0:T(8,128)(2,1)S(1)} collective-permute-done((bf16[512,512]{1,0:T(8,128)(2,1)S(1)}, bf16[512,512]{1,0:T(8,128)(2,1)S(1)}, u32[]{:S(2)}, u32[]{:S(2)}) %collective-permute-start.7) | collective-permute-done | bytes 524320 | tf_op jit(solution)/shard_map/ppermute | solution.py:191
  189.5 9.0 %convolution_bitcast_fusion.2 = f32[1024,1280]{1,0:T(8,128)S(1)} fusion(bf16[1024,4,512]{0,2,1:T(8,128)(2,1)} %copy.104, bf16[4,1280,512]{2,1,0:T(8,128)(2,1)} %bitcast.320), kind=kOutput, calls=%fused_computation.67 | convolution fusion | flops 5368709120 | bytes 14680064 | tf_op jit(solution)/shard_map/tjk,jhk->th/dot_general | solution.py:284
  202.0 11.7 %fusion.112 = f32[1024,1792]{1,0:T(8,128)S(1)} fusion(bf16[1024,2048]{1,0:T(8,128)(2,1)} %bitcast.302, bf16[2048,1792]{1,0:T(8,128)(2,1)} %all-gather.4.cloned.1.call-done), kind=kOutput, calls=%fused_computation.241 | convolution fusion | flops 7516192768 | bytes 18874368 | tf_op jit(solution)/shard_map/dot_general | solution.py:289
  246.8 12.9 %while.27 = (s32[]{:T(128)}, f32[2,512,4,64]{1,3,2,0:T(8,128)}, f32[2,512,4,64]{1,3,2,0:T(8,128)}, bf16[2,512,4,64]{1,3,2,0:T(8,128)(2,1)}, bf16[2,512,4,64]{1,3...) while((s32[]{:T(128)}, f32[2,512,4,64]{1,3,2,0:T(8,128)}, ...), condition=%wide.region_12.13_spmd, body=%wide.region_10.12_spmd.sunk | while | flops 683931648 | bytes 46722380 | solution.py:325
  288.9 12.0 %convert_bitcast_fusion.1 = bf16[4,1024,512]{1,2,0:T(8,128)(2,1)} fusion(bf16[4,512,1792]{2,1,0:T(8,128)(2,1)} %bitcast.319, bf16[1024,1024]{1,0:T(8,128)(2,1)S(1)} %get-tuple-element.254, bf16[1024,768]{1,0:T(8,128)(2,1)} %copy.101), kind=kOutput, calls=%fused_computation.83 | convolution fusion | flops 7525629952 | bytes 15204352 | tf_op jit(solution)/shard_map/tf,jkf->jtk/dot_general | solution.py:345
  308.8 9.9 %fusion.110 = (bf16[4,1,512,512]{2,1,3,0:T(2,128)(2,1)}, bf16[4,1,512,512]{2,1,3,0:T(2,128)(2,1)}) fusion(bf16[4,2,512,512]{2,1,3,0:T(2,128)(2,1)} %reshape.255), kind=kLoop, calls=%fused_computation.239 | loop fusion | bytes 8388608 | tf_op jit(solution)/shard_map/slice | solution.py:202
  318.8 10.5 %copy.119 = bf16[4,1,512,512]{3,2,0,1:T(8,128)(2,1)} copy(bf16[4,1,512,512]{2,1,3,0:T(2,128)(2,1)} %get-tuple-element.257) | data formatting | bytes 4194304
  329.4 10.4 %convert_bitcast_fusion.2 = bf16[4,1024,512]{1,2,0:T(8,128)(2,1)} fusion(bf16[4,1280,512]{2,1,0:T(8,128)(2,1)} %bitcast.321, bf16[1024,1024]{1,0:T(8,128)(2,1)} %copy-done.14, bf16[1024,256]{1,0:T(8,128)(2,1)S(1)} %copy.82), kind=kOutput, calls=%fused_computation.84 | convolution fusion | flops 5376049152 | bytes 12058624 | tf_op jit(solution)/shard_map/th,jhk->jtk/dot_general | solution.py:319
  356.1 10.0 %fusion.111 = (bf16[4,1,512,512]{2,1,3,0:T(2,128)(2,1)}, bf16[4,1,512,512]{2,1,3,0:T(2,128)(2,1)}) fusion(bf16[4,2,512,512]{2,1,3,0:T(2,128)(2,1)} %reshape.251), kind=kLoop, calls=%fused_computation.240 | loop fusion | bytes 8388608 | tf_op jit(solution)/shard_map/slice | solution.py:202
  366.2 10.6 %copy.117 = bf16[4,1,512,512]{3,2,0,1:T(8,128)(2,1)} copy(bf16[4,1,512,512]{2,1,3,0:T(2,128)(2,1)} %get-tuple-element.259) | data formatting | bytes 4194304
  377.1 9.1 %copy.118 = bf16[4,1,512,512]{3,2,0,1:T(8,128)(2,1)S(1)} copy(bf16[4,1,512,512]{2,1,3,0:T(2,128)(2,1)} %get-tuple-element.256) | data formatting | bytes 4194304
  386.2 10.7 %copy.116 = bf16[4,1,512,512]{3,2,0,1:T(8,128)(2,1)} copy(bf16[4,1,512,512]{2,1,3,0:T(2,128)(2,1)} %get-tuple-element.258) | data formatting | bytes 4194304
  408.8 12.2 %collective-permute-done.32 = bf16[512,512]{1,0:T(8,128)(2,1)S(1)} collective-permute-done((bf16[512,512]{1,0:T(8,128)(2,1)S(1)}, bf16[512,512]{1,0:T(8,128)(2,1)S(1)}, u32[]{:S(2)}, u32[]{:S(2)}) %collective-permute-start.32) | collective-permute-done | bytes 524320 | tf_op jit(solution)/shard_map/ppermute | solution.py:212
  422.6 10.5 %collective-permute-done.34 = bf16[512,512]{1,0:T(8,128)(2,1)S(1)} collective-permute-done((bf16[512,512]{1,0:T(8,128)(2,1)S(1)}, bf16[512,512]{1,0:T(8,128)(2,1)S(1)}, u32[]{:S(2)}, u32[]{:S(2)}) %collective-permute-start.34) | collective-permute-done | bytes 524320 | tf_op jit(solution)/shard_map/ppermute | solution.py:212
  443.7 19.9 %collective-permute-done.14 = bf16[512,512]{1,0:T(8,128)(2,1)S(1)} collective-permute-done((bf16[512,512]{1,0:T(8,128)(2,1)S(1)}, bf16[512,512]{1,0:T(8,128)(2,1)S(1)}, u32[]{:S(2)}, u32[]{:S(2)}) %collective-permute-start.14) | collective-permute-done | bytes 524320 | tf_op jit(solution)/shard_map/ppermute | solution.py:212
  527.4 14.3 %all-reduce.4 = (f32[512]{0:T(512)S(1)}, f32[512]{0:T(512)S(1)}, f32[1792]{0:T(1024)S(1)}) all-reduce(f32[512]{0:T(512)S(1)} %get-tuple-element.198, f32[512]{0:T(512)S(1)} %get-tuple-element.199, f32[1792]{0:T(1024)S(1)} %convert_reduce_fusion), channel_id=1, replica_groups=mesh['dp'=2,'row'=4,'col'=4] {'col'}, use_global_device_ids=true, to_apply=%region_16.17 | all-reduce | flops 2816 | bytes 22528 | tf_op jit(solution)/shard_map/psum | solution.py:357
  546.4 27.3 %all-reduce.3 = (f32[512]{0:T(512)}, f32[512]{0:T(512)}, f32[512]{0:T(512)S(1)}) all-reduce(f32[512]{0:T(512)S(1)} %get-tuple-element.197, f32[512]{0:T(512)S(1)} %get-tuple-element.200, f32[512]{0:T(512)S(1)} %get-tuple-element.292), channel_id=1, replica_groups=mesh['dp'=2,'row'=4,'col'=4] {'dp','row'}, use_global_device_ids=true, to_apply=%region_18.19 | all-reduce | flops 1536 | bytes 12288 | tf_op jit(solution)/shard_map/psum | solution.py:364
  (360 shorter events, 323.3 us)
Async XLA Ops:
  7.2 182.3 %all-gather.6.cloned.1.call-start = ((), (), s32[]{:S(2)}) async-start(), calls=%async_computation.7 | async-start | bytes 6553600 | tf_op jit(solution)/shard_map/all_gather | solution.py:262
  11.0 191.0 %all-gather.4.cloned.1.call-start = ((), (), s32[]{:S(2)}) async-start(), calls=%async_computation.4 | async-start | bytes 9175040 | tf_op jit(solution)/shard_map/all_gather | solution.py:263
  15.0 481.1 %reduce-scatter.13.cloned.1.call-start = ((), (), s32[]{:S(2)}) async-start(), calls=%async_computation.8 | async-start | bytes 1310720
  88.5 33.0 %collective-permute-start.28 = (bf16[512,512]{1,0:T(8,128)(2,1)S(1)}, bf16[512,512]{1,0:T(8,128)(2,1)S(1)}, u32[]{:S(2)}, u32[]{:S(2)}) collective-permute-start(bf16[512,512]{1,0:T(8,128)(2,1)S(1)} %get-tuple-element.271), channel_id=1, source_target_pairs={{0,2},{1,3},{2,0},{3,1},{4,6},{5,7},{6,4},{7,5},{8,10},{9,11},{10,... | collective-permute-start | bytes 1572872 | tf_op jit(solution)/shard_map/ppermute | solution.py:191
  89.5 42.9 %collective-permute-start.29 = (bf16[512,512]{1,0:T(8,128)(2,1)S(1)}, bf16[512,512]{1,0:T(8,128)(2,1)S(1)}, u32[]{:S(2)}, u32[]{:S(2)}) collective-permute-start(bf16[512,512]{1,0:T(8,128)(2,1)S(1)} %get-tuple-element.270), channel_id=1, source_target_pairs={{0,3},{1,2},{2,1},{3,0},{4,7},{5,6},{6,5},{7,4},{8,11},{9,10},{10,... | collective-permute-start | bytes 1572872 | tf_op jit(solution)/shard_map/ppermute | solution.py:191
  93.9 49.2 %collective-permute-start.6 = (bf16[512,512]{1,0:T(8,128)(2,1)S(1)}, bf16[512,512]{1,0:T(8,128)(2,1)S(1)}, u32[]{:S(2)}, u32[]{:S(2)}) collective-permute-start(bf16[512,512]{1,0:T(8,128)(2,1)S(1)} %get-tuple-element.283), channel_id=1, source_target_pairs={{0,1},{1,0},{2,3},{3,2},{4,5},{5,4},{6,7},{7,6},{8,9},{9,8},{10,11... | collective-permute-start | bytes 1572872 | tf_op jit(solution)/shard_map/ppermute | solution.py:191
  95.4 57.1 %collective-permute-start.7 = (bf16[512,512]{1,0:T(8,128)(2,1)S(1)}, bf16[512,512]{1,0:T(8,128)(2,1)S(1)}, u32[]{:S(2)}, u32[]{:S(2)}) collective-permute-start(bf16[512,512]{1,0:T(8,128)(2,1)S(1)} %get-tuple-element.282), channel_id=1, source_target_pairs={{0,2},{1,3},{2,0},{3,1},{4,6},{5,7},{6,4},{7,5},{8,10},{9,11},{10,... | collective-permute-start | bytes 1572872 | tf_op jit(solution)/shard_map/ppermute | solution.py:191
  114.5 43.0 %collective-permute-start.8 = (bf16[512,512]{1,0:T(8,128)(2,1)S(1)}, bf16[512,512]{1,0:T(8,128)(2,1)S(1)}, u32[]{:S(2)}, u32[]{:S(2)}) collective-permute-start(bf16[512,512]{1,0:T(8,128)(2,1)S(1)} %get-tuple-element.281), channel_id=1, source_target_pairs={{0,3},{1,2},{2,1},{3,0},{4,7},{5,6},{6,5},{7,4},{8,11},{9,10},{10,... | collective-permute-start | bytes 1572872 | tf_op jit(solution)/shard_map/ppermute | solution.py:191
  133.3 32.4 %collective-permute-start.30 = (bf16[512,2048]{1,0:T(8,128)(2,1)}, bf16[512,2048]{1,0:T(8,128)(2,1)S(1)}, u32[]{:S(2)}, u32[]{:S(2)}) collective-permute-start(bf16[512,2048]{1,0:T(8,128)(2,1)} %constant_dynamic-update-slice_fusion), channel_id=1, source_target_pairs={{16,0},{0,16},{17,1},{1,17},{18,2},{2,18},{19,3},{3,19},{20,4},{4,... | collective-permute-start | bytes 6291464 | tf_op jit(solution)/shard_map/ppermute | solution.py:194
  246.8 295.0 %reduce-scatter.9.cloned.1.call-start = ((), (), s32[]{:S(2)}) async-start(), calls=%async_computation.5 | async-start | bytes 3932160 | tf_op jit(solution)/shard_map/reduce_scatter | solution.py:303
  272.2 270.1 %reduce-scatter.15.cloned.1.call-start = ((), (), s32[]{:S(2)}) async-start(), calls=%async_computation.9 | async-start | bytes 5242880
  285.7 257.1 %reduce-scatter.11.cloned.1.call-start = ((), (), s32[]{:S(2)}) async-start(), calls=%async_computation.6 | async-start | bytes 5242880 | tf_op jit(solution)/shard_map/reduce_scatter | solution.py:303
  329.3 67.7 %collective-permute-start.31 = (bf16[4,512,512]{2,1,0:T(8,128)(2,1)}, bf16[4,512,512]{2,1,0:T(8,128)(2,1)}, u32[]{:S(2)}, u32[]{:S(2)}) collective-permute-start(bf16[4,512,512]{2,1,0:T(8,128)(2,1)} %bitcast.305), channel_id=1, source_target_pairs={{16,0},{0,16},{17,1},{1,17},{18,2},{2,18},{19,3},{3,19},{20,4},{4,... | collective-permute-start | bytes 6291464 | tf_op jit(solution)/shard_map/ppermute | solution.py:204
  402.7 30.4 %collective-permute-start.34 = (bf16[512,512]{1,0:T(8,128)(2,1)S(1)}, bf16[512,512]{1,0:T(8,128)(2,1)S(1)}, u32[]{:S(2)}, u32[]{:S(2)}) collective-permute-start(bf16[512,512]{1,0:T(8,128)(2,1)S(1)} %get-tuple-element.266), channel_id=1, source_target_pairs={{0,3},{1,2},{2,1},{3,0},{4,7},{5,6},{6,5},{7,4},{8,11},{9,10},{10,... | collective-permute-start | bytes 1572872 | tf_op jit(solution)/shard_map/ppermute | solution.py:212
  405.8 37.8 %collective-permute-start.12 = (bf16[512,512]{1,0:T(8,128)(2,1)S(1)}, bf16[512,512]{1,0:T(8,128)(2,1)S(1)}, u32[]{:S(2)}, u32[]{:S(2)}) collective-permute-start(bf16[512,512]{1,0:T(8,128)(2,1)S(1)} %get-tuple-element.279), channel_id=1, source_target_pairs={{0,1},{1,0},{2,3},{3,2},{4,5},{5,4},{6,7},{7,6},{8,9},{9,8},{10,11... | collective-permute-start | bytes 1572872 | tf_op jit(solution)/shard_map/ppermute | solution.py:212
  407.7 35.9 %collective-permute-start.13 = (bf16[512,512]{1,0:T(8,128)(2,1)S(1)}, bf16[512,512]{1,0:T(8,128)(2,1)S(1)}, u32[]{:S(2)}, u32[]{:S(2)}) collective-permute-start(bf16[512,512]{1,0:T(8,128)(2,1)S(1)} %get-tuple-element.278), channel_id=1, source_target_pairs={{0,2},{1,3},{2,0},{3,1},{4,6},{5,7},{6,4},{7,5},{8,10},{9,11},{10,... | collective-permute-start | bytes 1572872 | tf_op jit(solution)/shard_map/ppermute | solution.py:212
  421.1 42.5 %collective-permute-start.14 = (bf16[512,512]{1,0:T(8,128)(2,1)S(1)}, bf16[512,512]{1,0:T(8,128)(2,1)S(1)}, u32[]{:S(2)}, u32[]{:S(2)}) collective-permute-start(bf16[512,512]{1,0:T(8,128)(2,1)S(1)} %get-tuple-element.277), channel_id=1, source_target_pairs={{0,3},{1,2},{2,1},{3,0},{4,7},{5,6},{6,5},{7,4},{8,11},{9,10},{10,... | collective-permute-start | bytes 1572872 | tf_op jit(solution)/shard_map/ppermute | solution.py:212
  434.0 36.8 %collective-permute-start.35 = (bf16[512,512]{1,0:T(8,128)(2,1)S(1)}, bf16[512,512]{1,0:T(8,128)(2,1)S(1)}, u32[]{:S(2)}, u32[]{:S(2)}) collective-permute-start(bf16[512,512]{1,0:T(8,128)(2,1)S(1)} %get-tuple-element.264), channel_id=1, source_target_pairs={{0,4},{1,5},{2,6},{3,7},{16,20},{17,21},{18,22},{19,23}} | collective-permute-start | bytes 1572872 | tf_op jit(solution)/shard_map/ppermute | solution.py:158
  473.8 28.4 %collective-permute-start.18 = (bf16[512,512]{1,0:T(8,128)(2,1)}, bf16[512,512]{1,0:T(8,128)(2,1)}, u32[]{:S(2)}, u32[]{:S(2)}) collective-permute-start(bf16[512,512]{1,0:T(8,128)(2,1)} %get-tuple-element.276), channel_id=1, source_target_pairs={{12,8},{13,9},{14,10},{15,11},{28,24},{29,25},{30,26},{31,27}} | collective-permute-start | bytes 1572872 | tf_op jit(solution)/shard_map/ppermute | solution.py:159
  541.7 32.0 %collective-permute-start.42 = (f32[768]{0:T(1024)S(1)}, f32[768]{0:T(1024)S(1)}, u32[]{:S(2)}, u32[]{:S(2)}) collective-permute-start(f32[768]{0:T(1024)S(1)} %slice.146), channel_id=1, source_target_pairs={{16,0},{0,16},{17,1},{1,17},{18,2},{2,18},{19,3},{3,19},{20,4},{4,... | collective-permute-start | bytes 9224 | tf_op jit(solution)/shard_map/ppermute | solution.py:226
  541.8 33.1 %collective-permute-start.41 = (bf16[512,768]{1,0:T(8,128)(2,1)}, bf16[512,768]{1,0:T(8,128)(2,1)}, u32[]{:S(2)}, u32[]{:S(2)}) collective-permute-start(bf16[512,768]{1,0:T(8,128)(2,1)} %reduce-scatter.9.cloned.1.call-done), channel_id=1, source_target_pairs={{16,0},{0,16},{17,1},{1,17},{18,2},{2,18},{19,3},{3,19},{20,4},{4,... | collective-permute-start | bytes 2359304 | tf_op jit(solution)/shard_map/ppermute | solution.py:226
  542.3 36.7 %collective-permute-start.46 = (bf16[1024,512]{0,1:T(8,128)(2,1)}, bf16[1024,512]{0,1:T(8,128)(2,1)S(1)}, u32[]{:S(2)}, u32[]{:S(2)}) collective-permute-start(bf16[1024,512]{0,1:T(8,128)(2,1)} %bitcast.310), channel_id=1, source_target_pairs={{16,0},{0,16},{17,1},{1,17},{18,2},{2,18},{19,3},{3,19},{20,4},{4,... | collective-permute-start | bytes 3145736 | tf_op jit(solution)/shard_map/ppermute | solution.py:226
  542.4 31.9 %collective-permute-start.45 = (f32[1024]{0:T(1024)S(1)}, f32[1024]{0:T(1024)S(1)}, u32[]{:S(2)}, u32[]{:S(2)}) collective-permute-start(f32[1024]{0:T(1024)S(1)} %slice.147), channel_id=1, source_target_pairs={{16,0},{0,16},{17,1},{1,17},{18,2},{2,18},{19,3},{3,19},{20,4},{4,... | collective-permute-start | bytes 12296 | tf_op jit(solution)/shard_map/ppermute | solution.py:226
  542.8 44.4 %collective-permute-start.44 = (bf16[512,1024]{1,0:T(8,128)(2,1)}, bf16[512,1024]{1,0:T(8,128)(2,1)}, u32[]{:S(2)}, u32[]{:S(2)}) collective-permute-start(bf16[512,1024]{1,0:T(8,128)(2,1)} %reduce-scatter.11.cloned.1.call-done), channel_id=1, source_target_pairs={{16,0},{0,16},{17,1},{1,17},{18,2},{2,18},{19,3},{3,19},{20,4},{4,... | collective-permute-start | bytes 3145736 | tf_op jit(solution)/shard_map/ppermute | solution.py:226
  (79 other events, 1135.2 us)
Sparse Core Ops, SparseCore 0:
  11.1 64.1 all-gather.5
  77.1 114.4 all-gather.3
  246.9 26.0 reduce-scatter.12
  276.4 43.8 reduce-scatter.8
  323.1 52.5 reduce-scatter.14
  378.6 89.6 reduce-scatter.10

commit v2 on v1

v2 whole, which is shorter than its diff:
```python
import math

import jax
import jax.numpy as jnp
from jax import lax
from jax.experimental import pallas as pl
from jax.experimental.pallas import tpu as pltpu
from jax.sharding import PartitionSpec as P

HEAD_DIM = 64
ROT = 32
PACK = 512


EPS = 1e-05


def gelu_tanh(values):
    inner = 0.7978845608028654 * (values + 0.044715 * values * values * values)
    return 0.5 * values * (1.0 + jnp.tanh(inner))


def gelu_slope(values):
    inner = 0.7978845608028654 * (values + 0.044715 * values * values * values)
    tangent = jnp.tanh(inner)
    return 0.5 * (1.0 + tangent) + 0.5 * values * (1.0 - tangent * tangent) * 0.7978845608028654 * (
        1.0 + 0.134145 * values * values
    )


def rotary_tables(segment, columns):
    width = segment.shape[1]
    places = jnp.arange(width, dtype=jnp.int32)
    fresh = jnp.concatenate(
        [jnp.ones((segment.shape[0], 1), dtype=jnp.bool_), segment[:, 1:] != segment[:, :-1]],
        axis=1,
    )
    starts = lax.cummax(jnp.where(fresh, places[None, :], jnp.zeros_like(segment)), axis=1)
    offsets = (places[None, :] - starts).astype(jnp.float32).reshape(-1, 1)
    half_rot = ROT // 2
    column = jnp.arange(3 * HEAD_DIM, dtype=jnp.int32)
    part = column % HEAD_DIM
    turned = (column < 2 * HEAD_DIM) & (part < ROT)
    freqs = jnp.exp((part % half_rot).astype(jnp.float32) * (-2.0 * math.log(10000.0) / ROT))
    freqs = jnp.where(turned, freqs, 0.0)
    sign = jnp.where(turned, jnp.where(part < half_rot, -1.0, 1.0), 0.0)
    angles = offsets * freqs[None, :]
    repeats = columns // (3 * HEAD_DIM)
    cosines = jnp.concatenate([jnp.cos(angles)] * repeats, axis=1)
    sines = jnp.concatenate([jnp.sin(angles) * sign[None, :]] * repeats, axis=1)
    return cosines, sines


def dot_nt(left, right):
    return lax.dot_general(
        left, right, (((1,), (1,)), ((), ())), preferred_element_type=jnp.float32
    )


def dot_tn(left, right):
    return lax.dot_general(
        left, right, (((0,), (0,)), ((), ())), preferred_element_type=jnp.float32
    )


def dot_nn(left, right):
    return jnp.dot(left, right, preferred_element_type=jnp.float32)


def attention_kernel(
    qkv_ref, bias_ref, cos_ref, sin_ref, seg_col_ref, seg_row_ref, grad_ref, out_ref, back_ref, turned, grads
):
    heads = out_ref.shape[1] // HEAD_DIM
    columns = qkv_ref.shape[1]
    half_rot = ROT // 2
    lanes = lax.broadcasted_iota(jnp.int32, (1, columns), 1) % HEAD_DIM
    first = lanes < half_rot

    def partner(values):
        ahead = pltpu.roll(values, columns - half_rot, 1)
        behind = pltpu.roll(values, half_rot, 1)
        return jnp.where(first, ahead, behind)

    full = qkv_ref[...] + bias_ref[...]
    turned[...] = (full * cos_ref[...] + partner(full) * sin_ref[...]).astype(jnp.bfloat16)
    size = qkv_ref.shape[0]
    rows = lax.broadcasted_iota(jnp.int32, (size, size), 0)
    places = lax.broadcasted_iota(jnp.int32, (size, size), 1)
    allowed = (seg_col_ref[0] == seg_row_ref[0]) & (places <= rows)
    scale = HEAD_DIM ** (-0.5)
    for head in range(heads):
        base = head * 3 * HEAD_DIM
        own = slice(head * HEAD_DIM, (head + 1) * HEAD_DIM)
        query = turned[:, base : base + HEAD_DIM]
        key = turned[:, base + HEAD_DIM : base + 2 * HEAD_DIM]
        value = turned[:, base + 2 * HEAD_DIM : base + 3 * HEAD_DIM]
        scores = jnp.where(allowed, dot_nt(query, key) * scale, -1e30)
        powers = jnp.exp(scores - jnp.max(scores, axis=1, keepdims=True))
        chances = powers * (1.0 / jnp.sum(powers, axis=1, keepdims=True))
        rounded = chances.astype(jnp.bfloat16)
        attended = dot_nn(rounded, value).astype(jnp.bfloat16)
        out_ref[:, own] = attended
        grad_att = grad_ref[:, own]
        delta = jnp.sum(
            grad_att.astype(jnp.float32) * attended.astype(jnp.float32), axis=1, keepdims=True
        )
        grad_scores = (chances * (dot_nt(grad_att, value) - delta) * scale).astype(jnp.bfloat16)
        grads[:, base : base + HEAD_DIM] = dot_nn(grad_scores, key)
        grads[:, base + HEAD_DIM : base + 2 * HEAD_DIM] = dot_tn(grad_scores, query)
        grads[:, base + 2 * HEAD_DIM : base + 3 * HEAD_DIM] = dot_tn(rounded, grad_att)
    whole = grads[...]
    back_ref[...] = (whole * cos_ref[...] - partner(whole) * sin_ref[...]).astype(jnp.bfloat16)


def attention(qkv, bias, cosines, sines, segment, grad_att, interpret=False):
    packs, size = segment.shape
    columns = qkv.shape[1]
    att_cols = grad_att.shape[1]
    by_rows = lambda width: pl.BlockSpec((size, width), lambda i: (i, 0))
    return pl.pallas_call(
        attention_kernel,
        grid=(packs,),
        in_specs=[
            by_rows(columns),
            pl.BlockSpec((1, columns), lambda i: (0, 0)),
            by_rows(columns),
            by_rows(columns),
            pl.BlockSpec((1, size, 1), lambda i: (i, 0, 0)),
            pl.BlockSpec((1, 1, size), lambda i: (i, 0, 0)),
            by_rows(att_cols),
        ],
        out_specs=[by_rows(att_cols), by_rows(columns)],
        out_shape=[
            jax.ShapeDtypeStruct((packs * size, att_cols), jnp.bfloat16),
            jax.ShapeDtypeStruct((packs * size, columns), jnp.bfloat16),
        ],
        scratch_shapes=[
            pltpu.VMEM((size, columns), jnp.bfloat16),
            pltpu.VMEM((size, columns), jnp.float32),
        ],
        interpret=interpret,
    )(
        qkv,
        bias.reshape(1, columns),
        cosines,
        sines,
        segment.reshape(packs, size, 1),
        segment.reshape(packs, 1, size),
        grad_att,
    )


def add_wide(left, right):
    return (left.astype(jnp.float32) + right.astype(jnp.float32)).astype(left.dtype)


def swap(array, axis, step):
    return lax.ppermute(array, axis, [(i, i ^ step) for i in range(lax.axis_size(axis))])


def total_over(array, axes):
    for axis in axes:
        step = 1
        while step < lax.axis_size(axis):
            array = array + swap(array, axis, step)
            step *= 2
    return array


def line_gather(block, axis):
    count = lax.axis_size(axis)
    here = lax.axis_index(axis)
    ups = [block]
    downs = [block]
    for step in range(count - 1):
        ups.append(lax.ppermute(ups[-1], axis, [(i, i + 1) for i in range(step, count - 1)]))
        downs.append(
            lax.ppermute(downs[-1], axis, [(i + 1, i) for i in range(0, count - 1 - step)])
        )
    zero = (0,) * block.ndim
    stacked = jnp.zeros((count,) + block.shape, block.dtype)
    stacked = lax.dynamic_update_slice(stacked, block[None], (here,) + zero)
    for step in range(1, count):
        piece = jnp.where(here >= step, ups[step], downs[count - step])
        stacked = lax.dynamic_update_slice(stacked, piece[None], ((here - step) % count,) + zero)
    return stacked


def line_scatter(blocks, axis):
    count = lax.axis_size(axis)
    here = lax.axis_index(axis)

    def pick(index):
        return lax.dynamic_index_in_dim(blocks, jnp.clip(index, 0, count - 1), 0, keepdims=False)

    total = pick(here).astype(jnp.float32)
    if count == 1:
        return total
    up = None
    down = None
    for step in range(count - 1):
        send_up = pick(here + count - 1 - step)
        send_down = pick(here - (count - 1) + step)
        if step:
            send_up = add_wide(send_up, up)
            send_down = add_wide(send_down, down)
        up = lax.ppermute(send_up, axis, [(i, i + 1) for i in range(0, step + 1)])
        down = lax.ppermute(
            send_down, axis, [(i + 1, i) for i in range(count - 2 - step, count - 1)]
        )
    return total + up.astype(jnp.float32) + down.astype(jnp.float32)


def grid_gather(block):
    count = lax.axis_size("col")
    if count != 4:
        return [block] + [swap(block, "col", step) for step in range(1, count)]
    cut = block.shape[0] // 2
    by_one = swap(block, "col", 1)
    by_two = swap(block, "col", 2)
    low = swap(by_one[:cut], "col", 2)
    high = swap(by_two[cut:], "col", 1)
    return [block, by_one, by_two, jnp.concatenate([low, high])]


def grid_scatter(part):
    count = lax.axis_size("col")
    size = part.shape[0] // count
    blocks = part.reshape(count, size, part.shape[1])
    if count != 4:
        total = blocks[0]
        for step in range(1, count):
            total = add_wide(total, swap(blocks[step], "col", step))
        return total
    cut = size // 2
    low = swap(jnp.stack([blocks[1, :cut], blocks[3, :cut]]), "col", 1)
    high = swap(jnp.stack([blocks[2, cut:], blocks[3, cut:]]), "col", 2)
    low_last = swap(add_wide(blocks[2, :cut], low[1]), "col", 2)
    high_last = swap(add_wide(blocks[1, cut:], high[1]), "col", 1)
    wide = lambda array: array.astype(jnp.float32)
    return jnp.concatenate(
        [
            (wide(blocks[0, :cut]) + wide(low[0]) + wide(low_last)).astype(part.dtype),
            (wide(blocks[0, cut:]) + wide(high[0]) + wide(high_last)).astype(part.dtype),
        ]
    )


def spread_tokens(block):
    n_col = lax.axis_size("col")
    n_dp = lax.axis_size("dp")
    col = lax.axis_index("col")
    width = block.shape[1]
    groups = line_gather(block, "row").reshape(n_col, -1, width)
    take = lambda step: lax.dynamic_index_in_dim(groups, col ^ step, 0, keepdims=False)
    pieces = [take(0)] + [swap(take(step), "col", step) for step in range(1, n_col)]
    own = jnp.concatenate(pieces, axis=1)
    return jnp.concatenate([own] + [swap(own, "dp", step) for step in range(1, n_dp)])


def collect_tokens(partial):
    n_col = lax.axis_size("col")
    n_dp = lax.axis_size("dp")
    n_row = lax.axis_size("row")
    col = lax.axis_index("col")
    tokens = partial.shape[0] // n_dp
    width = partial.shape[1] // n_col
    summed = partial[:tokens]
    for step in range(1, n_dp):
        summed = add_wide(summed, swap(partial[step * tokens : (step + 1) * tokens], "dp", step))
    groups = jnp.zeros((n_col, tokens, width), partial.dtype)
    for step in range(n_col):
        piece = summed[:, step * width : (step + 1) * width]
        if step:
            piece = swap(piece, "col", step)
        groups = lax.dynamic_update_slice(groups, piece[None], (col ^ step, 0, 0))
    return line_scatter(groups.reshape(n_row, -1, width), "row")


def half_of(array, axis):
    size = array.shape[axis] // lax.axis_size("dp")
    return lax.dynamic_slice_in_dim(array, lax.axis_index("dp") * size, size, axis)


def both_halves(own, axis):
    n_dp = lax.axis_size("dp")
    here = lax.axis_index("dp")
    parts = [own] + [swap(own, "dp", step) for step in range(1, n_dp)]
    if n_dp == 2:
        low = jnp.where(here == 0, parts[0], parts[1])
        high = jnp.where(here == 0, parts[1], parts[0])
        return jnp.concatenate([low, high], axis=axis)
    size = own.shape[axis]
    out = jnp.concatenate(parts, axis=axis)
    for step in range(n_dp):
        out = lax.dynamic_update_slice_in_dim(out, parts[step], (here ^ step) * size, axis)
    return out


def body(
    inputs,
    segment,
    grad_output,
    norm_gain,
    norm_bias,
    qkv_weight,
    qkv_bias,
    dense_weight,
    dense_bias,
    fc1_weight,
    fc1_bias,
    fc2_weight,
    fc2_bias,
):
    n_col = lax.axis_size("col")
    n_dp = lax.axis_size("dp")
    width = inputs.shape[1]
    full_width = n_col * width
    qkv_cols = qkv_weight.shape[1] // n_dp
    att_cols = dense_weight.shape[0] // n_dp
    grad_rows = spread_tokens(grad_output)
    in_half = jnp.concatenate([half_of(qkv_weight, 1), half_of(fc1_weight, 1)], axis=1)
    back_half = jnp.concatenate([half_of(dense_weight, 0), half_of(fc2_weight, 0)], axis=0)
    in_all = jnp.concatenate(grid_gather(in_half))
    back_all = jnp.concatenate(grid_gather(back_half), axis=1)

    wide_in = inputs.astype(jnp.float32)
    sums = total_over(
        jnp.stack([jnp.sum(wide_in, axis=1), jnp.sum(wide_in * wide_in, axis=1)]), ("col",)
    )
    row_mean = (sums[0] / full_width)[:, None]
    row_square = (sums[1] / full_width)[:, None]
    inv_std = lax.rsqrt(row_square - row_mean * row_mean + EPS)
    centered = (wide_in - row_mean) * inv_std
    normed = (centered * norm_gain + norm_bias).astype(jnp.bfloat16)
    normed_rows = spread_tokens(normed)
    seg_rows = jnp.concatenate([segment] + [swap(segment, "dp", step) for step in range(1, n_dp)])
    cosines, sines = rotary_tables(seg_rows, qkv_cols)

    projected = dot_nn(normed_rows, in_all)
    pre_act = projected[:, qkv_cols:] + half_of(fc1_bias, 0)
    hidden = gelu_tanh(pre_act).astype(jnp.bfloat16)
    backed = dot_nt(grad_rows, back_all)
    grad_att = backed[:, :att_cols].astype(jnp.bfloat16)
    grad_fc2_t = grid_scatter(dot_tn(grad_rows, hidden).astype(jnp.bfloat16))
    grad_pre = (backed[:, att_cols:] * gelu_slope(pre_act)).astype(jnp.bfloat16)
    grad_fc1 = grid_scatter(dot_tn(normed_rows, grad_pre).astype(jnp.bfloat16))

    attended, grad_qkv = attention(
        projected[:, :qkv_cols], half_of(qkv_bias, 0), cosines, sines, seg_rows, grad_att
    )
    acts = jnp.concatenate([attended, hidden], axis=1)
    mixed = collect_tokens(dot_nn(acts, back_all).astype(jnp.bfloat16))
    output = (wide_in + (mixed + dense_bias + fc2_bias)).astype(jnp.bfloat16)

    grad_first = jnp.concatenate([grad_qkv, grad_pre], axis=1)
    grad_normed = collect_tokens(dot_nt(grad_first, in_all).astype(jnp.bfloat16))
    late = grid_scatter(
        jnp.concatenate(
            [
                dot_tn(normed_rows, grad_qkv).astype(jnp.bfloat16),
                dot_tn(grad_rows, attended).astype(jnp.bfloat16),
            ],
            axis=1,
        )
    )
    grad_in_b = total_over(jnp.sum(grad_first.astype(jnp.float32), axis=0, keepdims=True), ("col",))

    scaled = grad_normed * norm_gain
    cross = total_over(
        jnp.stack([jnp.sum(scaled, axis=1), jnp.sum(scaled * centered, axis=1)]), ("col",)
    )
    grad_wide = grad_output.astype(jnp.float32)
    grad_input = grad_wide + inv_std * (
        scaled - (cross[0] / full_width)[:, None] - centered * (cross[1] / full_width)[:, None]
    )
    norm_sums = total_over(
        jnp.stack(
            [
                jnp.sum(grad_normed * centered, axis=0),
                jnp.sum(grad_normed, axis=0),
                jnp.sum(grad_wide, axis=0),
            ]
        ),
        ("dp", "row"),
    )
    wide = lambda array: array.astype(jnp.float32)
    return (
        output,
        grad_input,
        norm_sums[0],
        norm_sums[1],
        wide(both_halves(late[:, :qkv_cols], 1)),
        both_halves(grad_in_b[0, :qkv_cols], 0),
        wide(both_halves(late[:, qkv_cols:].T, 0)),
        norm_sums[2],
        wide(both_halves(grad_fc1, 1)),
        both_halves(grad_in_b[0, qkv_cols:], 0),
        wide(both_halves(grad_fc2_t.T, 0)),
        norm_sums[2],
    )


def solution(mesh):
    in_specs = (
        P(("dp", "row"), "col"),
        P(("dp", "col"), None),
        P(("dp", "row"), "col"),
        P("col"),
        P("col"),
        P("col", "row"),
        P("row"),
        P("row", "col"),
        P("col"),
        P("col", "row"),
        P("row"),
        P("row", "col"),
        P("col"),
    )
    out_specs = (
        P(("dp", "row"), "col"),
        P(("dp", "row"), "col"),
        P("col"),
        P("col"),
        P("col", "row"),
        P("row"),
        P("row", "col"),
        P("col"),
        P("col", "row"),
        P("row"),
        P("row", "col"),
        P("col"),
    )
    return jax.shard_map(body, mesh=mesh, in_specs=in_specs, out_specs=out_specs, check_vma=False)
```

time: 607 us -> 618 us (1.018)
  waiting for transfers between devices: 151 us -> 234 us
  local copies, waits for them, and re-layouts: 155 us -> 84.8 us
  blocking collectives: 52 us -> 0 us
  starting transfers between devices: 76.3 us -> 111 us
  Pallas kernels: 0 us -> 24.5 us
  between operations: 15.5 us -> 2.49 us
    ppermute x23 -> x52, waiting for transfers between devices: 104 us -> 176 us  [swap(): lax.ppermute(array, axis, [(i, i ^ step) for i in range(lax.axis_size(axi...]
    psum x3 -> x0, blocking collectives: 52 us -> none  [the longest x1 27.3 us: body(): lax.psum((jnp.sum(grad_normed * centered, axis=0), jnp.sum(grad_normed, a...]
    ppermute x23 -> x52, starting transfers between devices: 17.3 us -> 48.2 us  [swap(): lax.ppermute(array, axis, [(i, i ^ step) for i in range(lax.axis_size(axi...]
    unnamed x79 -> x177, local copies, waits for them, and re-layouts: 60.3 us -> 31.5 us
    reshape x8 -> x5, local copies, waits for them, and re-layouts: 37.7 us -> 10.1 us  [the longest x1 7.9 us: grid_scatter(): blocks = part.reshape(count, size, part.shape[1])]
    pallas_call x0 -> x1, Pallas kernels: none -> 24.5 us  [attention(): pl.pallas_call(attention_kernel, grid=(packs,), in_specs=[by_rows(columns...]
    concatenate x2 -> x10, other arithmetic: 1.48 us -> 12.4 us  [the longest x2 2.89 us: spread_tokens(): own = jnp.concatenate(pieces, axis=1)]
    ppermute x6, waiting for transfers between devices: 0.02 us -> 8.61 us  [line_scatter(): lax.ppermute(send_down, axis, [(i + 1, i) for i in range(count - 2 - step...]
  transfers between devices with their start and end apart: 53 -> 76, of which waited for: 19 -> 29; matrix products, arithmetic and copies ran while one was open for 41% -> 25% of each run, Pallas kernels for 0% -> 0%
where the time goes in v2:
time: 618 us; the launch traced here: 608 us
  waiting for transfers between devices  234 us (38%)
  starting transfers between devices  111 us (18%)
  local copies, waits for them, and re-layouts  84.8 us (14%)
  matrix products  77.4 us (13%)
  other arithmetic  73.2 us (12%)
  Pallas kernels  24.5 us (4%)
    ppermute x52, waiting for transfers between devices, swap(): lax.ppermute(array, axis, [(i, i ^ step) for i in range(lax.axis_size(axi...  176 us
    ppermute x52, starting transfers between devices, swap(): lax.ppermute(array, axis, [(i, i ^ step) for i in range(lax.axis_size(axi...  48.2 us
    ppermute x6, starting transfers between devices, line_scatter(): up = lax.ppermute(send_up, axis, [(i, i + 1) for i in range(0, step + 1)])  33.1 us
    unnamed x177, local copies, waits for them, and re-layouts  31.5 us
    ppermute x6, waiting for transfers between devices, line_gather(): lax.ppermute(downs[-1], axis, [(i + 1, i) for i in range(0, count - 1 - s...  30.8 us
    dot_general x2, matrix products, dot_nn(): return jnp.dot(left, right, preferred_element_type=jnp.float32)  30.6 us
    dot_general x4, matrix products, dot_tn(): lax.dot_general(left, right, (((0,), (0,)), ((), ())), preferred_element_...  28.2 us
    pallas_call x1, Pallas kernels, attention(): pl.pallas_call(attention_kernel, grid=(packs,), in_specs=[by_rows(columns...  24.5 us
  transfers between devices with their start and end apart: 76, of which 29 were waited for; matrix products, arithmetic and copies ran while one was open for 25% of the time, Pallas kernels for 0%

profile of v2, /device:TPU:0, one launch (start us, length us, event | category | flops | bytes accessed | tf_op | source)
XLA Modules:
  0.0 608.0 jit_solution(10674437476930535608)
XLA Ops:
  34.5 9.3 %collective-permute-done.3 = bf16[512,512]{1,0:T(8,128)(2,1)S(1)} collective-permute-done((bf16[512,512]{1,0:T(8,128)(2,1)}, bf16[512,512]{1,0:T(8,128)(2,1)S(1)}, u32[]{:S(2)}, u32[]{:S(2)}) %collective-permute-start.3) | collective-permute-done | bytes 524320 | tf_op jit(solution)/shard_map/ppermute | solution.py:178
  46.6 8.6 %collective-permute-done.19 = bf16[512,512]{1,0:T(8,128)(2,1)} collective-permute-done((bf16[512,512]{1,0:T(8,128)(2,1)}, bf16[512,512]{1,0:T(8,128)(2,1)}, u32[]{:S(2)}, u32[]{:S(2)}) %collective-permute-start.19) | collective-permute-done | bytes 524320 | tf_op jit(solution)/shard_map/ppermute | solution.py:178
  68.3 9.3 %collective-permute-done.20 = bf16[512,512]{1,0:T(8,128)(2,1)} collective-permute-done((bf16[512,512]{1,0:T(8,128)(2,1)}, bf16[512,512]{1,0:T(8,128)(2,1)}, u32[]{:S(2)}, u32[]{:S(2)}) %collective-permute-start.20) | collective-permute-done | bytes 524320 | tf_op jit(solution)/shard_map/ppermute | solution.py:178
  90.1 22.0 %collective-permute-done.25 = bf16[512,512]{1,0:T(8,128)(2,1)S(1)} collective-permute-done((bf16[512,512]{1,0:T(8,128)(2,1)S(1)}, bf16[512,512]{1,0:T(8,128)(2,1)S(1)}, u32[]{:S(2)}, u32[]{:S(2)}) %collective-permute-start.25) | collective-permute-done | bytes 524320 | tf_op jit(solution)/shard_map/ppermute | solution.py:158
  112.8 13.9 %collective-permute-done.24 = bf16[512,512]{1,0:T(8,128)(2,1)S(1)} collective-permute-done((bf16[512,512]{1,0:T(8,128)(2,1)S(1)}, bf16[512,512]{1,0:T(8,128)(2,1)S(1)}, u32[]{:S(2)}, u32[]{:S(2)}) %collective-permute-start.24) | collective-permute-done | bytes 524320 | tf_op jit(solution)/shard_map/ppermute | solution.py:158
  141.2 22.1 %collective-permute-done.28 = bf16[1280,512]{1,0:T(8,128)(2,1)S(1)} collective-permute-done((bf16[1280,512]{1,0:T(8,128)(2,1)}, bf16[1280,512]{1,0:T(8,128)(2,1)S(1)}, u32[]{:S(2)}, u32[]{:S(2)}) %collective-permute-start.28) | collective-permute-done | bytes 1310752 | tf_op jit(solution)/shard_map/ppermute | solution.py:158
  180.7 13.3 %collective-permute-done.9 = bf16[512,512]{1,0:T(8,128)(2,1)S(1)} collective-permute-done((bf16[512,512]{1,0:T(8,128)(2,1)}, bf16[512,512]{1,0:T(8,128)(2,1)S(1)}, u32[]{:S(2)}, u32[]{:S(2)}) %collective-permute-start.9) | collective-permute-done | bytes 524320 | tf_op jit(solution)/shard_map/ppermute | solution.py:158
  209.6 9.1 %fusion.67 = f32[1024,1280]{1,0:T(8,128)S(1)} fusion(bf16[640,512]{1,0:T(8,128)(2,1)} %copy-done.71, bf16[640,512]{1,0:T(8,128)(2,1)} %copy-done.73, bf16[1280,512]{1,0:T(8,128)(2,1)} %copy-done.57, bf16[1280,512]{1,0:T(8,128)(2,1)} %collective-permute-done.27, bf16[1024,512]{1,0:T(8,128)(2,1)S(1)} %copy-done.22, bf16[256,512]{1,0:T(8,128)(2,1)S(1)} %copy-done.38, ...), kind=kOutput, calls=%fused_computation.212 | convolution fusion | flops 5421137920 | bytes 14680064 | tf_op jit(solution)/shard_map/dot_general | solution.py:55
  219.7 12.7 %fusion.68 = f32[1024,1792]{1,0:T(8,128)S(1)} fusion(bf16[2048,1792]{1,0:T(8,128)(2,1)} %constant_dynamic-update-slice_fusion, bf16[512,2048]{1,0:T(8,128)(2,1)} %collective-permute-done.11, bf16[512,512]{1,0:T(8,128)(2,1)} %collective-permute-done.10, bf16[512,512]{1,0:T(8,128)(2,1)S(1)} %copy-done.50, bf16[512,512]{1,0:T(8,128)(2,1)S(1)} %copy-done.54, ...), kind=kOutput, calls=%fused_computation.213 | convolution fusion | flops 7537164288 | bytes 18874368 | tf_op jit(solution)/shard_map/dot_general | solution.py:67
  237.1 24.5 %shard_map.220 = (bf16[1024,256]{1,0:T(8,128)(2,1)}, bf16[1024,768]{1,0:T(8,128)(2,1)}) custom-call(f32[1024,768]{1,0:T(8,128)} %slice.275.qkv_ref, f32[1,768]{1,0:T(1,128)} %reshape.209.bias_ref, f32[1024,768]{1,0:T(8,128)} %pad_maximum_fusion.4.cos_ref, f32[1024,768]{1,0:T(8,128)} %pad_maximum_fusion.5.sin_ref, s32[2,512,1]{2,1,0:T(8,128)} %copy.41.seg_col_ref, ...), custom_call_target="tpu_custom_call" | custom-call | tf_op jit(solution)/shard_map/pallas_call | solution.py:120
  265.1 12.3 %convolution_convert_fusion.4 = bf16[2048,768]{0,1:T(8,128)(2,1)S(1)} fusion(bf16[1024,768]{1,0:T(8,128)(2,1)S(1)} %copy-done.35, bf16[512,2048]{1,0:T(8,128)(2,1)} %collective-permute-done.11, bf16[512,512]{1,0:T(8,128)(2,1)} %collective-permute-done.10, bf16[512,512]{1,0:T(8,128)(2,1)S(1)} %copy-done.51, bf16[512,512]{1,0:T(8,128)(2,1)S(1)} %copy-done.55, ...), kind=kOutput, calls=%fused_computation.23 | convolution fusion | flops 3243769856 | bytes 8912896 | tf_op jit(solution)/shard_map/dot_general | solution.py:61
  279.7 7.9 %reshape.214 = bf16[4,512,1024]{1,0,2:T(4,128)(2,1)} reshape(bf16[2048,1024]{0,1:T(8,128)(2,1)} %pad_maximum_fusion.2) | data formatting | bytes 8388608 | tf_op jit(solution)/shard_map/reshape | solution.py:229
  287.6 10.7 %fusion.73 = (bf16[1,256,1024]{1,0,2:T(2,128)(2,1)}, bf16[1,256,1024]{1,0,2:T(2,128)(2,1)}, bf16[1,256,1024]{1,0,2:T(2,128)(2,1)S(1)}, bf16[1,256,1024]{1,0,2:T(...) fusion(bf16[4,512,1024]{1,0,2:T(4,128)(2,1)} %reshape.214), kind=kLoop, calls=%fused_computation.216 | loop fusion | bytes 6291456 | tf_op jit(solution)/shard_map/slice | solution.py:244
  306.3 9.5 %convolution_convert_fusion = bf16[1024,2048]{1,0:T(8,128)(2,1)} fusion(bf16[2048,1792]{1,0:T(8,128)(2,1)S(1)} %bitcast.176, bf16[1024,1024]{1,0:T(8,128)(2,1)S(1)} %get-tuple-element.49, bf16[1024,768]{1,0:T(8,128)(2,1)S(1)} %copy-done.36), kind=kOutput, calls=%fused_computation.18 | convolution fusion | flops 7525629952 | bytes 15204352 | tf_op jit(solution)/shard_map/dot_general | solution.py:55
  333.2 17.9 %convolution_convert_fusion.1 = bf16[1024,2048]{1,0:T(8,128)(2,1)} fusion(bf16[1024,1024]{1,0:T(8,128)(2,1)S(1)} %get-tuple-element.50, bf16[1024,256]{1,0:T(8,128)(2,1)S(1)} %copy-done.75, bf16[640,512]{1,0:T(8,128)(2,1)S(1)} %copy-done.72, bf16[640,512]{1,0:T(8,128)(2,1)S(1)} %copy-done.74, bf16[1280,512]{1,0:T(8,128)(2,1)S(1)} %copy-done.58, ...), kind=kOutput, calls=%fused_computation.19 | convolution fusion | flops 5407506432 | bytes 12058624 | tf_op jit(solution)/shard_map/dot_general | solution.py:67
  388.6 8.9 %collective-permute-done.65 = bf16[2,256,1024]{2,1,0:T(8,128)(2,1)} collective-permute-done((bf16[2,256,1024]{2,1,0:T(8,128)(2,1)}, bf16[2,256,1024]{2,1,0:T(8,128)(2,1)}, u32[]{:S(2)}, u32[]{:S(2)}) %collective-permute-start.65) | collective-permute-done | bytes 1048608 | tf_op jit(solution)/shard_map/ppermute | solution.py:158
  401.0 20.4 %collective-permute-done.73 = bf16[2,256,1024]{1,2,0:T(8,128)(2,1)S(1)} collective-permute-done((bf16[2,256,1024]{1,2,0:T(8,128)(2,1)}, bf16[2,256,1024]{1,2,0:T(8,128)(2,1)S(1)}, u32[]{:S(2)}, u32[]{:S(2)}) %collective-permute-start.73) | collective-permute-done | bytes 1048608 | tf_op jit(solution)/shard_map/ppermute | solution.py:158
  422.6 10.0 %collective-permute-done.57 = bf16[256,1024]{0,1:T(8,128)(2,1)S(1)} collective-permute-done((bf16[256,1024]{0,1:T(8,128)(2,1)S(1)}, bf16[256,1024]{0,1:T(8,128)(2,1)S(1)}, u32[]{:S(2)}, u32[]{:S(2)}) %collective-permute-start.57) | collective-permute-done | bytes 524320 | tf_op jit(solution)/shard_map/ppermute | solution.py:158
  464.1 9.8 %collective-permute-done.42 = bf16[512,512]{1,0:T(8,128)(2,1)S(1)} collective-permute-done((bf16[512,512]{1,0:T(8,128)(2,1)S(1)}, bf16[512,512]{1,0:T(8,128)(2,1)S(1)}, u32[]{:S(2)}, u32[]{:S(2)}) %collective-permute-start.42) | collective-permute-done | bytes 524320 | tf_op jit(solution)/shard_map/ppermute | solution.py:158
  474.4 10.8 %collective-permute-done.43 = bf16[512,512]{1,0:T(8,128)(2,1)S(1)} collective-permute-done((bf16[512,512]{1,0:T(8,128)(2,1)S(1)}, bf16[512,512]{1,0:T(8,128)(2,1)S(1)}, u32[]{:S(2)}, u32[]{:S(2)}) %collective-permute-start.43) | collective-permute-done | bytes 524320 | tf_op jit(solution)/shard_map/ppermute | solution.py:158
  488.1 8.3 %collective-permute-done.32 = bf16[512,512]{1,0:T(8,128)(2,1)S(1)} collective-permute-done((bf16[512,512]{1,0:T(8,128)(2,1)S(1)}, bf16[512,512]{1,0:T(8,128)(2,1)S(1)}, u32[]{:S(2)}, u32[]{:S(2)}) %collective-permute-start.32) | collective-permute-done | bytes 524320 | tf_op jit(solution)/shard_map/ppermute | solution.py:158
  519.4 9.1 %collective-permute-done.46 = bf16[512,512]{1,0:T(8,128)(2,1)S(1)} collective-permute-done((bf16[512,512]{1,0:T(8,128)(2,1)S(1)}, bf16[512,512]{1,0:T(8,128)(2,1)S(1)}, u32[]{:S(2)}, u32[]{:S(2)}) %collective-permute-start.46) | collective-permute-done | bytes 524320 | tf_op jit(solution)/shard_map/ppermute | solution.py:207
  543.1 12.4 %collective-permute-start.47 = (bf16[512,512]{1,0:T(8,128)(2,1)}, bf16[512,512]{1,0:T(8,128)(2,1)}, u32[]{:S(2)}, u32[]{:S(2)}) collective-permute-start(bf16[512,512]{1,0:T(8,128)(2,1)} %get-tuple-element.73), channel_id=1, source_target_pairs={{0,4},{4,8},{8,12},{1,5},{5,9},{9,13},{2,6},{6,10},{10,14},{3,7},{... | collective-permute-start | bytes 1572872 | tf_op jit(solution)/shard_map/ppermute | solution.py:207
  584.0 8.6 %collective-permute-done.40 = bf16[512,512]{1,0:T(8,128)(2,1)S(1)} collective-permute-done((bf16[512,512]{1,0:T(8,128)(2,1)S(1)}, bf16[512,512]{1,0:T(8,128)(2,1)S(1)}, u32[]{:S(2)}, u32[]{:S(2)}) %collective-permute-start.40) | collective-permute-done | bytes 524320 | tf_op jit(solution)/shard_map/ppermute | solution.py:208
  (446 shorter events, 304.1 us)
Async XLA Ops:
  0.7 32.4 %collective-permute-start.17 = (bf16[512,512]{1,0:T(8,128)(2,1)}, bf16[512,512]{1,0:T(8,128)(2,1)}, u32[]{:S(2)}, u32[]{:S(2)}) collective-permute-start(bf16[512,512]{1,0:T(8,128)(2,1)} %param.15), channel_id=1, source_target_pairs={{0,4},{4,8},{8,12},{1,5},{5,9},{9,13},{2,6},{6,10},{10,14},{3,7},{... | collective-permute-start | bytes 1572872 | tf_op jit(solution)/shard_map/ppermute | solution.py:176
  10.7 48.7 %collective-permute-start.16 = (s32[1,512]{1,0:T(1,128)}, s32[1,512]{1,0:T(1,128)S(1)}, u32[]{:S(2)}, u32[]{:S(2)}) collective-permute-start(s32[1,512]{1,0:T(1,128)} %param.14), channel_id=1, source_target_pairs={{0,16},{16,0},{1,17},{17,1},{2,18},{18,2},{3,19},{19,3},{4,20},{20... | collective-permute-start | bytes 6152 | tf_op jit(solution)/shard_map/ppermute | solution.py:158
  33.0 28.1 %collective-permute-start.21 = (bf16[512,512]{1,0:T(8,128)(2,1)}, bf16[512,512]{1,0:T(8,128)(2,1)}, u32[]{:S(2)}, u32[]{:S(2)}) collective-permute-start(bf16[512,512]{1,0:T(8,128)(2,1)} %collective-permute-done.17), channel_id=1, source_target_pairs={{4,8},{8,12},{5,9},{9,13},{6,10},{10,14},{7,11},{11,15},{20,24},{2... | collective-permute-start | bytes 1572872 | tf_op jit(solution)/shard_map/ppermute | solution.py:176
  59.4 71.8 %collective-permute-start.12 = (bf16[512,1792]{1,0:T(8,128)(2,1)}, bf16[512,1792]{1,0:T(8,128)(2,1)}, u32[]{:S(2)}, u32[]{:S(2)}) collective-permute-start(bf16[512,1792]{1,0:T(8,128)(2,1)} %get-tuple-element.95), channel_id=1, source_target_pairs={{0,1},{1,0},{2,3},{3,2},{4,5},{5,4},{6,7},{7,6},{8,9},{9,8},{10,11... | collective-permute-start | bytes 5505032 | tf_op jit(solution)/shard_map/ppermute | solution.py:158
  61.2 110.5 %collective-permute-start.13 = (bf16[512,1792]{1,0:T(8,128)(2,1)}, bf16[512,1792]{1,0:T(8,128)(2,1)}, u32[]{:S(2)}, u32[]{:S(2)}) collective-permute-start(bf16[512,1792]{1,0:T(8,128)(2,1)} %get-tuple-element.95), channel_id=1, source_target_pairs={{0,2},{1,3},{2,0},{3,1},{4,6},{5,7},{6,4},{7,5},{8,10},{9,11},{10,... | collective-permute-start | bytes 5505032 | tf_op jit(solution)/shard_map/ppermute | solution.py:158
  87.8 38.9 %collective-permute-start.24 = (bf16[512,512]{1,0:T(8,128)(2,1)S(1)}, bf16[512,512]{1,0:T(8,128)(2,1)S(1)}, u32[]{:S(2)}, u32[]{:S(2)}) collective-permute-start(bf16[512,512]{1,0:T(8,128)(2,1)S(1)} %get-tuple-element.89), channel_id=1, source_target_pairs={{0,2},{1,3},{2,0},{3,1},{4,6},{5,7},{6,4},{7,5},{8,10},{9,11},{10,... | collective-permute-start | bytes 1572872 | tf_op jit(solution)/shard_map/ppermute | solution.py:158
  88.9 74.3 %collective-permute-start.28 = (bf16[1280,512]{1,0:T(8,128)(2,1)}, bf16[1280,512]{1,0:T(8,128)(2,1)S(1)}, u32[]{:S(2)}, u32[]{:S(2)}) collective-permute-start(bf16[1280,512]{1,0:T(8,128)(2,1)} %pad_maximum_fusion.10), channel_id=1, source_target_pairs={{0,2},{1,3},{2,0},{3,1},{4,6},{5,7},{6,4},{7,5},{8,10},{9,11},{10,... | collective-permute-start | bytes 3932168 | tf_op jit(solution)/shard_map/ppermute | solution.py:158
  126.7 43.1 %collective-permute-start.27 = (bf16[1280,512]{1,0:T(8,128)(2,1)}, bf16[1280,512]{1,0:T(8,128)(2,1)}, u32[]{:S(2)}, u32[]{:S(2)}) collective-permute-start(bf16[1280,512]{1,0:T(8,128)(2,1)} %pad_maximum_fusion.10), channel_id=1, source_target_pairs={{0,1},{1,0},{2,3},{3,2},{4,5},{5,4},{6,7},{7,6},{8,9},{9,8},{10,11... | collective-permute-start | bytes 3932168 | tf_op jit(solution)/shard_map/ppermute | solution.py:158
  130.0 79.5 %collective-permute-start.26 = (bf16[512,2048]{1,0:T(8,128)(2,1)}, bf16[512,2048]{1,0:T(8,128)(2,1)}, u32[]{:S(2)}, u32[]{:S(2)}) collective-permute-start(bf16[512,2048]{1,0:T(8,128)(2,1)} %pad_maximum_fusion.8), channel_id=1, source_target_pairs={{0,16},{16,0},{1,17},{17,1},{2,18},{18,2},{3,19},{19,3},{4,20},{20... | collective-permute-start | bytes 6291464 | tf_op jit(solution)/shard_map/ppermute | solution.py:158
  131.3 43.1 %collective-permute-start.10 = (bf16[512,512]{1,0:T(8,128)(2,1)}, bf16[512,512]{1,0:T(8,128)(2,1)}, u32[]{:S(2)}, u32[]{:S(2)}) collective-permute-start(bf16[512,512]{1,0:T(8,128)(2,1)} %get-tuple-element.92), channel_id=1, source_target_pairs={{0,3},{1,2},{2,1},{3,0},{4,7},{5,6},{6,5},{7,4},{8,11},{9,10},{10,... | collective-permute-start | bytes 1572872 | tf_op jit(solution)/shard_map/ppermute | solution.py:158
  163.3 35.8 %collective-permute-start.14 = (bf16[256,1792]{1,0:T(8,128)(2,1)}, bf16[256,1792]{1,0:T(8,128)(2,1)S(1)}, u32[]{:S(2)}, u32[]{:S(2)}) collective-permute-start(bf16[256,1792]{1,0:T(8,128)(2,1)} %slice.273), channel_id=1, source_target_pairs={{0,2},{1,3},{2,0},{3,1},{4,6},{5,7},{6,4},{7,5},{8,10},{9,11},{10,... | collective-permute-start | bytes 2752520 | tf_op jit(solution)/shard_map/ppermute | solution.py:158
  317.7 67.8 %collective-permute-start.56 = (bf16[2,256,1024]{1,2,0:T(8,128)(2,1)}, bf16[2,256,1024]{1,2,0:T(8,128)(2,1)}, u32[]{:S(2)}, u32[]{:S(2)}) collective-permute-start(bf16[2,256,1024]{1,2,0:T(8,128)(2,1)} %pad_maximum_fusion.11), channel_id=1, source_target_pairs={{0,1},{1,0},{2,3},{3,2},{4,5},{5,4},{6,7},{7,6},{8,9},{9,8},{10,11... | collective-permute-start | bytes 3145736 | tf_op jit(solution)/shard_map/ppermute | solution.py:158
  320.3 66.9 %collective-permute-start.58 = (bf16[2,256,1024]{1,2,0:T(8,128)(2,1)}, bf16[2,256,1024]{1,2,0:T(8,128)(2,1)}, u32[]{:S(2)}, u32[]{:S(2)}) collective-permute-start(bf16[2,256,1024]{1,2,0:T(8,128)(2,1)} %copy.62), channel_id=1, source_target_pairs={{0,2},{1,3},{2,0},{3,1},{4,6},{5,7},{6,4},{7,5},{8,10},{9,11},{10,... | collective-permute-start | bytes 3145736 | tf_op jit(solution)/shard_map/ppermute | solution.py:158
  322.0 37.5 %collective-permute-start.61 = (f32[1,1792]{1,0:T(1,128)S(1)}, f32[1,1792]{1,0:T(1,128)S(1)}, u32[]{:S(2)}, u32[]{:S(2)}) collective-permute-start(f32[1,1792]{1,0:T(1,128)S(1)} %broadcast_in_dim.108), channel_id=1, source_target_pairs={{0,1},{1,0},{2,3},{3,2},{4,5},{5,4},{6,7},{7,6},{8,9},{9,8},{10,11... | collective-permute-start | bytes 21512 | tf_op jit(solution)/shard_map/ppermute | solution.py:158
  383.3 38.1 %collective-permute-start.73 = (bf16[2,256,1024]{1,2,0:T(8,128)(2,1)}, bf16[2,256,1024]{1,2,0:T(8,128)(2,1)S(1)}, u32[]{:S(2)}, u32[]{:S(2)}) collective-permute-start(bf16[2,256,1024]{1,2,0:T(8,128)(2,1)} %copy.69), channel_id=1, source_target_pairs={{0,2},{1,3},{2,0},{3,1},{4,6},{5,7},{6,4},{7,5},{8,10},{9,11},{10,... | collective-permute-start | bytes 3145736 | tf_op jit(solution)/shard_map/ppermute | solution.py:158
  385.5 36.5 %collective-permute-start.71 = (bf16[2,256,1024]{1,2,0:T(8,128)(2,1)}, bf16[2,256,1024]{1,2,0:T(8,128)(2,1)S(1)}, u32[]{:S(2)}, u32[]{:S(2)}) collective-permute-start(bf16[2,256,1024]{1,2,0:T(8,128)(2,1)} %pad_maximum_fusion.14), channel_id=1, source_target_pairs={{0,1},{1,0},{2,3},{3,2},{4,5},{5,4},{6,7},{7,6},{8,9},{9,8},{10,11... | collective-permute-start | bytes 3145736 | tf_op jit(solution)/shard_map/ppermute | solution.py:158
  387.3 70.7 %collective-permute-start.41 = (bf16[512,2048]{1,0:T(8,128)(2,1)}, bf16[512,2048]{1,0:T(8,128)(2,1)S(1)}, u32[]{:S(2)}, u32[]{:S(2)}) collective-permute-start(bf16[512,2048]{1,0:T(8,128)(2,1)} %slice.293), channel_id=1, source_target_pairs={{0,16},{16,0},{1,17},{17,1},{2,18},{18,2},{3,19},{19,3},{4,20},{20... | collective-permute-start | bytes 6291464 | tf_op jit(solution)/shard_map/ppermute | solution.py:158
  397.5 62.5 %collective-permute-start.31 = (bf16[512,2048]{1,0:T(8,128)(2,1)}, bf16[512,2048]{1,0:T(8,128)(2,1)S(1)}, u32[]{:S(2)}, u32[]{:S(2)}) collective-permute-start(bf16[512,2048]{1,0:T(8,128)(2,1)} %slice.286), channel_id=1, source_target_pairs={{0,16},{16,0},{1,17},{17,1},{2,18},{18,2},{3,19},{19,3},{4,20},{20... | collective-permute-start | bytes 6291464 | tf_op jit(solution)/shard_map/ppermute | solution.py:158
  399.0 33.6 %collective-permute-start.57 = (bf16[256,1024]{0,1:T(8,128)(2,1)S(1)}, bf16[256,1024]{0,1:T(8,128)(2,1)S(1)}, u32[]{:S(2)}, u32[]{:S(2)}) collective-permute-start(bf16[256,1024]{0,1:T(8,128)(2,1)S(1)} %fusion.43), channel_id=1, source_target_pairs={{0,2},{1,3},{2,0},{3,1},{4,6},{5,7},{6,4},{7,5},{8,10},{9,11},{10,... | collective-permute-start | bytes 1572872 | tf_op jit(solution)/shard_map/ppermute | solution.py:158
  447.4 90.5 %collective-permute-start.60 = (bf16[512,768]{0,1:T(8,128)(2,1)S(1)}, bf16[512,768]{0,1:T(8,128)(2,1)S(1)}, u32[]{:S(2)}, u32[]{:S(2)}) collective-permute-start(bf16[512,768]{0,1:T(8,128)(2,1)S(1)} %fusion.42), channel_id=1, source_target_pairs={{0,16},{16,0},{1,17},{17,1},{2,18},{18,2},{3,19},{19,3},{4,20},{20... | collective-permute-start | bytes 2359304 | tf_op jit(solution)/shard_map/ppermute | solution.py:158
  456.3 60.0 %collective-permute-start.64 = (bf16[256,512]{1,0:T(8,128)(2,1)S(1)}, bf16[256,512]{1,0:T(8,128)(2,1)S(1)}, u32[]{:S(2)}, u32[]{:S(2)}) collective-permute-start(bf16[256,512]{1,0:T(8,128)(2,1)S(1)} %fusion.51), channel_id=1, source_target_pairs={{0,16},{16,0},{1,17},{17,1},{2,18},{18,2},{3,19},{19,3},{4,20},{20... | collective-permute-start | bytes 786440 | tf_op jit(solution)/shard_map/ppermute | solution.py:158
  507.4 73.0 %collective-permute-start.69 = (bf16[512,1024]{1,0:T(8,128)(2,1)}, bf16[512,1024]{1,0:T(8,128)(2,1)}, u32[]{:S(2)}, u32[]{:S(2)}) collective-permute-start(bf16[512,1024]{1,0:T(8,128)(2,1)} %pad_maximum_fusion.13), channel_id=1, source_target_pairs={{0,16},{16,0},{1,17},{17,1},{2,18},{18,2},{3,19},{19,3},{4,20},{20... | collective-permute-start | bytes 3145736 | tf_op jit(solution)/shard_map/ppermute | solution.py:158
  519.4 80.5 %collective-permute-start.75 = (bf16[1024,512]{1,0:T(8,128)(2,1)}, bf16[1024,512]{1,0:T(8,128)(2,1)}, u32[]{:S(2)}, u32[]{:S(2)}) collective-permute-start(bf16[1024,512]{1,0:T(8,128)(2,1)} %maximum_bitcast_fusion), channel_id=1, source_target_pairs={{0,16},{16,0},{1,17},{17,1},{2,18},{18,2},{3,19},{19,3},{4,20},{20... | collective-permute-start | bytes 3145736 | tf_op jit(solution)/shard_map/ppermute | solution.py:158
  528.5 27.9 %collective-permute-start.38 = (bf16[512,512]{1,0:T(8,128)(2,1)S(1)}, bf16[512,512]{1,0:T(8,128)(2,1)S(1)}, u32[]{:S(2)}, u32[]{:S(2)}) collective-permute-start(bf16[512,512]{1,0:T(8,128)(2,1)S(1)} %get-tuple-element.83), channel_id=1, source_target_pairs={{12,8},{13,9},{14,10},{15,11},{28,24},{29,25},{30,26},{31,27}} | collective-permute-start | bytes 1572872 | tf_op jit(solution)/shard_map/ppermute | solution.py:208
  (133 other events, 2265.7 us)

commit v3 on v2

--- a/solution.py
+++ b/solution.py
@@ -7,9 +7,9 @@
 from jax.experimental.pallas import tpu as pltpu
 from jax.sharding import PartitionSpec as P
 
+
 HEAD_DIM = 64
 ROT = 32
-PACK = 512
 
 
 EPS = 1e-05
@@ -158,123 +158,191 @@
     return lax.ppermute(array, axis, [(i, i ^ step) for i in range(lax.axis_size(axis))])
 
 
-def total_over(array, axes):
+def total_over(array, axes, *late):
+    number = 0
     for axis in axes:
         step = 1
         while step < lax.axis_size(axis):
-            array = array + swap(array, axis, step)
+            number += 1
+            other = swap(array, axis, step)
+            if number <= len(late):
+                other = lax.optimization_barrier((other, late[number - 1]))[0]
+            array = array + other
             step *= 2
     return array
 
 
-def line_gather(block, axis):
-    count = lax.axis_size(axis)
-    here = lax.axis_index(axis)
-    ups = [block]
-    downs = [block]
-    for step in range(count - 1):
-        ups.append(lax.ppermute(ups[-1], axis, [(i, i + 1) for i in range(step, count - 1)]))
-        downs.append(
-            lax.ppermute(downs[-1], axis, [(i + 1, i) for i in range(0, count - 1 - step)])
-        )
-    zero = (0,) * block.ndim
-    stacked = jnp.zeros((count,) + block.shape, block.dtype)
-    stacked = lax.dynamic_update_slice(stacked, block[None], (here,) + zero)
-    for step in range(1, count):
-        piece = jnp.where(here >= step, ups[step], downs[count - step])
-        stacked = lax.dynamic_update_slice(stacked, piece[None], ((here - step) % count,) + zero)
-    return stacked
-
-
-def line_scatter(blocks, axis):
-    count = lax.axis_size(axis)
-    here = lax.axis_index(axis)
-
-    def pick(index):
-        return lax.dynamic_index_in_dim(blocks, jnp.clip(index, 0, count - 1), 0, keepdims=False)
-
-    total = pick(here).astype(jnp.float32)
-    if count == 1:
-        return total
-    up = None
-    down = None
-    for step in range(count - 1):
-        send_up = pick(here + count - 1 - step)
-        send_down = pick(here - (count - 1) + step)
-        if step:
-            send_up = add_wide(send_up, up)
-            send_down = add_wide(send_down, down)
-        up = lax.ppermute(send_up, axis, [(i, i + 1) for i in range(0, step + 1)])
-        down = lax.ppermute(
-            send_down, axis, [(i + 1, i) for i in range(count - 2 - step, count - 1)]
-        )
-    return total + up.astype(jnp.float32) + down.astype(jnp.float32)
+def after(value, *others):
+    return lax.optimization_barrier((value,) + others)[0]
 
 
 def grid_gather(block):
     count = lax.axis_size("col")
     if count != 4:
-        return [block] + [swap(block, "col", step) for step in range(1, count)]
+        got = [swap(block, "col", step) for step in range(1, count)]
+        return [block] + got, got
     cut = block.shape[0] // 2
     by_one = swap(block, "col", 1)
     by_two = swap(block, "col", 2)
     low = swap(by_one[:cut], "col", 2)
     high = swap(by_two[cut:], "col", 1)
-    return [block, by_one, by_two, jnp.concatenate([low, high])]
-
-
-def grid_scatter(part):
+    return [block, by_one, by_two, jnp.concatenate([low, high])], [by_one, by_two]
+
+
+def scatter_first(part):
     count = lax.axis_size("col")
     size = part.shape[0] // count
     blocks = part.reshape(count, size, part.shape[1])
     if count != 4:
-        total = blocks[0]
-        for step in range(1, count):
-            total = add_wide(total, swap(blocks[step], "col", step))
-        return total
+        return [blocks[0]], [swap(blocks[step], "col", step) for step in range(1, count)]
     cut = size // 2
     low = swap(jnp.stack([blocks[1, :cut], blocks[3, :cut]]), "col", 1)
     high = swap(jnp.stack([blocks[2, cut:], blocks[3, cut:]]), "col", 2)
-    low_last = swap(add_wide(blocks[2, :cut], low[1]), "col", 2)
-    high_last = swap(add_wide(blocks[1, cut:], high[1]), "col", 1)
-    wide = lambda array: array.astype(jnp.float32)
-    return jnp.concatenate(
-        [
-            (wide(blocks[0, :cut]) + wide(low[0]) + wide(low_last)).astype(part.dtype),
-            (wide(blocks[0, cut:]) + wide(high[0]) + wide(high_last)).astype(part.dtype),
-        ]
-    )
-
-
-def spread_tokens(block):
+    return [blocks[0, :cut], blocks[0, cut:], blocks[2, :cut], blocks[1, cut:]], [low, high]
+
+
+def scatter_second(kept, got):
+    if lax.axis_size("col") != 4:
+        return [], kept + got
+    low, high = got
+    low_sum = add_wide(kept[2], low[1])
+    high_sum = add_wide(kept[3], high[1])
+    low_last = swap(low_sum, "col", 2)
+    high_last = swap(high_sum, "col", 1)
+    return [low_sum, high_sum], [kept[0], low[0], low_last, kept[1], high[0], high_last]
+
+
+def scatter_last(parts):
+    def total(arrays):
+        out = arrays[0].astype(jnp.float32)
+        for array in arrays[1:]:
+            out = out + array.astype(jnp.float32)
+        return out.astype(arrays[0].dtype)
+
+    if lax.axis_size("col") != 4:
+        return total(parts)
+    return jnp.concatenate([total(parts[:3]), total(parts[3:])])
+
+
+def place(row, col, n_col):
+    return row * n_col + col
+
+
+def spread_start(block):
     n_col = lax.axis_size("col")
+    n_row = lax.axis_size("row")
+    deep = n_row // n_col
+    pieces = []
+    for low in range(deep):
+        for step in range(n_col):
+            pairs = []
+            for to_row in range(n_row):
+                for to_col in range(n_col):
+                    from_row = to_col * deep + ((to_row % deep) ^ low)
+                    from_col = (to_row // deep) ^ step
+                    pairs.append(
+                        (place(from_row, from_col, n_col), place(to_row, to_col, n_col))
+                    )
+            pieces.append(lax.ppermute(block, ("row", "col"), pairs))
+    return pieces
+
+
+def spread_finish(pieces):
+    n_col = lax.axis_size("col")
+    deep = lax.axis_size("row") // n_col
+    row = lax.axis_index("row")
+    tokens, width = pieces[0].shape
+    wide = jnp.zeros((deep * tokens, n_col * width), pieces[0].dtype)
+    offset = (row // deep) ^ lax.axis_index("col")
+    for number, piece in enumerate(pieces):
+        at_row = ((row % deep) ^ (number // n_col)) * tokens
+        at_col = (offset ^ (number % n_col)) * width
+        wide = lax.dynamic_update_slice(wide, piece, (at_row, at_col))
+    return wide
+
+
+def dp_parts(own):
+    return [own] + [swap(own, "dp", step) for step in range(1, lax.axis_size("dp"))]
+
+
+def collect_first(partial):
     n_dp = lax.axis_size("dp")
-    col = lax.axis_index("col")
-    width = block.shape[1]
-    groups = line_gather(block, "row").reshape(n_col, -1, width)
-    take = lambda step: lax.dynamic_index_in_dim(groups, col ^ step, 0, keepdims=False)
-    pieces = [take(0)] + [swap(take(step), "col", step) for step in range(1, n_col)]
-    own = jnp.concatenate(pieces, axis=1)
-    return jnp.concatenate([own] + [swap(own, "dp", step) for step in range(1, n_dp)])
-
-
-def collect_tokens(partial):
-    n_col = lax.axis_size("col")
-    n_dp = lax.axis_size("dp")
-    n_row = lax.axis_size("row")
-    col = lax.axis_index("col")
     tokens = partial.shape[0] // n_dp
-    width = partial.shape[1] // n_col
     summed = partial[:tokens]
     for step in range(1, n_dp):
-        summed = add_wide(summed, swap(partial[step * tokens : (step + 1) * tokens], "dp", step))
-    groups = jnp.zeros((n_col, tokens, width), partial.dtype)
+        other = swap(partial[step * tokens : (step + 1) * tokens], "dp", step)
+        summed = add_wide(summed, other)
+    return summed
+
+
+def collect_second(summed):
+    n_col = lax.axis_size("col")
+    col = lax.axis_index("col")
+    tokens = summed.shape[0]
+    width = summed.shape[1] // n_col
+    groups = jnp.zeros((n_col, tokens, width), summed.dtype)
     for step in range(n_col):
         piece = summed[:, step * width : (step + 1) * width]
         if step:
             piece = swap(piece, "col", step)
         groups = lax.dynamic_update_slice(groups, piece[None], (col ^ step, 0, 0))
-    return line_scatter(groups.reshape(n_row, -1, width), "row")
+    return groups
+
+
+def collect_third(groups):
+    n_row = lax.axis_size("row")
+    row = lax.axis_index("row")
+    blocks = groups.reshape(n_row, -1, groups.shape[-1])
+    take = lambda step: lax.dynamic_index_in_dim(blocks, row ^ step, 0, keepdims=False)
+    held = {step: take(step) for step in range(n_row)}
+    bit = 1
+    while bit < n_row:
+        sent = jnp.stack([held[step] for step in sorted(held) if step & bit])
+        got = swap(sent, "row", bit)
+        kept = [step for step in sorted(held) if not step & bit]
+        last = 2 * bit >= n_row
+        held = {
+            step: held[step].astype(jnp.float32) + got[place].astype(jnp.float32)
+            for place, step in enumerate(kept)
+        }
+        if not last:
+            held = {step: value.astype(groups.dtype) for step, value in held.items()}
+        bit *= 2
+    return held[0].astype(jnp.float32)
+
+
+def late_kernel(*refs):
+    out_ref = refs[-1]
+    count = len(refs) // 4
+    split = refs[count].shape[1]
+
+    def total(lefts, rights):
+        out = dot_tn(lefts[0][...], rights[0][...])
+        for left, right in zip(lefts[1:], rights[1:]):
+            out = out + dot_tn(left[...], right[...])
+        return out.astype(jnp.bfloat16)
+
+    out_ref[:, :split] = total(refs[:count], refs[count : 2 * count])
+    out_ref[:, split:] = total(refs[2 * count : 3 * count], refs[3 * count : 4 * count])
+
+
+def late_grads(normed_parts, grad_qkv, grad_parts, attended):
+    tokens, full = normed_parts[0].shape
+    count = len(normed_parts)
+    columns = grad_qkv.shape[1] + attended.shape[1]
+    tile = 512
+    left = [pl.BlockSpec((tokens, tile), lambda i: (0, i))] * count
+    right = lambda array: [
+        pl.BlockSpec((tokens, array.shape[1]), lambda i, part=part: (part, 0))
+        for part in range(count)
+    ]
+    return pl.pallas_call(
+        late_kernel,
+        grid=(full // tile,),
+        in_specs=left + right(grad_qkv) + left + right(attended),
+        out_specs=pl.BlockSpec((tile, columns), lambda i: (i, 0)),
+        out_shape=jax.ShapeDtypeStruct((full, columns), jnp.bfloat16),
+    )(*normed_parts, *[grad_qkv] * count, *grad_parts, *[attended] * count)
 
 
 def half_of(array, axis):
@@ -318,54 +386,111 @@
     full_width = n_col * width
     qkv_cols = qkv_weight.shape[1] // n_dp
     att_cols = dense_weight.shape[0] // n_dp
-    grad_rows = spread_tokens(grad_output)
-    in_half = jnp.concatenate([half_of(qkv_weight, 1), half_of(fc1_weight, 1)], axis=1)
+    wide_in = inputs.astype(jnp.float32)
+    own_sums = jnp.stack([jnp.sum(wide_in, axis=1), jnp.sum(wide_in * wide_in, axis=1)])
+    scales = jnp.stack([norm_gain, norm_bias])
+    scales = jnp.concatenate(
+        [scales]
+        + [swap(scales, "col", step) for step in range(1, n_col)],
+        axis=1,
+    )
+    in_pieces = spread_start(inputs)
+    fc1_blocks, fc1_early = grid_gather(half_of(fc1_weight, 1))
+    grad_pieces = spread_start(grad_output)
     back_half = jnp.concatenate([half_of(dense_weight, 0), half_of(fc2_weight, 0)], axis=0)
-    in_all = jnp.concatenate(grid_gather(in_half))
-    back_all = jnp.concatenate(grid_gather(back_half), axis=1)
-
-    wide_in = inputs.astype(jnp.float32)
-    sums = total_over(
-        jnp.stack([jnp.sum(wide_in, axis=1), jnp.sum(wide_in * wide_in, axis=1)]), ("col",)
-    )
-    row_mean = (sums[0] / full_width)[:, None]
-    row_square = (sums[1] / full_width)[:, None]
-    inv_std = lax.rsqrt(row_square - row_mean * row_mean + EPS)
-    centered = (wide_in - row_mean) * inv_std
-    normed = (centered * norm_gain + norm_bias).astype(jnp.bfloat16)
-    normed_rows = spread_tokens(normed)
-    seg_rows = jnp.concatenate([segment] + [swap(segment, "dp", step) for step in range(1, n_dp)])
+    back_blocks, back_early = grid_gather(after(back_half, *fc1_early))
+    qkv_blocks, _ = grid_gather(after(half_of(qkv_weight, 1), *back_early))
+    fc1_all = jnp.concatenate(fc1_blocks)
+    back_all = jnp.concatenate(back_blocks, axis=1)
+    qkv_all = jnp.concatenate(qkv_blocks)
+    seg_rows = jnp.concatenate(dp_parts(segment))
     cosines, sines = rotary_tables(seg_rows, qkv_cols)
 
-    projected = dot_nn(normed_rows, in_all)
-    pre_act = projected[:, qkv_cols:] + half_of(fc1_bias, 0)
+    def centre(wide_in, row_total, row_squares):
+        row_mean = (row_total / full_width)[:, None]
+        row_square = (row_squares / full_width)[:, None]
+        inv_std = lax.rsqrt(row_square - row_mean * row_mean + EPS)
+        return (wide_in - row_mean) * inv_std, inv_std
+
+    in_pieces = list(
+        lax.optimization_barrier(tuple(in_pieces) + (cosines, sines))[:-2]
+    )
+    wide_rows = spread_finish(in_pieces).astype(jnp.float32)
+    centered_rows, _ = centre(
+        wide_rows, jnp.sum(wide_rows, axis=1), jnp.sum(wide_rows * wide_rows, axis=1)
+    )
+    normed_own = (centered_rows * scales[:1] + scales[1:]).astype(jnp.bfloat16)
+    normed_parts = dp_parts(normed_own)
+    normed_rows = jnp.concatenate(normed_parts)
+
+    fc1_shift = half_of(fc1_bias, 0)
+    pre_act = dot_nn(normed_rows, fc1_all) + fc1_shift
     hidden = gelu_tanh(pre_act).astype(jnp.bfloat16)
-    backed = dot_nt(grad_rows, back_all)
+    grad_pieces = list(lax.optimization_barrier(tuple(grad_pieces) + (normed_own,))[:-1])
+    grad_parts = dp_parts(spread_finish(grad_pieces))
+    grad_rows = jnp.concatenate(grad_parts)
+    fc2_part = dot_tn(grad_rows, hidden).astype(jnp.bfloat16)
+    fc2_kept, fc2_got = scatter_first(fc2_part)
+
+    backed = dot_nt(after(grad_rows, fc2_part), back_all)
     grad_att = backed[:, :att_cols].astype(jnp.bfloat16)
-    grad_fc2_t = grid_scatter(dot_tn(grad_rows, hidden).astype(jnp.bfloat16))
     grad_pre = (backed[:, att_cols:] * gelu_slope(pre_act)).astype(jnp.bfloat16)
-    grad_fc1 = grid_scatter(dot_tn(normed_rows, grad_pre).astype(jnp.bfloat16))
+    fc1_part = dot_tn(normed_rows, grad_pre).astype(jnp.bfloat16)
+    fc1_kept, fc1_got = scatter_first(fc1_part)
 
     attended, grad_qkv = attention(
-        projected[:, :qkv_cols], half_of(qkv_bias, 0), cosines, sines, seg_rows, grad_att
-    )
-    acts = jnp.concatenate([attended, hidden], axis=1)
-    mixed = collect_tokens(dot_nn(acts, back_all).astype(jnp.bfloat16))
-    output = (wide_in + (mixed + dense_bias + fc2_bias)).astype(jnp.bfloat16)
-
-    grad_first = jnp.concatenate([grad_qkv, grad_pre], axis=1)
-    grad_normed = collect_tokens(dot_nt(grad_first, in_all).astype(jnp.bfloat16))
-    late = grid_scatter(
-        jnp.concatenate(
-            [
-                dot_tn(normed_rows, grad_qkv).astype(jnp.bfloat16),
-                dot_tn(grad_rows, attended).astype(jnp.bfloat16),
-            ],
-            axis=1,
-        )
-    )
-    grad_in_b = total_over(jnp.sum(grad_first.astype(jnp.float32), axis=0, keepdims=True), ("col",))
-
+        after(dot_nn(normed_rows, qkv_all), fc1_part),
+        half_of(qkv_bias, 0),
+        cosines,
+        sines,
+        seg_rows,
+        grad_att,
+    )
+    bias_sums = jnp.concatenate(
+        [
+            jnp.sum(grad_qkv.astype(jnp.float32), axis=0, keepdims=True),
+            jnp.sum(grad_pre.astype(jnp.float32), axis=0, keepdims=True),
+        ],
+        axis=1,
+    )
+    fc2_got = list(lax.optimization_barrier((tuple(fc2_got), grad_qkv))[0])
+    fc2_sent, fc2_parts = scatter_second(fc2_kept, fc2_got)
+    fc1_got = list(lax.optimization_barrier((tuple(fc1_got), grad_qkv))[0])
+    fc1_sent, fc1_parts = scatter_second(fc1_kept, fc1_got)
+    norm_part = (
+        dot_nt(after(grad_qkv, *fc2_sent), qkv_all) + dot_nt(after(grad_pre, fc1_part), fc1_all)
+    ).astype(jnp.bfloat16)
+    norm_summed = collect_first(norm_part)
+    acts = after(jnp.concatenate([attended, hidden], axis=1), norm_summed, *fc1_sent)
+    mixed_part = dot_nn(acts, back_all).astype(jnp.bfloat16)
+    mixed_summed = after(collect_first(mixed_part), norm_summed)
+    norm_groups = collect_second(norm_summed)
+    mixed_groups = collect_second(mixed_summed)
+
+    late_part = late_grads(
+        normed_parts, after(grad_qkv, mixed_summed), grad_parts, attended
+    )
+    late_kept, late_got = scatter_first(late_part)
+    norm_groups = after(norm_groups, late_part)
+    grad_normed = collect_third(norm_groups)
+    mixed_groups = after(mixed_groups, norm_groups)
+    mixed = collect_third(mixed_groups)
+    late_got = list(lax.optimization_barrier((tuple(late_got), mixed_groups))[0])
+    late_sent, late_parts = scatter_second(late_kept, late_got)
+
+    fc2_parts = lax.optimization_barrier((tuple(fc2_parts), tuple(late_sent)))[0]
+    grad_fc2_t = scatter_last(list(fc2_parts))
+    fc1_parts = lax.optimization_barrier((tuple(fc1_parts), grad_fc2_t))[0]
+    grad_fc1 = scatter_last(list(fc1_parts))
+    wide = lambda array: array.astype(jnp.float32)
+    out_fc1 = wide(both_halves(grad_fc1, 1))
+    out_fc2 = wide(both_halves(grad_fc2_t.T, 0))
+    grad_normed = after(grad_normed, out_fc1, out_fc2, *late_sent)
+    late = scatter_last(list(lax.optimization_barrier((tuple(late_parts), grad_normed))[0]))
+
+    grad_in_b = total_over(bias_sums, ("col",), norm_groups, grad_fc1)
+    sums = total_over(own_sums, ("col",), scales, late_part)
+    centered, inv_std = centre(wide_in, sums[0], sums[1])
     scaled = grad_normed * norm_gain
     cross = total_over(
         jnp.stack([jnp.sum(scaled, axis=1), jnp.sum(scaled * centered, axis=1)]), ("col",)
@@ -374,17 +499,16 @@
     grad_input = grad_wide + inv_std * (
         scaled - (cross[0] / full_width)[:, None] - centered * (cross[1] / full_width)[:, None]
     )
-    norm_sums = total_over(
-        jnp.stack(
-            [
-                jnp.sum(grad_normed * centered, axis=0),
-                jnp.sum(grad_normed, axis=0),
-                jnp.sum(grad_wide, axis=0),
-            ]
-        ),
-        ("dp", "row"),
-    )
-    wide = lambda array: array.astype(jnp.float32)
+    own_norm = jnp.stack(
+        [
+            jnp.sum(grad_normed * centered, axis=0),
+            jnp.sum(grad_normed, axis=0),
+            jnp.sum(grad_wide, axis=0),
+        ]
+    )
+    norm_sums = total_over(own_norm, ("dp", "row"))
+    mixed = after(mixed, own_norm)
+    output = (wide_in + (mixed + dense_bias + fc2_bias)).astype(jnp.bfloat16)
     return (
         output,
         grad_input,
@@ -394,9 +518,9 @@
         both_halves(grad_in_b[0, :qkv_cols], 0),
         wide(both_halves(late[:, qkv_cols:].T, 0)),
         norm_sums[2],
-        wide(both_halves(grad_fc1, 1)),
+        out_fc1,
         both_halves(grad_in_b[0, qkv_cols:], 0),
-        wide(both_halves(grad_fc2_t.T, 0)),
+        out_fc2,
         norm_sums[2],
     )
 
@@ -431,4 +555,5 @@
         P("row", "col"),
         P("col"),
     )
+
     return jax.shard_map(body, mesh=mesh, in_specs=in_specs, out_specs=out_specs, check_vma=False)

time: 618 us -> 556 us (0.90)
  waiting for transfers between devices: 234 us -> 151 us
  starting transfers between devices: 111 us -> 141 us
  other arithmetic: 73.2 us -> 58.4 us
  Pallas kernels: 24.5 us -> 33.7 us
    ppermute x24 -> x8, waiting for transfers between devices: 58.8 us -> 11.6 us  [spread_start(): pieces.append(lax.ppermute(block, ('row', 'col'), pairs))]
    ppermute x52 -> x57, waiting for transfers between devices: 176 us -> 140 us  [swap(): lax.ppermute(array, axis, [(i, i ^ step) for i in range(lax.axis_size(axi...]
    ppermute x52 -> x57, starting transfers between devices: 48.2 us -> 80.1 us  [swap(): lax.ppermute(array, axis, [(i, i ^ step) for i in range(lax.axis_size(axi...]
    unnamed x177 -> x116, local copies, waits for them, and re-layouts: 31.5 us -> 44.4 us
    slice x9 -> x8, local copies, waits for them, and re-layouts: 17.6 us -> 6.65 us  [the longest x2 4.79 us: scatter_first(): blocks[0, cut:]]
    pallas_call x0 -> x1, Pallas kernels: none -> 9.25 us  [late_grads(): pl.pallas_call(late_kernel, grid=(full // tile,), in_specs=left + right(g...]
    reshape x2 -> x1, local copies, waits for them, and re-layouts: 7.92 us -> 0.02 us  [the longest x1 7.9 us: grid_scatter(): blocks = part.reshape(count, size, part.shape[1])]
    dynamic_update_slice x7 -> x0, other arithmetic: 7.4 us -> none  [the longest x6 6.34 us: line_gather(): lax.dynamic_update_slice(stacked, piece[None], ((here - step) % count,) +...]
  transfers between devices with their start and end apart: 76 -> 65, of which waited for: 29 -> 18; matrix products, arithmetic and copies ran while one was open for 25% -> 37% of each run, Pallas kernels for 0% -> 6%
where the time goes in v3:
time: 556 us; the launch traced here: 547 us
  waiting for transfers between devices  151 us (27%)
  starting transfers between devices  141 us (25%)
  local copies, waits for them, and re-layouts  84.7 us (15%)
  matrix products  74.8 us (13%)
  other arithmetic  58.4 us (11%)
  Pallas kernels  33.7 us (6%)
    ppermute x57, waiting for transfers between devices, swap(): lax.ppermute(array, axis, [(i, i ^ step) for i in range(lax.axis_size(axi...  140 us
    ppermute x57, starting transfers between devices, swap(): lax.ppermute(array, axis, [(i, i ^ step) for i in range(lax.axis_size(axi...  80.1 us
    ppermute x8, starting transfers between devices, spread_start(): pieces.append(lax.ppermute(block, ('row', 'col'), pairs))  61 us
    unnamed x116, local copies, waits for them, and re-layouts  44.4 us
    dot_general x3, matrix products, dot_nn(): return jnp.dot(left, right, preferred_element_type=jnp.float32)  26.4 us
    dot_general x2, matrix products, dot_tn(): lax.dot_general(left, right, (((0,), (0,)), ((), ())), preferred_element_...  25.3 us
    pallas_call x1, Pallas kernels, attention(): pl.pallas_call(attention_kernel, grid=(packs,), in_specs=[by_rows(columns...  24.5 us
    dot_general x3, matrix products, dot_nt(): lax.dot_general(left, right, (((1,), (1,)), ((), ())), preferred_element_...  23.1 us
  transfers between devices with their start and end apart: 65, of which 18 were waited for; matrix products, arithmetic and copies ran while one was open for 37% of the time, Pallas kernels for 6%

profile of v3, /device:TPU:0, one launch (start us, length us, event | category | flops | bytes accessed | tf_op | source)
XLA Modules:
  0.0 546.6 jit_solution(1767618192466777285)
XLA Ops:
  30.8 6.2 %collective-permute-start.3 = (bf16[512,512]{1,0:T(8,128)(2,1)S(1)}, bf16[512,512]{1,0:T(8,128)(2,1)S(1)}, u32[]{:S(2)}, u32[]{:S(2)}) collective-permute-start(bf16[512,512]{1,0:T(8,128)(2,1)S(1)} %copy-done.11), channel_id=1, source_target_pairs={{3,0},{7,1},{11,2},{15,3},{2,4},{6,5},{10,6},{14,7},{1,8},{5,9},{9... | collective-permute-start | bytes 1572872 | tf_op jit(solution)/shard_map/ppermute | solution.py:246
  44.0 11.5 %collective-permute-done.2 = bf16[512,512]{1,0:T(8,128)(2,1)S(1)} collective-permute-done((bf16[512,512]{1,0:T(8,128)(2,1)S(1)}, bf16[512,512]{1,0:T(8,128)(2,1)S(1)}, u32[]{:S(2)}, u32[]{:S(2)}) %collective-permute-start.2) | collective-permute-done | bytes 524320 | tf_op jit(solution)/shard_map/ppermute | solution.py:246
  55.6 10.9 %collective-permute-start.18 = (bf16[512,512]{1,0:T(8,128)(2,1)}, bf16[512,512]{1,0:T(8,128)(2,1)}, u32[]{:S(2)}, u32[]{:S(2)}) collective-permute-start(bf16[512,512]{1,0:T(8,128)(2,1)} %param.15), channel_id=1, source_target_pairs={{1,0},{5,1},{9,2},{13,3},{0,4},{4,5},{8,6},{12,7},{3,8},{7,9},{11,... | collective-permute-start | bytes 1572872 | tf_op jit(solution)/shard_map/ppermute | solution.py:246
  72.8 20.9 %collective-permute-start.19 = (bf16[512,512]{1,0:T(8,128)(2,1)}, bf16[512,512]{1,0:T(8,128)(2,1)S(1)}, u32[]{:S(2)}, u32[]{:S(2)}) collective-permute-start(bf16[512,512]{1,0:T(8,128)(2,1)} %param.15), channel_id=1, source_target_pairs={{2,0},{6,1},{10,2},{14,3},{3,4},{7,5},{11,6},{15,7},{0,8},{4,9},{8... | collective-permute-start | bytes 1572872 | tf_op jit(solution)/shard_map/ppermute | solution.py:246
  93.7 9.9 %collective-permute-start.20 = (bf16[512,512]{1,0:T(8,128)(2,1)}, bf16[512,512]{1,0:T(8,128)(2,1)S(1)}, u32[]{:S(2)}, u32[]{:S(2)}) collective-permute-start(bf16[512,512]{1,0:T(8,128)(2,1)} %param.15), channel_id=1, source_target_pairs={{3,0},{7,1},{11,2},{15,3},{2,4},{6,5},{10,6},{14,7},{1,8},{5,9},{9... | collective-permute-start | bytes 1572872 | tf_op jit(solution)/shard_map/ppermute | solution.py:246
  104.9 16.3 %collective-permute-start.50 = (f32[2,512]{1,0:T(2,128)S(1)}, f32[2,512]{1,0:T(2,128)S(1)}, u32[]{:S(2)}, u32[]{:S(2)}) collective-permute-start(f32[2,512]{1,0:T(2,128)S(1)} %pad_maximum_fusion.23), channel_id=1, source_target_pairs={{0,1},{1,0},{2,3},{3,2},{4,5},{5,4},{6,7},{7,6},{8,9},{9,8},{10,11... | collective-permute-start | bytes 12296 | tf_op jit(solution)/shard_map/ppermute | solution.py:158
  126.7 14.3 %collective-permute-start.12 = (bf16[1280,512]{1,0:T(8,128)(2,1)}, bf16[1280,512]{1,0:T(8,128)(2,1)}, u32[]{:S(2)}, u32[]{:S(2)}) collective-permute-start(bf16[1280,512]{1,0:T(8,128)(2,1)} %pad_maximum_fusion.5), channel_id=1, source_target_pairs={{0,2},{1,3},{2,0},{3,1},{4,6},{5,7},{6,4},{7,5},{8,10},{9,11},{10,... | collective-permute-start | bytes 3932168 | tf_op jit(solution)/shard_map/ppermute | solution.py:158
  148.8 32.6 %collective-permute-done.22 = bf16[256,1024]{1,0:T(8,128)(2,1)} collective-permute-done((bf16[256,1024]{1,0:T(8,128)(2,1)}, bf16[256,1024]{1,0:T(8,128)(2,1)}, u32[]{:S(2)}, u32[]{:S(2)}) %collective-permute-start.22) | collective-permute-done | bytes 524320 | tf_op jit(solution)/shard_map/ppermute | solution.py:158
  188.3 6.4 %collective-permute-done.23 = bf16[256,1024]{1,0:T(8,128)(2,1)S(1)} collective-permute-done((bf16[256,1024]{1,0:T(8,128)(2,1)S(1)}, bf16[256,1024]{1,0:T(8,128)(2,1)S(1)}, u32[]{:S(2)}, u32[]{:S(2)}) %collective-permute-start.23) | collective-permute-done | bytes 524320 | tf_op jit(solution)/shard_map/ppermute | solution.py:158
  205.3 10.7 %multiply_convert_fusion = (bf16[1024,1024]{1,0:T(8,128)(2,1)S(1)}, f32[1024,1024]{1,0:T(8,128)}) fusion(f32[1024]{0:T(1024)S(1)} %dynamic_slice.47, bf16[2048,1024]{1,0:T(8,128)(2,1)} %constant_dynamic-update-slice_fusion.5, bf16[512,2048]{1,0:T(8,128)(2,1)} %collective-permute-done.8.refs_1_, bf16[512,2048]{1,0:T(8,128)(2,1)} %fusion.3.refs_0_), kind=kOutput, calls=%fused_computation.24 | convolution fusion | flops 4313841664 | bytes 14684160 | tf_op jit(solution)/shard_map/dot_general | solution.py:67
  217.4 6.7 %convolution_convert_fusion.2 = bf16[2048,1024]{1,0:T(8,128)(2,1)S(1)} fusion(bf16[1024,1024]{1,0:T(8,128)(2,1)S(1)} %get-tuple-element.207, bf16[512,2048]{1,0:T(8,128)(2,1)} %collective-permute-done.21.refs_5_, bf16[512,2048]{1,0:T(8,128)(2,1)S(1)} %constant_dynamic-update-slice_fusion.10.refs_4_), kind=kOutput, calls=%fused_computation.27 | convolution fusion | flops 4305453056 | bytes 10485760 | tf_op jit(solution)/shard_map/dot_general | solution.py:61
  241.1 10.2 %fusion.51 = f32[1024,1280]{1,0:T(8,128)S(1)} fusion(bf16[1024,2048]{1,0:T(8,128)(2,1)} %pad_maximum_fusion.1, bf16[640,512]{1,0:T(8,128)(2,1)} %collective-permute-done.25, bf16[640,512]{1,0:T(8,128)(2,1)} %collective-permute-done.24, bf16[1280,512]{1,0:T(8,128)(2,1)} %collective-permute-done.12, bf16[1280,512]{1,0:T(8,128)(2,1)} %collective-permute-done.11, ...), kind=kOutput, calls=%fused_computation.201 | convolution fusion | flops 5394923520 | bytes 14680064 | tf_op jit(solution)/shard_map/dot_general | solution.py:55
  254.4 18.5 %convolution_convert_fusion.1 = bf16[2048,1024]{1,0:T(8,128)(2,1)S(1)} fusion(bf16[1024,1024]{1,0:T(8,128)(2,1)S(1)} %get-tuple-element.80, bf16[512,2048]{1,0:T(8,128)(2,1)} %collective-permute-done.8.refs_1_, bf16[512,2048]{1,0:T(8,128)(2,1)} %fusion.3.refs_0_), kind=kOutput, calls=%fused_computation.26 | convolution fusion | flops 4305453056 | bytes 10485760 | tf_op jit(solution)/shard_map/dot_general | solution.py:61
  277.0 6.8 %fusion.60 = f32[1024,2048]{1,0:T(8,128)} fusion(bf16[1024,1024]{1,0:T(8,128)(2,1)S(1)} %get-tuple-element.80, bf16[2048,1024]{1,0:T(8,128)(2,1)S(1)} %copy-done.30), kind=kOutput, calls=%fused_computation.209 | convolution fusion | flops 4294967296 | bytes 14680064 | tf_op jit(solution)/shard_map/dot_general | solution.py:55
  299.8 7.3 %fusion.13.qkv_ref = f32[1024,768]{1,0:T(8,128)} fusion(bf16[2048,768]{1,0:T(8,128)(2,1)S(1)} %constant_dynamic-update-slice_fusion, bf16[512,2048]{1,0:T(8,128)(2,1)} %collective-permute-done.8.refs_1_, bf16[512,2048]{1,0:T(8,128)(2,1)} %fusion.3.refs_0_), kind=kOutput, calls=%fused_computation.45 | convolution fusion | flops 3229614080 | bytes 10485760 | tf_op jit(solution)/shard_map/dot_general | solution.py:67
  307.2 24.5 %shard_map.220 = (bf16[1024,256]{1,0:T(8,128)(2,1)}, bf16[1024,768]{1,0:T(8,128)(2,1)}) custom-call(f32[1024,768]{1,0:T(8,128)} %fusion.13.qkv_ref, f32[1,768]{1,0:T(1,128)} %reshape.204.bias_ref, f32[1024,768]{1,0:T(8,128)} %pad_maximum_fusion.2.cos_ref, f32[1024,768]{1,0:T(8,128)} %pad_maximum_fusion.3.sin_ref, s32[2,512,1]{2,1,0:T(8,128)} %copy.41.seg_col_ref, ...), custom_call_target="tpu_custom_call" | custom-call | tf_op jit(solution)/shard_map/pallas_call | solution.py:120
  363.3 8.4 %convolution_convert_fusion = bf16[1024,2048]{1,0:T(8,128)(2,1)S(1)} fusion(bf16[1024,1280]{1,0:T(8,128)(2,1)S(1)} %pad_maximum_fusion.4, bf16[640,512]{1,0:T(8,128)(2,1)} %collective-permute-done.25, bf16[640,512]{1,0:T(8,128)(2,1)} %collective-permute-done.24, bf16[1280,512]{1,0:T(8,128)(2,1)} %collective-permute-done.12, ...), kind=kOutput, calls=%fused_computation.25 | convolution fusion | flops 5397020672 | bytes 12058624 | tf_op jit(solution)/shard_map/dot_general | solution.py:67
  381.3 8.5 %collective-permute-done.35 = bf16[512,512]{1,0:T(8,128)(2,1)S(1)} collective-permute-done((bf16[512,512]{1,0:T(8,128)(2,1)S(1)}, bf16[512,512]{1,0:T(8,128)(2,1)S(1)}, u32[]{:S(2)}, u32[]{:S(2)}) %collective-permute-start.35) | collective-permute-done | bytes 524320 | tf_op jit(solution)/shard_map/ppermute | solution.py:158
  391.6 10.0 %collective-permute-done.36 = bf16[512,512]{1,0:T(8,128)(2,1)S(1)} collective-permute-done((bf16[512,512]{1,0:T(8,128)(2,1)S(1)}, bf16[512,512]{1,0:T(8,128)(2,1)S(1)}, u32[]{:S(2)}, u32[]{:S(2)}) %collective-permute-start.36) | collective-permute-done | bytes 524320 | tf_op jit(solution)/shard_map/ppermute | solution.py:158
  405.1 9.2 %shard_map.221 = bf16[2048,1024]{1,0:T(8,128)(2,1)} custom-call(bf16[512,2048]{1,0:T(8,128)(2,1)} %fusion.3.refs_0_, bf16[512,2048]{1,0:T(8,128)(2,1)} %collective-permute-done.8.refs_1_, bf16[1024,768]{1,0:T(8,128)(2,1)} %get-tuple-element.85.refs_2_.refs_3_, bf16[1024,768]{1,0:T(8,128)(2,1)} %get-tuple-element.85.refs_2_.refs_3_, ...), custom_call_target="tpu_custom_call" | custom-call | tf_op jit(solution)/shard_map/pallas_call | solution.py:339
  447.2 18.2 %collective-permute-done.46 = bf16[2,256,1024]{1,2,0:T(8,128)(2,1)} collective-permute-done((bf16[2,256,1024]{1,2,0:T(8,128)(2,1)}, bf16[2,256,1024]{1,2,0:T(8,128)(2,1)}, u32[]{:S(2)}, u32[]{:S(2)}) %collective-permute-start.46) | collective-permute-done | bytes 1048608 | tf_op jit(solution)/shard_map/ppermute | solution.py:158
  468.5 7.9 %collective-permute-done.45 = bf16[256,1024]{0,1:T(8,128)(2,1)S(1)} collective-permute-done((bf16[256,1024]{0,1:T(8,128)(2,1)}, bf16[256,1024]{0,1:T(8,128)(2,1)S(1)}, u32[]{:S(2)}, u32[]{:S(2)}) %collective-permute-start.45) | collective-permute-done | bytes 524320 | tf_op jit(solution)/shard_map/ppermute | solution.py:158
  480.9 21.4 %collective-permute-done.38 = bf16[2,512,512]{2,1,0:T(8,128)(2,1)S(1)} collective-permute-done((bf16[2,512,512]{2,1,0:T(8,128)(2,1)S(1)}, bf16[2,512,512]{2,1,0:T(8,128)(2,1)S(1)}, u32[]{:S(2)}, u32[]{:S(2)}) %collective-permute-start.38) | collective-permute-done | bytes 1048608 | tf_op jit(solution)/shard_map/ppermute | solution.py:158
  503.1 14.3 %collective-permute-done.41 = bf16[1,512,512]{2,1,0:T(8,128)(2,1)S(1)} collective-permute-done((bf16[1,512,512]{2,1,0:T(8,128)(2,1)S(1)}, bf16[1,512,512]{2,1,0:T(8,128)(2,1)S(1)}, u32[]{:S(2)}, u32[]{:S(2)}) %collective-permute-start.41) | collective-permute-done | bytes 524320 | tf_op jit(solution)/shard_map/ppermute | solution.py:158
  (372 shorter events, 232.5 us)
Async XLA Ops:
  0.7 36.4 %collective-permute-start = (bf16[512,512]{1,0:T(8,128)(2,1)}, bf16[512,512]{1,0:T(8,128)(2,1)}, u32[]{:S(2)}, u32[]{:S(2)}) collective-permute-start(bf16[512,512]{1,0:T(8,128)(2,1)} %param.13), channel_id=1, source_target_pairs={{0,0},{4,1},{8,2},{12,3},{1,4},{5,5},{9,6},{13,7},{2,8},{6,9},{10,... | collective-permute-start | bytes 1572872 | tf_op jit(solution)/shard_map/ppermute | solution.py:246
  37.0 84.2 %collective-permute-start.10 = (bf16[512,1024]{1,0:T(8,128)(2,1)}, bf16[512,1024]{1,0:T(8,128)(2,1)S(1)}, u32[]{:S(2)}, u32[]{:S(2)}) collective-permute-start(bf16[512,1024]{1,0:T(8,128)(2,1)} %get-tuple-element.149), channel_id=1, source_target_pairs={{0,2},{1,3},{2,0},{3,1},{4,6},{5,7},{6,4},{7,5},{8,10},{9,11},{10,... | collective-permute-start | bytes 3145736 | tf_op jit(solution)/shard_map/ppermute | solution.py:158
  37.1 84.1 %collective-permute-start.9 = (bf16[512,1024]{1,0:T(8,128)(2,1)}, bf16[512,1024]{1,0:T(8,128)(2,1)}, u32[]{:S(2)}, u32[]{:S(2)}) collective-permute-start(bf16[512,1024]{1,0:T(8,128)(2,1)} %get-tuple-element.149), channel_id=1, source_target_pairs={{0,1},{1,0},{2,3},{3,2},{4,5},{5,4},{6,7},{7,6},{8,9},{9,8},{10,11... | collective-permute-start | bytes 3145736 | tf_op jit(solution)/shard_map/ppermute | solution.py:158
  55.6 38.1 %collective-permute-start.18 = (bf16[512,512]{1,0:T(8,128)(2,1)}, bf16[512,512]{1,0:T(8,128)(2,1)}, u32[]{:S(2)}, u32[]{:S(2)}) collective-permute-start(bf16[512,512]{1,0:T(8,128)(2,1)} %param.15), channel_id=1, source_target_pairs={{1,0},{5,1},{9,2},{13,3},{0,4},{4,5},{8,6},{12,7},{3,8},{7,9},{11,... | collective-permute-start | bytes 1572872 | tf_op jit(solution)/shard_map/ppermute | solution.py:246
  72.0 131.8 %collective-permute-start.8 = (bf16[512,2048]{1,0:T(8,128)(2,1)}, bf16[512,2048]{1,0:T(8,128)(2,1)}, u32[]{:S(2)}, u32[]{:S(2)}) collective-permute-start(bf16[512,2048]{1,0:T(8,128)(2,1)} %fusion.3.refs_0_), channel_id=1, source_target_pairs={{0,16},{16,0},{1,17},{17,1},{2,18},{18,2},{3,19},{19,3},{4,20},{20... | collective-permute-start | bytes 6291464 | tf_op jit(solution)/shard_map/ppermute | solution.py:158
  104.9 40.8 %collective-permute-start.50 = (f32[2,512]{1,0:T(2,128)S(1)}, f32[2,512]{1,0:T(2,128)S(1)}, u32[]{:S(2)}, u32[]{:S(2)}) collective-permute-start(f32[2,512]{1,0:T(2,128)S(1)} %pad_maximum_fusion.23), channel_id=1, source_target_pairs={{0,1},{1,0},{2,3},{3,2},{4,5},{5,4},{6,7},{7,6},{8,9},{9,8},{10,11... | collective-permute-start | bytes 12296 | tf_op jit(solution)/shard_map/ppermute | solution.py:158
  121.2 75.8 %collective-permute-start.11 = (bf16[1280,512]{1,0:T(8,128)(2,1)}, bf16[1280,512]{1,0:T(8,128)(2,1)}, u32[]{:S(2)}, u32[]{:S(2)}) collective-permute-start(bf16[1280,512]{1,0:T(8,128)(2,1)} %pad_maximum_fusion.5), channel_id=1, source_target_pairs={{0,1},{1,0},{2,3},{3,2},{4,5},{5,4},{6,7},{7,6},{8,9},{9,8},{10,11... | collective-permute-start | bytes 3932168 | tf_op jit(solution)/shard_map/ppermute | solution.py:158
  126.7 70.3 %collective-permute-start.12 = (bf16[1280,512]{1,0:T(8,128)(2,1)}, bf16[1280,512]{1,0:T(8,128)(2,1)}, u32[]{:S(2)}, u32[]{:S(2)}) collective-permute-start(bf16[1280,512]{1,0:T(8,128)(2,1)} %pad_maximum_fusion.5), channel_id=1, source_target_pairs={{0,2},{1,3},{2,0},{3,1},{4,6},{5,7},{6,4},{7,5},{8,10},{9,11},{10,... | collective-permute-start | bytes 3932168 | tf_op jit(solution)/shard_map/ppermute | solution.py:158
  142.8 38.6 %collective-permute-start.22 = (bf16[256,1024]{1,0:T(8,128)(2,1)}, bf16[256,1024]{1,0:T(8,128)(2,1)}, u32[]{:S(2)}, u32[]{:S(2)}) collective-permute-start(bf16[256,1024]{1,0:T(8,128)(2,1)} %slice.304), channel_id=1, source_target_pairs={{0,2},{1,3},{2,0},{3,1},{4,6},{5,7},{6,4},{7,5},{8,10},{9,11},{10,... | collective-permute-start | bytes 1572872 | tf_op jit(solution)/shard_map/ppermute | solution.py:158
  145.7 70.3 %collective-permute-start.21 = (bf16[512,2048]{1,0:T(8,128)(2,1)S(1)}, bf16[512,2048]{1,0:T(8,128)(2,1)}, u32[]{:S(2)}, u32[]{:S(2)}) collective-permute-start(bf16[512,2048]{1,0:T(8,128)(2,1)S(1)} %constant_dynamic-update-slice_fusion.10.refs_4_), channel_id=1, source_target_pairs={{0,16},{16,0},{1,17},{17,1},{2,18},{18,2},{3,19},{19,3},{4,20},{20... | collective-permute-start | bytes 6291464 | tf_op jit(solution)/shard_map/ppermute | solution.py:158
  194.7 232.0 %collective-permute-start.51 = (f32[2,512]{1,0:T(2,128)S(1)}, f32[2,512]{1,0:T(2,128)S(1)}, u32[]{:S(2)}, u32[]{:S(2)}) collective-permute-start(f32[2,512]{1,0:T(2,128)S(1)} %fusion.47), channel_id=1, source_target_pairs={{0,2},{1,3},{2,0},{3,1},{4,6},{5,7},{6,4},{7,5},{8,10},{9,11},{10,... | collective-permute-start | bytes 12296 | tf_op jit(solution)/shard_map/ppermute | solution.py:158
  197.0 86.8 %collective-permute-start.13 = (bf16[512,768]{1,0:T(8,128)(2,1)S(1)}, bf16[512,768]{1,0:T(8,128)(2,1)}, u32[]{:S(2)}, u32[]{:S(2)}) collective-permute-start(bf16[512,768]{1,0:T(8,128)(2,1)S(1)} %constant_dynamic-slice_fusion.7), channel_id=1, source_target_pairs={{0,1},{1,0},{2,3},{3,2},{4,5},{5,4},{6,7},{7,6},{8,9},{9,8},{10,11... | collective-permute-start | bytes 2359304 | tf_op jit(solution)/shard_map/ppermute | solution.py:158
  198.4 87.9 %collective-permute-start.14 = (bf16[512,768]{1,0:T(8,128)(2,1)S(1)}, bf16[512,768]{1,0:T(8,128)(2,1)}, u32[]{:S(2)}, u32[]{:S(2)}) collective-permute-start(bf16[512,768]{1,0:T(8,128)(2,1)S(1)} %constant_dynamic-slice_fusion.7), channel_id=1, source_target_pairs={{0,2},{1,3},{2,0},{3,1},{4,6},{5,7},{6,4},{7,5},{8,10},{9,11},{10,... | collective-permute-start | bytes 2359304 | tf_op jit(solution)/shard_map/ppermute | solution.py:158
  203.9 36.0 %collective-permute-start.24 = (bf16[640,512]{1,0:T(8,128)(2,1)}, bf16[640,512]{1,0:T(8,128)(2,1)}, u32[]{:S(2)}, u32[]{:S(2)}) collective-permute-start(bf16[640,512]{1,0:T(8,128)(2,1)} %slice.306), channel_id=1, source_target_pairs={{0,2},{1,3},{2,0},{3,1},{4,6},{5,7},{6,4},{7,5},{8,10},{9,11},{10,... | collective-permute-start | bytes 1966088 | tf_op jit(solution)/shard_map/ppermute | solution.py:158
  239.9 93.7 %collective-permute-start.26 = (bf16[2,256,1024]{1,2,0:T(8,128)(2,1)}, bf16[2,256,1024]{1,2,0:T(8,128)(2,1)}, u32[]{:S(2)}, u32[]{:S(2)}) collective-permute-start(bf16[2,256,1024]{1,2,0:T(8,128)(2,1)} %pad_maximum_fusion.9), channel_id=1, source_target_pairs={{0,1},{1,0},{2,3},{3,2},{4,5},{5,4},{6,7},{7,6},{8,9},{9,8},{10,11... | collective-permute-start | bytes 3145736 | tf_op jit(solution)/shard_map/ppermute | solution.py:158
  240.5 93.0 %collective-permute-start.27 = (bf16[2,256,1024]{1,2,0:T(8,128)(2,1)}, bf16[2,256,1024]{1,2,0:T(8,128)(2,1)}, u32[]{:S(2)}, u32[]{:S(2)}) collective-permute-start(bf16[2,256,1024]{1,2,0:T(8,128)(2,1)} %copy.60), channel_id=1, source_target_pairs={{0,2},{1,3},{2,0},{3,1},{4,6},{5,7},{6,4},{7,5},{8,10},{9,11},{10,... | collective-permute-start | bytes 3145736 | tf_op jit(solution)/shard_map/ppermute | solution.py:158
  294.1 51.4 %collective-permute-start.29 = (bf16[2,256,1024]{2,1,0:T(8,128)(2,1)}, bf16[2,256,1024]{2,1,0:T(8,128)(2,1)}, u32[]{:S(2)}, u32[]{:S(2)}) collective-permute-start(bf16[2,256,1024]{2,1,0:T(8,128)(2,1)} %pad_maximum_fusion.10), channel_id=1, source_target_pairs={{0,1},{1,0},{2,3},{3,2},{4,5},{5,4},{6,7},{7,6},{8,9},{9,8},{10,11... | collective-permute-start | bytes 3145736 | tf_op jit(solution)/shard_map/ppermute | solution.py:158
  297.6 48.0 %collective-permute-start.30 = (bf16[2,256,1024]{2,1,0:T(8,128)(2,1)}, bf16[2,256,1024]{2,1,0:T(8,128)(2,1)}, u32[]{:S(2)}, u32[]{:S(2)}) collective-permute-start(bf16[2,256,1024]{2,1,0:T(8,128)(2,1)} %stack.91), channel_id=1, source_target_pairs={{0,2},{1,3},{2,0},{3,1},{4,6},{5,7},{6,4},{7,5},{8,10},{9,11},{10,... | collective-permute-start | bytes 3145736 | tf_op jit(solution)/shard_map/ppermute | solution.py:158
  426.7 38.6 %collective-permute-start.46 = (bf16[2,256,1024]{1,2,0:T(8,128)(2,1)}, bf16[2,256,1024]{1,2,0:T(8,128)(2,1)}, u32[]{:S(2)}, u32[]{:S(2)}) collective-permute-start(bf16[2,256,1024]{1,2,0:T(8,128)(2,1)} %pad_maximum_fusion.13), channel_id=1, source_target_pairs={{0,1},{1,0},{2,3},{3,2},{4,5},{5,4},{6,7},{7,6},{8,9},{9,8},{10,11... | collective-permute-start | bytes 3145736 | tf_op jit(solution)/shard_map/ppermute | solution.py:158
  465.4 36.9 %collective-permute-start.38 = (bf16[2,512,512]{2,1,0:T(8,128)(2,1)S(1)}, bf16[2,512,512]{2,1,0:T(8,128)(2,1)S(1)}, u32[]{:S(2)}, u32[]{:S(2)}) collective-permute-start(bf16[2,512,512]{2,1,0:T(8,128)(2,1)S(1)} %pad_maximum_fusion.11), channel_id=1, source_target_pairs={{0,4},{4,0},{8,12},{12,8},{1,5},{5,1},{9,13},{13,9},{2,6},{6,2},{1... | collective-permute-start | bytes 3145736 | tf_op jit(solution)/shard_map/ppermute | solution.py:158
  466.5 54.2 %collective-permute-start.58 = (bf16[256,1024]{0,1:T(8,128)(2,1)S(1)}, bf16[256,1024]{0,1:T(8,128)(2,1)S(1)}, u32[]{:S(2)}, u32[]{:S(2)}) collective-permute-start(bf16[256,1024]{0,1:T(8,128)(2,1)S(1)} %fusion.31), channel_id=1, source_target_pairs={{0,1},{1,0},{2,3},{3,2},{4,5},{5,4},{6,7},{7,6},{8,9},{9,8},{10,11... | collective-permute-start | bytes 1572872 | tf_op jit(solution)/shard_map/ppermute | solution.py:158
  476.5 44.2 %collective-permute-start.57 = (bf16[256,1024]{0,1:T(8,128)(2,1)S(1)}, bf16[256,1024]{0,1:T(8,128)(2,1)S(1)}, u32[]{:S(2)}, u32[]{:S(2)}) collective-permute-start(bf16[256,1024]{0,1:T(8,128)(2,1)S(1)} %fusion.30), channel_id=1, source_target_pairs={{0,2},{1,3},{2,0},{3,1},{4,6},{5,7},{6,4},{7,5},{8,10},{9,11},{10,... | collective-permute-start | bytes 1572872 | tf_op jit(solution)/shard_map/ppermute | solution.py:158
  478.6 39.0 %collective-permute-start.49 = (bf16[1024,512]{1,0:T(8,128)(2,1)S(1)}, bf16[1024,512]{1,0:T(8,128)(2,1)S(1)}, u32[]{:S(2)}, u32[]{:S(2)}) collective-permute-start(bf16[1024,512]{1,0:T(8,128)(2,1)S(1)} %fusion.52), channel_id=1, source_target_pairs={{0,16},{16,0},{1,17},{17,1},{2,18},{18,2},{3,19},{19,3},{4,20},{20... | collective-permute-start | bytes 3145736 | tf_op jit(solution)/shard_map/ppermute | solution.py:158
  479.7 37.7 %collective-permute-start.41 = (bf16[1,512,512]{2,1,0:T(8,128)(2,1)S(1)}, bf16[1,512,512]{2,1,0:T(8,128)(2,1)S(1)}, u32[]{:S(2)}, u32[]{:S(2)}) collective-permute-start(bf16[1,512,512]{2,1,0:T(8,128)(2,1)S(1)} %add_convert_fusion.11), channel_id=1, source_target_pairs={{0,8},{4,12},{8,0},{12,4},{1,9},{5,13},{9,1},{13,5},{2,10},{6,14},... | collective-permute-start | bytes 1572872 | tf_op jit(solution)/shard_map/ppermute | solution.py:158
  (86 other events, 1449.8 us)

commit v4 on v3

--- a/solution.py
+++ b/solution.py
@@ -471,7 +471,6 @@
         normed_parts, after(grad_qkv, mixed_summed), grad_parts, attended
     )
     late_kept, late_got = scatter_first(late_part)
-    norm_groups = after(norm_groups, late_part)
     grad_normed = collect_third(norm_groups)
     mixed_groups = after(mixed_groups, norm_groups)
     mixed = collect_third(mixed_groups)
@@ -486,7 +485,9 @@
     out_fc1 = wide(both_halves(grad_fc1, 1))
     out_fc2 = wide(both_halves(grad_fc2_t.T, 0))
     grad_normed = after(grad_normed, out_fc1, out_fc2, *late_sent)
-    late = scatter_last(list(lax.optimization_barrier((tuple(late_parts), grad_normed))[0]))
+    late_parts = lax.optimization_barrier((tuple(late_parts), grad_normed))[0]
+    late_qkv = scatter_last([part[:, :qkv_cols] for part in late_parts])
+    late_dense = scatter_last([part[:, qkv_cols:] for part in late_parts])
 
     grad_in_b = total_over(bias_sums, ("col",), norm_groups, grad_fc1)
     sums = total_over(own_sums, ("col",), scales, late_part)
@@ -514,9 +515,9 @@
         grad_input,
         norm_sums[0],
         norm_sums[1],
-        wide(both_halves(late[:, :qkv_cols], 1)),
+        wide(both_halves(late_qkv, 1)),
         both_halves(grad_in_b[0, :qkv_cols], 0),
-        wide(both_halves(late[:, qkv_cols:].T, 0)),
+        wide(both_halves(late_dense.T, 0)),
         norm_sums[2],
         out_fc1,
         both_halves(grad_in_b[0, qkv_cols:], 0),

time: 556 us -> 556 us (level)
  waiting for transfers between devices: 151 us -> 141 us
  other arithmetic: 58.4 us -> 67.2 us
    ppermute x57, waiting for transfers between devices: 140 us -> 130 us  [swap(): lax.ppermute(array, axis, [(i, i ^ step) for i in range(lax.axis_size(axi...]
    unnamed x116 -> x128, local copies, waits for them, and re-layouts: 44.4 us -> 43.8 us
  transfers between devices with their start and end apart: 65 -> 65, of which waited for: 18 -> 21; matrix products, arithmetic and copies ran while one was open for 37% -> 39% of each run, Pallas kernels for 6% -> 6%
where the time goes in v4:
time: 556 us; the launch traced here: 546 us
  starting transfers between devices  141 us (25%)
  waiting for transfers between devices  141 us (25%)
  local copies, waits for them, and re-layouts  85.2 us (15%)
  matrix products  75.1 us (14%)
  other arithmetic  67.2 us (12%)
  Pallas kernels  33.7 us (6%)
    ppermute x57, waiting for transfers between devices, swap(): lax.ppermute(array, axis, [(i, i ^ step) for i in range(lax.axis_size(axi...  130 us
    ppermute x57, starting transfers between devices, swap(): lax.ppermute(array, axis, [(i, i ^ step) for i in range(lax.axis_size(axi...  79.9 us
    ppermute x8, starting transfers between devices, spread_start(): pieces.append(lax.ppermute(block, ('row', 'col'), pairs))  61 us
    unnamed x128, local copies, waits for them, and re-layouts  43.8 us
    dot_general x3, matrix products, dot_nn(): return jnp.dot(left, right, preferred_element_type=jnp.float32)  26.4 us
    dot_general x2, matrix products, dot_tn(): lax.dot_general(left, right, (((0,), (0,)), ((), ())), preferred_element_...  25.6 us
    pallas_call x1, Pallas kernels, attention(): pl.pallas_call(attention_kernel, grid=(packs,), in_specs=[by_rows(columns...  24.5 us
    dot_general x3, matrix products, dot_nt(): lax.dot_general(left, right, (((1,), (1,)), ((), ())), preferred_element_...  23.1 us
  transfers between devices with their start and end apart: 65, of which 21 were waited for; matrix products, arithmetic and copies ran while one was open for 39% of the time, Pallas kernels for 6%

profile of v4, /device:TPU:0, one launch (start us, length us, event | category | flops | bytes accessed | tf_op | source)
XLA Modules:
  0.0 545.9 jit_solution(17870680683536914217)
XLA Ops:
  30.8 6.1 %collective-permute-start.3 = (bf16[512,512]{1,0:T(8,128)(2,1)S(1)}, bf16[512,512]{1,0:T(8,128)(2,1)S(1)}, u32[]{:S(2)}, u32[]{:S(2)}) collective-permute-start(bf16[512,512]{1,0:T(8,128)(2,1)S(1)} %copy-done.10), channel_id=1, source_target_pairs={{3,0},{7,1},{11,2},{15,3},{2,4},{6,5},{10,6},{14,7},{1,8},{5,9},{9... | collective-permute-start | bytes 1572872 | tf_op jit(solution)/shard_map/ppermute | solution.py:246
  44.0 11.5 %collective-permute-done.2 = bf16[512,512]{1,0:T(8,128)(2,1)S(1)} collective-permute-done((bf16[512,512]{1,0:T(8,128)(2,1)S(1)}, bf16[512,512]{1,0:T(8,128)(2,1)S(1)}, u32[]{:S(2)}, u32[]{:S(2)}) %collective-permute-start.2) | collective-permute-done | bytes 524320 | tf_op jit(solution)/shard_map/ppermute | solution.py:246
  55.6 10.9 %collective-permute-start.18 = (bf16[512,512]{1,0:T(8,128)(2,1)}, bf16[512,512]{1,0:T(8,128)(2,1)}, u32[]{:S(2)}, u32[]{:S(2)}) collective-permute-start(bf16[512,512]{1,0:T(8,128)(2,1)} %param.15), channel_id=1, source_target_pairs={{1,0},{5,1},{9,2},{13,3},{0,4},{4,5},{8,6},{12,7},{3,8},{7,9},{11,... | collective-permute-start | bytes 1572872 | tf_op jit(solution)/shard_map/ppermute | solution.py:246
  72.8 20.9 %collective-permute-start.19 = (bf16[512,512]{1,0:T(8,128)(2,1)}, bf16[512,512]{1,0:T(8,128)(2,1)S(1)}, u32[]{:S(2)}, u32[]{:S(2)}) collective-permute-start(bf16[512,512]{1,0:T(8,128)(2,1)} %param.15), channel_id=1, source_target_pairs={{2,0},{6,1},{10,2},{14,3},{3,4},{7,5},{11,6},{15,7},{0,8},{4,9},{8... | collective-permute-start | bytes 1572872 | tf_op jit(solution)/shard_map/ppermute | solution.py:246
  93.7 9.9 %collective-permute-start.20 = (bf16[512,512]{1,0:T(8,128)(2,1)}, bf16[512,512]{1,0:T(8,128)(2,1)S(1)}, u32[]{:S(2)}, u32[]{:S(2)}) collective-permute-start(bf16[512,512]{1,0:T(8,128)(2,1)} %param.15), channel_id=1, source_target_pairs={{3,0},{7,1},{11,2},{15,3},{2,4},{6,5},{10,6},{14,7},{1,8},{5,9},{9... | collective-permute-start | bytes 1572872 | tf_op jit(solution)/shard_map/ppermute | solution.py:246
  104.9 16.3 %collective-permute-start.50 = (f32[2,512]{1,0:T(2,128)S(1)}, f32[2,512]{1,0:T(2,128)S(1)}, u32[]{:S(2)}, u32[]{:S(2)}) collective-permute-start(f32[2,512]{1,0:T(2,128)S(1)} %pad_maximum_fusion.23), channel_id=1, source_target_pairs={{0,1},{1,0},{2,3},{3,2},{4,5},{5,4},{6,7},{7,6},{8,9},{9,8},{10,11... | collective-permute-start | bytes 12296 | tf_op jit(solution)/shard_map/ppermute | solution.py:158
  126.7 14.3 %collective-permute-start.12 = (bf16[1280,512]{1,0:T(8,128)(2,1)}, bf16[1280,512]{1,0:T(8,128)(2,1)}, u32[]{:S(2)}, u32[]{:S(2)}) collective-permute-start(bf16[1280,512]{1,0:T(8,128)(2,1)} %pad_maximum_fusion.5), channel_id=1, source_target_pairs={{0,2},{1,3},{2,0},{3,1},{4,6},{5,7},{6,4},{7,5},{8,10},{9,11},{10,... | collective-permute-start | bytes 3932168 | tf_op jit(solution)/shard_map/ppermute | solution.py:158
  148.8 32.6 %collective-permute-done.22 = bf16[256,1024]{1,0:T(8,128)(2,1)} collective-permute-done((bf16[256,1024]{1,0:T(8,128)(2,1)}, bf16[256,1024]{1,0:T(8,128)(2,1)}, u32[]{:S(2)}, u32[]{:S(2)}) %collective-permute-start.22) | collective-permute-done | bytes 524320 | tf_op jit(solution)/shard_map/ppermute | solution.py:158
  188.4 6.4 %collective-permute-done.23 = bf16[256,1024]{1,0:T(8,128)(2,1)S(1)} collective-permute-done((bf16[256,1024]{1,0:T(8,128)(2,1)S(1)}, bf16[256,1024]{1,0:T(8,128)(2,1)S(1)}, u32[]{:S(2)}, u32[]{:S(2)}) %collective-permute-start.23) | collective-permute-done | bytes 524320 | tf_op jit(solution)/shard_map/ppermute | solution.py:158
  205.3 10.7 %multiply_convert_fusion = (bf16[1024,1024]{1,0:T(8,128)(2,1)S(1)}, f32[1024,1024]{1,0:T(8,128)}) fusion(f32[1024]{0:T(1024)S(1)} %dynamic_slice.47, bf16[2048,1024]{1,0:T(8,128)(2,1)} %constant_dynamic-update-slice_fusion.5, bf16[512,2048]{1,0:T(8,128)(2,1)} %collective-permute-done.8.refs_1_, bf16[512,2048]{1,0:T(8,128)(2,1)} %fusion.3.refs_0_), kind=kOutput, calls=%fused_computation.24 | convolution fusion | flops 4313841664 | bytes 14684160 | tf_op jit(solution)/shard_map/dot_general | solution.py:67
  217.4 6.7 %convolution_convert_fusion.2 = bf16[2048,1024]{1,0:T(8,128)(2,1)S(1)} fusion(bf16[1024,1024]{1,0:T(8,128)(2,1)S(1)} %get-tuple-element.205, bf16[512,2048]{1,0:T(8,128)(2,1)} %collective-permute-done.21.refs_5_, bf16[512,2048]{1,0:T(8,128)(2,1)S(1)} %constant_dynamic-update-slice_fusion.10.refs_4_), kind=kOutput, calls=%fused_computation.27 | convolution fusion | flops 4305453056 | bytes 10485760 | tf_op jit(solution)/shard_map/dot_general | solution.py:61
  241.0 10.3 %fusion.49 = f32[1024,1280]{1,0:T(8,128)S(1)} fusion(bf16[1024,2048]{1,0:T(8,128)(2,1)} %pad_maximum_fusion.1, bf16[640,512]{1,0:T(8,128)(2,1)} %collective-permute-done.25, bf16[640,512]{1,0:T(8,128)(2,1)} %collective-permute-done.24, bf16[1280,512]{1,0:T(8,128)(2,1)} %collective-permute-done.12, bf16[1280,512]{1,0:T(8,128)(2,1)} %collective-permute-done.11, ...), kind=kOutput, calls=%fused_computation.200 | convolution fusion | flops 5394923520 | bytes 14680064 | tf_op jit(solution)/shard_map/dot_general | solution.py:55
  254.4 18.9 %convolution_convert_fusion.1 = bf16[2048,1024]{1,0:T(8,128)(2,1)S(1)} fusion(bf16[1024,1024]{1,0:T(8,128)(2,1)S(1)} %get-tuple-element.79, bf16[512,2048]{1,0:T(8,128)(2,1)} %collective-permute-done.8.refs_1_, bf16[512,2048]{1,0:T(8,128)(2,1)} %fusion.3.refs_0_), kind=kOutput, calls=%fused_computation.26 | convolution fusion | flops 4305453056 | bytes 10485760 | tf_op jit(solution)/shard_map/dot_general | solution.py:61
  277.3 6.7 %fusion.58 = f32[1024,2048]{1,0:T(8,128)} fusion(bf16[1024,1024]{1,0:T(8,128)(2,1)S(1)} %get-tuple-element.79, bf16[2048,1024]{1,0:T(8,128)(2,1)S(1)} %copy-done.30), kind=kOutput, calls=%fused_computation.208 | convolution fusion | flops 4294967296 | bytes 14680064 | tf_op jit(solution)/shard_map/dot_general | solution.py:55
  300.1 7.3 %fusion.13.qkv_ref = f32[1024,768]{1,0:T(8,128)} fusion(bf16[2048,768]{1,0:T(8,128)(2,1)S(1)} %constant_dynamic-update-slice_fusion, bf16[512,2048]{1,0:T(8,128)(2,1)} %collective-permute-done.8.refs_1_, bf16[512,2048]{1,0:T(8,128)(2,1)} %fusion.3.refs_0_), kind=kOutput, calls=%fused_computation.45 | convolution fusion | flops 3229614080 | bytes 10485760 | tf_op jit(solution)/shard_map/dot_general | solution.py:67
  307.4 24.5 %shard_map.220 = (bf16[1024,256]{1,0:T(8,128)(2,1)}, bf16[1024,768]{1,0:T(8,128)(2,1)}) custom-call(f32[1024,768]{1,0:T(8,128)} %fusion.13.qkv_ref, f32[1,768]{1,0:T(1,128)} %reshape.204.bias_ref, f32[1024,768]{1,0:T(8,128)} %pad_maximum_fusion.2.cos_ref, f32[1024,768]{1,0:T(8,128)} %pad_maximum_fusion.3.sin_ref, s32[2,512,1]{2,1,0:T(8,128)} %copy.41.seg_col_ref, ...), custom_call_target="tpu_custom_call" | custom-call | tf_op jit(solution)/shard_map/pallas_call | solution.py:120
  343.0 6.1 %add_convert_fusion = bf16[1024,2048]{1,0:T(8,128)(2,1)S(1)} fusion(f32[1024,2048]{1,0:T(8,128)} %fusion.58, bf16[1024,768]{1,0:T(8,128)(2,1)S(1)} %copy-done.3, bf16[2048,768]{1,0:T(8,128)(2,1)S(1)} %copy-done.33), kind=kOutput, calls=%fused_computation | convolution fusion | flops 3225419776 | bytes 17301504 | tf_op jit(solution)/shard_map/dot_general | solution.py:55
  362.4 8.4 %convolution_convert_fusion = bf16[1024,2048]{1,0:T(8,128)(2,1)S(1)} fusion(bf16[1024,1280]{1,0:T(8,128)(2,1)S(1)} %pad_maximum_fusion.4, bf16[640,512]{1,0:T(8,128)(2,1)} %collective-permute-done.25, bf16[640,512]{1,0:T(8,128)(2,1)} %collective-permute-done.24, bf16[1280,512]{1,0:T(8,128)(2,1)} %collective-permute-done.12, ...), kind=kOutput, calls=%fused_computation.25 | convolution fusion | flops 5397020672 | bytes 12058624 | tf_op jit(solution)/shard_map/dot_general | solution.py:67
  373.8 11.2 %collective-permute-done.36 = bf16[512,512]{1,0:T(8,128)(2,1)S(1)} collective-permute-done((bf16[512,512]{1,0:T(8,128)(2,1)S(1)}, bf16[512,512]{1,0:T(8,128)(2,1)S(1)}, u32[]{:S(2)}, u32[]{:S(2)}) %collective-permute-start.36) | collective-permute-done | bytes 524320 | tf_op jit(solution)/shard_map/ppermute | solution.py:158
  393.5 17.2 %collective-permute-done.40 = bf16[2,512,512]{2,1,0:T(8,128)(2,1)S(1)} collective-permute-done((bf16[2,512,512]{2,1,0:T(8,128)(2,1)S(1)}, bf16[2,512,512]{2,1,0:T(8,128)(2,1)S(1)}, u32[]{:S(2)}, u32[]{:S(2)}) %collective-permute-start.40) | collective-permute-done | bytes 1048608 | tf_op jit(solution)/shard_map/ppermute | solution.py:158
  413.9 9.2 %shard_map.221 = bf16[2048,1024]{1,0:T(8,128)(2,1)} custom-call(bf16[512,2048]{1,0:T(8,128)(2,1)} %fusion.3.refs_0_, bf16[512,2048]{1,0:T(8,128)(2,1)} %collective-permute-done.8.refs_1_, bf16[1024,768]{1,0:T(8,128)(2,1)} %get-tuple-element.85.refs_2_.refs_3_, bf16[1024,768]{1,0:T(8,128)(2,1)} %get-tuple-element.85.refs_2_.refs_3_, ...), custom_call_target="tpu_custom_call" | custom-call | tf_op jit(solution)/shard_map/pallas_call | solution.py:339
  447.5 7.0 %collective-permute-done.33 = bf16[512,512]{1,0:T(8,128)(2,1)} collective-permute-done((bf16[512,512]{1,0:T(8,128)(2,1)}, bf16[512,512]{1,0:T(8,128)(2,1)}, u32[]{:S(2)}, u32[]{:S(2)}) %collective-permute-start.33) | collective-permute-done | bytes 524320 | tf_op jit(solution)/shard_map/ppermute | solution.py:158
  460.7 17.7 %collective-permute-done.46 = bf16[2,256,1024]{1,2,0:T(8,128)(2,1)} collective-permute-done((bf16[2,256,1024]{1,2,0:T(8,128)(2,1)}, bf16[2,256,1024]{1,2,0:T(8,128)(2,1)}, u32[]{:S(2)}, u32[]{:S(2)}) %collective-permute-start.46) | collective-permute-done | bytes 1048608 | tf_op jit(solution)/shard_map/ppermute | solution.py:158
  512.7 13.0 %collective-permute-done.39 = bf16[1,512,512]{2,1,0:T(8,128)(2,1)S(1)} collective-permute-done((bf16[1,512,512]{2,1,0:T(8,128)(2,1)S(1)}, bf16[1,512,512]{2,1,0:T(8,128)(2,1)S(1)}, u32[]{:S(2)}, u32[]{:S(2)}) %collective-permute-start.39) | collective-permute-done | bytes 524320 | tf_op jit(solution)/shard_map/ppermute | solution.py:158
  (386 shorter events, 239.6 us)
Async XLA Ops:
  0.7 36.4 %collective-permute-start = (bf16[512,512]{1,0:T(8,128)(2,1)}, bf16[512,512]{1,0:T(8,128)(2,1)}, u32[]{:S(2)}, u32[]{:S(2)}) collective-permute-start(bf16[512,512]{1,0:T(8,128)(2,1)} %param.13), channel_id=1, source_target_pairs={{0,0},{4,1},{8,2},{12,3},{1,4},{5,5},{9,6},{13,7},{2,8},{6,9},{10,... | collective-permute-start | bytes 1572872 | tf_op jit(solution)/shard_map/ppermute | solution.py:246
  30.8 35.6 %collective-permute-start.3 = (bf16[512,512]{1,0:T(8,128)(2,1)S(1)}, bf16[512,512]{1,0:T(8,128)(2,1)S(1)}, u32[]{:S(2)}, u32[]{:S(2)}) collective-permute-start(bf16[512,512]{1,0:T(8,128)(2,1)S(1)} %copy-done.10), channel_id=1, source_target_pairs={{3,0},{7,1},{11,2},{15,3},{2,4},{6,5},{10,6},{14,7},{1,8},{5,9},{9... | collective-permute-start | bytes 1572872 | tf_op jit(solution)/shard_map/ppermute | solution.py:246
  37.0 84.2 %collective-permute-start.10 = (bf16[512,1024]{1,0:T(8,128)(2,1)}, bf16[512,1024]{1,0:T(8,128)(2,1)S(1)}, u32[]{:S(2)}, u32[]{:S(2)}) collective-permute-start(bf16[512,1024]{1,0:T(8,128)(2,1)} %get-tuple-element.147), channel_id=1, source_target_pairs={{0,2},{1,3},{2,0},{3,1},{4,6},{5,7},{6,4},{7,5},{8,10},{9,11},{10,... | collective-permute-start | bytes 3145736 | tf_op jit(solution)/shard_map/ppermute | solution.py:158
  37.1 84.1 %collective-permute-start.9 = (bf16[512,1024]{1,0:T(8,128)(2,1)}, bf16[512,1024]{1,0:T(8,128)(2,1)}, u32[]{:S(2)}, u32[]{:S(2)}) collective-permute-start(bf16[512,1024]{1,0:T(8,128)(2,1)} %get-tuple-element.147), channel_id=1, source_target_pairs={{0,1},{1,0},{2,3},{3,2},{4,5},{5,4},{6,7},{7,6},{8,9},{9,8},{10,11... | collective-permute-start | bytes 3145736 | tf_op jit(solution)/shard_map/ppermute | solution.py:158
  55.6 38.1 %collective-permute-start.18 = (bf16[512,512]{1,0:T(8,128)(2,1)}, bf16[512,512]{1,0:T(8,128)(2,1)}, u32[]{:S(2)}, u32[]{:S(2)}) collective-permute-start(bf16[512,512]{1,0:T(8,128)(2,1)} %param.15), channel_id=1, source_target_pairs={{1,0},{5,1},{9,2},{13,3},{0,4},{4,5},{8,6},{12,7},{3,8},{7,9},{11,... | collective-permute-start | bytes 1572872 | tf_op jit(solution)/shard_map/ppermute | solution.py:246
  72.0 131.8 %collective-permute-start.8 = (bf16[512,2048]{1,0:T(8,128)(2,1)}, bf16[512,2048]{1,0:T(8,128)(2,1)}, u32[]{:S(2)}, u32[]{:S(2)}) collective-permute-start(bf16[512,2048]{1,0:T(8,128)(2,1)} %fusion.3.refs_0_), channel_id=1, source_target_pairs={{0,16},{16,0},{1,17},{17,1},{2,18},{18,2},{3,19},{19,3},{4,20},{20... | collective-permute-start | bytes 6291464 | tf_op jit(solution)/shard_map/ppermute | solution.py:158
  104.9 40.8 %collective-permute-start.50 = (f32[2,512]{1,0:T(2,128)S(1)}, f32[2,512]{1,0:T(2,128)S(1)}, u32[]{:S(2)}, u32[]{:S(2)}) collective-permute-start(f32[2,512]{1,0:T(2,128)S(1)} %pad_maximum_fusion.23), channel_id=1, source_target_pairs={{0,1},{1,0},{2,3},{3,2},{4,5},{5,4},{6,7},{7,6},{8,9},{9,8},{10,11... | collective-permute-start | bytes 12296 | tf_op jit(solution)/shard_map/ppermute | solution.py:158
  121.2 75.8 %collective-permute-start.11 = (bf16[1280,512]{1,0:T(8,128)(2,1)}, bf16[1280,512]{1,0:T(8,128)(2,1)}, u32[]{:S(2)}, u32[]{:S(2)}) collective-permute-start(bf16[1280,512]{1,0:T(8,128)(2,1)} %pad_maximum_fusion.5), channel_id=1, source_target_pairs={{0,1},{1,0},{2,3},{3,2},{4,5},{5,4},{6,7},{7,6},{8,9},{9,8},{10,11... | collective-permute-start | bytes 3932168 | tf_op jit(solution)/shard_map/ppermute | solution.py:158
  126.7 70.4 %collective-permute-start.12 = (bf16[1280,512]{1,0:T(8,128)(2,1)}, bf16[1280,512]{1,0:T(8,128)(2,1)}, u32[]{:S(2)}, u32[]{:S(2)}) collective-permute-start(bf16[1280,512]{1,0:T(8,128)(2,1)} %pad_maximum_fusion.5), channel_id=1, source_target_pairs={{0,2},{1,3},{2,0},{3,1},{4,6},{5,7},{6,4},{7,5},{8,10},{9,11},{10,... | collective-permute-start | bytes 3932168 | tf_op jit(solution)/shard_map/ppermute | solution.py:158
  142.8 38.6 %collective-permute-start.22 = (bf16[256,1024]{1,0:T(8,128)(2,1)}, bf16[256,1024]{1,0:T(8,128)(2,1)}, u32[]{:S(2)}, u32[]{:S(2)}) collective-permute-start(bf16[256,1024]{1,0:T(8,128)(2,1)} %slice.344), channel_id=1, source_target_pairs={{0,2},{1,3},{2,0},{3,1},{4,6},{5,7},{6,4},{7,5},{8,10},{9,11},{10,... | collective-permute-start | bytes 1572872 | tf_op jit(solution)/shard_map/ppermute | solution.py:158
  145.7 70.3 %collective-permute-start.21 = (bf16[512,2048]{1,0:T(8,128)(2,1)S(1)}, bf16[512,2048]{1,0:T(8,128)(2,1)}, u32[]{:S(2)}, u32[]{:S(2)}) collective-permute-start(bf16[512,2048]{1,0:T(8,128)(2,1)S(1)} %constant_dynamic-update-slice_fusion.10.refs_4_), channel_id=1, source_target_pairs={{0,16},{16,0},{1,17},{17,1},{2,18},{18,2},{3,19},{19,3},{4,20},{20... | collective-permute-start | bytes 6291464 | tf_op jit(solution)/shard_map/ppermute | solution.py:158
  194.7 246.5 %collective-permute-start.51 = (f32[2,512]{1,0:T(2,128)S(1)}, f32[2,512]{1,0:T(2,128)S(1)}, u32[]{:S(2)}, u32[]{:S(2)}) collective-permute-start(f32[2,512]{1,0:T(2,128)S(1)} %fusion.45), channel_id=1, source_target_pairs={{0,2},{1,3},{2,0},{3,1},{4,6},{5,7},{6,4},{7,5},{8,10},{9,11},{10,... | collective-permute-start | bytes 12296 | tf_op jit(solution)/shard_map/ppermute | solution.py:158
  197.0 87.0 %collective-permute-start.13 = (bf16[512,768]{1,0:T(8,128)(2,1)S(1)}, bf16[512,768]{1,0:T(8,128)(2,1)}, u32[]{:S(2)}, u32[]{:S(2)}) collective-permute-start(bf16[512,768]{1,0:T(8,128)(2,1)S(1)} %constant_dynamic-slice_fusion.7), channel_id=1, source_target_pairs={{0,1},{1,0},{2,3},{3,2},{4,5},{5,4},{6,7},{7,6},{8,9},{9,8},{10,11... | collective-permute-start | bytes 2359304 | tf_op jit(solution)/shard_map/ppermute | solution.py:158
  198.4 88.2 %collective-permute-start.14 = (bf16[512,768]{1,0:T(8,128)(2,1)S(1)}, bf16[512,768]{1,0:T(8,128)(2,1)}, u32[]{:S(2)}, u32[]{:S(2)}) collective-permute-start(bf16[512,768]{1,0:T(8,128)(2,1)S(1)} %constant_dynamic-slice_fusion.7), channel_id=1, source_target_pairs={{0,2},{1,3},{2,0},{3,1},{4,6},{5,7},{6,4},{7,5},{8,10},{9,11},{10,... | collective-permute-start | bytes 2359304 | tf_op jit(solution)/shard_map/ppermute | solution.py:158
  203.9 35.9 %collective-permute-start.24 = (bf16[640,512]{1,0:T(8,128)(2,1)}, bf16[640,512]{1,0:T(8,128)(2,1)}, u32[]{:S(2)}, u32[]{:S(2)}) collective-permute-start(bf16[640,512]{1,0:T(8,128)(2,1)} %slice.346), channel_id=1, source_target_pairs={{0,2},{1,3},{2,0},{3,1},{4,6},{5,7},{6,4},{7,5},{8,10},{9,11},{10,... | collective-permute-start | bytes 1966088 | tf_op jit(solution)/shard_map/ppermute | solution.py:158
  239.8 93.8 %collective-permute-start.26 = (bf16[2,256,1024]{1,2,0:T(8,128)(2,1)}, bf16[2,256,1024]{1,2,0:T(8,128)(2,1)}, u32[]{:S(2)}, u32[]{:S(2)}) collective-permute-start(bf16[2,256,1024]{1,2,0:T(8,128)(2,1)} %pad_maximum_fusion.9), channel_id=1, source_target_pairs={{0,1},{1,0},{2,3},{3,2},{4,5},{5,4},{6,7},{7,6},{8,9},{9,8},{10,11... | collective-permute-start | bytes 3145736 | tf_op jit(solution)/shard_map/ppermute | solution.py:158
  240.5 93.2 %collective-permute-start.27 = (bf16[2,256,1024]{1,2,0:T(8,128)(2,1)}, bf16[2,256,1024]{1,2,0:T(8,128)(2,1)}, u32[]{:S(2)}, u32[]{:S(2)}) collective-permute-start(bf16[2,256,1024]{1,2,0:T(8,128)(2,1)} %copy.60), channel_id=1, source_target_pairs={{0,2},{1,3},{2,0},{3,1},{4,6},{5,7},{6,4},{7,5},{8,10},{9,11},{10,... | collective-permute-start | bytes 3145736 | tf_op jit(solution)/shard_map/ppermute | solution.py:158
  294.4 43.4 %collective-permute-start.29 = (bf16[2,256,1024]{2,1,0:T(8,128)(2,1)}, bf16[2,256,1024]{2,1,0:T(8,128)(2,1)}, u32[]{:S(2)}, u32[]{:S(2)}) collective-permute-start(bf16[2,256,1024]{2,1,0:T(8,128)(2,1)} %pad_maximum_fusion.10), channel_id=1, source_target_pairs={{0,1},{1,0},{2,3},{3,2},{4,5},{5,4},{6,7},{7,6},{8,9},{9,8},{10,11... | collective-permute-start | bytes 3145736 | tf_op jit(solution)/shard_map/ppermute | solution.py:158
  297.8 39.9 %collective-permute-start.30 = (bf16[2,256,1024]{2,1,0:T(8,128)(2,1)}, bf16[2,256,1024]{2,1,0:T(8,128)(2,1)}, u32[]{:S(2)}, u32[]{:S(2)}) collective-permute-start(bf16[2,256,1024]{2,1,0:T(8,128)(2,1)} %stack.91), channel_id=1, source_target_pairs={{0,2},{1,3},{2,0},{3,1},{4,6},{5,7},{6,4},{7,5},{8,10},{9,11},{10,... | collective-permute-start | bytes 3145736 | tf_op jit(solution)/shard_map/ppermute | solution.py:158
  373.8 38.0 %collective-permute-start.31 = (bf16[512,2048]{1,0:T(8,128)(2,1)S(1)}, bf16[512,2048]{1,0:T(8,128)(2,1)S(1)}, u32[]{:S(2)}, u32[]{:S(2)}) collective-permute-start(bf16[512,2048]{1,0:T(8,128)(2,1)S(1)} %slice.361), channel_id=1, source_target_pairs={{0,16},{16,0},{1,17},{17,1},{2,18},{18,2},{3,19},{19,3},{4,20},{20... | collective-permute-start | bytes 6291464 | tf_op jit(solution)/shard_map/ppermute | solution.py:158
  439.5 38.8 %collective-permute-start.46 = (bf16[2,256,1024]{1,2,0:T(8,128)(2,1)}, bf16[2,256,1024]{1,2,0:T(8,128)(2,1)}, u32[]{:S(2)}, u32[]{:S(2)}) collective-permute-start(bf16[2,256,1024]{1,2,0:T(8,128)(2,1)} %pad_maximum_fusion.13), channel_id=1, source_target_pairs={{0,1},{1,0},{2,3},{3,2},{4,5},{5,4},{6,7},{7,6},{8,9},{9,8},{10,11... | collective-permute-start | bytes 3145736 | tf_op jit(solution)/shard_map/ppermute | solution.py:158
  441.2 37.4 %collective-permute-start.47 = (bf16[2,256,1024]{1,2,0:T(8,128)(2,1)}, bf16[2,256,1024]{1,2,0:T(8,128)(2,1)}, u32[]{:S(2)}, u32[]{:S(2)}) collective-permute-start(bf16[2,256,1024]{1,2,0:T(8,128)(2,1)} %copy.67), channel_id=1, source_target_pairs={{0,2},{1,3},{2,0},{3,1},{4,6},{5,7},{6,4},{7,5},{8,10},{9,11},{10,... | collective-permute-start | bytes 3145736 | tf_op jit(solution)/shard_map/ppermute | solution.py:158
  444.6 42.4 %collective-permute-start.45 = (bf16[256,1024]{0,1:T(8,128)(2,1)}, bf16[256,1024]{0,1:T(8,128)(2,1)S(1)}, u32[]{:S(2)}, u32[]{:S(2)}) collective-permute-start(bf16[256,1024]{0,1:T(8,128)(2,1)} %fusion.26), channel_id=1, source_target_pairs={{0,1},{1,0},{2,3},{3,2},{4,5},{5,4},{6,7},{7,6},{8,9},{9,8},{10,11... | collective-permute-start | bytes 1572872 | tf_op jit(solution)/shard_map/ppermute | solution.py:158
  456.0 36.6 %collective-permute-start.41 = (bf16[1,512,512]{2,1,0:T(8,128)(2,1)}, bf16[1,512,512]{2,1,0:T(8,128)(2,1)}, u32[]{:S(2)}, u32[]{:S(2)}) collective-permute-start(bf16[1,512,512]{2,1,0:T(8,128)(2,1)} %add_convert_fusion.9), channel_id=1, source_target_pairs={{0,8},{4,12},{8,0},{12,4},{1,9},{5,13},{9,1},{13,5},{2,10},{6,14},... | collective-permute-start | bytes 1572872 | tf_op jit(solution)/shard_map/ppermute | solution.py:158
  (92 other events, 1772.6 us)
